TPU v7x, 32 devices: a whole 2x2x4 slice. The times are simulated.
32 devices in a mesh: exp: 2 (over x), tile: 2 (over core), depth: 8 (over z, y).
Axes of the slice: x: 2, y: 2, z: 4, core: 2. Of those that a mesh axis runs over, the one named last changes fastest.
Arguments:
- images: float32 [2, 4, 256, 256], P('exp', None, 'tile'), may hold values from 0.25 to 4
- offsets: int32 [4, 64], P(None, 'depth'), may hold values from -6 to 6
- fractions: float32 [4, 64], P(None, 'depth'), may hold values from 0 to 1
- shifts: int32 [16, 3], P(('tile', 'depth')), may hold values from -8 to 7
Outputs:
- correlation: float32 [16, 64, 4096], P(('tile', 'depth'), 'exp')
All inputs are finite; a program needn't handle non-finite values.
Results may differ from a plain program's by a relative error of at most 0.0003.
Values sent between devices are 32-bit elements; how exact they have to be, the bound alone decides.
No kernel may reach another device: no remote copies, remote signals or barrier semaphores. Data moves between devices by JAX's collectives and lax.ppermute only.
A program may use at most 64 MiB of HBM per device.

v0:
```python
import functools
import math

import jax
import jax.numpy as jnp
import numpy as np
from jax import lax
from jax.experimental import pallas as pl
from jax.experimental.pallas import tpu as pltpu
from jax.sharding import PartitionSpec as P

BRICK = 64
HALF = BRICK // 2
ROWS = 40
MARGIN = 32
SHIFT_LOW = -8
PAIRS = 9
REACH = 18
KZ_STEPS = 6
KZ_PER_STEP = 6
spectral_floor = 0.01
f32, bf16 = jnp.float32, jnp.bfloat16


def split(value):
    high = value.astype(bf16)
    return high, (value - high.astype(f32)).astype(bf16)


def dot(a, b):
    return jnp.dot(a, b, preferred_element_type=f32)


def tent_value(distance, fraction):
    return jnp.maximum(0.0, 1.0 - jnp.abs(distance - fraction) / 1.5)


def dft_parts():
    wave = np.arange(BRICK)
    angle = (wave[:, None] * wave[None, :] % BRICK) * (2.0 * math.pi / BRICK)
    return np.cos(angle) / math.sqrt(BRICK), np.sin(angle) / math.sqrt(BRICK)


def host_split(value):
    high = value.astype(np.float32).astype(bf16)
    return high, (value - high.astype(np.float64)).astype(np.float32).astype(bf16)


def constant_tables():
    c, s = dft_parts()
    n = BRICK
    zt = np.zeros((2 * ROWS, n))
    zt[: HALF + 1], zt[ROWS : ROWS + HALF + 1] = c[: HALF + 1], -s[: HALF + 1]
    high, low = host_split(zt)
    z_fwd = np.concatenate([high, high, low], axis=1)
    yt = np.zeros((2, 2, n, 2, 2, n))
    for p in range(2):
        yt[0, p, :, p, 0], yt[0, p, :, p, 1] = c, -s
        yt[1, p, :, p, 0], yt[1, p, :, p, 1] = s, c
    high, low = host_split(yt.reshape(4 * n, 4 * n))
    y_fwd = np.concatenate([high, high, low], axis=0)
    order = np.concatenate([np.arange(0, n, 2), np.arange(1, n, 2)])
    high, low = host_split(np.concatenate([c[:, order], s[:, order]], axis=1))
    x_fwd = np.concatenate([np.concatenate([high, high], 1), np.concatenate([low, low], 1)], 0)
    twice = lambda t: np.concatenate([t, t], axis=0)
    x_inv = twice(np.concatenate([c, -s], axis=1)).astype(np.float32)
    y_inv = np.stack([np.concatenate([twice(c), twice(-s)], 1).T, np.concatenate([twice(s), twice(c)], 1).T])
    y_inv = y_inv.astype(np.float32)
    weight = np.full(ROWS, 2.0)
    weight[0] = weight[HALF] = 1.0
    weight[HALF + 1 :] = 0.0
    third = lambda t: np.pad(np.tile(t[:, :ROWS] * weight, (1, 3)), ((0, 0), (0, 2 * n - 3 * ROWS)))
    z_inv = np.stack([twice(third(c)), twice(third(-s))]).astype(np.float32)
    return z_fwd, y_fwd, x_fwd, x_inv, y_inv, z_inv


def kernel(
    shift_ref, own_ref, other_ref, pad_own_ref, pad_other_ref, tab_ref,
    z_fwd_ref, y_fwd_ref, x_fwd_ref, x_inv_ref, y_inv_ref, z_inv_ref,
    out_ref,
    raw_ref, log_ref, pack_ref, high_ref, shifted_ref, spec_ref, line_ref,
    back_ref, forward_ref, xi_ref, yi_ref, zi_ref,
    *, bricks_y,
):
    n = BRICK
    exp_index = lax.axis_index("exp")
    part = lax.axis_index("depth") // bricks_y
    window = (n + 2 * MARGIN) * n
    pad = MARGIN * n
    strip = own_ref.shape[1]

    tab = tab_ref[...]
    rows = lax.broadcasted_iota(jnp.int32, (8, 2 * n), 0)
    offs = jnp.where(rows < 4, tab, pltpu.roll(tab, 4, 0))
    frac = jnp.where(rows < 4, pltpu.roll(tab, 4, 0), tab)
    total = sum(tent_value(float(d), frac) for d in range(-2, 4))
    parity = (rows >= 4).astype(f32)
    blocks = [tent_value(SHIFT_LOW + 2 * q + parity - offs, frac) / total for q in range(PAIRS)]
    sums = jnp.sum(sum(blocks)[:, :n], axis=1, keepdims=True) / n
    uniform = jnp.log(sums + pltpu.roll(jnp.broadcast_to(sums, (8, 2 * n)), 4, 0)[:, :1])
    both_high, back_low = [], []
    for block in blocks:
        high, low = split(block / 4.0)
        both_high += [high.astype(f32)] * 2
        back_low.append(low.astype(f32))
    stacked = jnp.concatenate(both_high + back_low + [jnp.zeros((40, 2 * n), f32)], axis=0)
    back_ref[...] = jnp.transpose(stacked)[:n, :224].astype(bf16)
    high, low = split(jnp.concatenate(blocks, axis=0) / n)
    forward_ref[...] = jnp.concatenate([high, low], axis=1)[:, : 3 * n]

    sz, sx, sy = (shift_ref[0, i] + n for i in range(3))
    high, low = split(x_inv_ref[pl.ds(lax.rem(sx, n), n), :])
    xi_ref[0:n, 0 : 2 * n] = high
    xi_ref[0:n, 2 * n :] = high
    xi_ref[n:, 0 : 2 * n] = low
    xi_ref[n:, 2 * n :] = low
    lane = lax.broadcasted_iota(jnp.int32, (2 * n, 2 * n), 1)
    back = lax.rem(2 * n - lax.rem(sy, n), 2 * n)
    turned = jnp.where(lane < n, pltpu.roll(y_inv_ref[0], back, 1), pltpu.roll(y_inv_ref[1], back, 1))
    high, low = split(turned)
    yi_ref[0 : 2 * n, 0 : 2 * n] = high
    yi_ref[2 * n :, 0 : 2 * n] = high
    yi_ref[0 : 2 * n, 2 * n :] = low
    yi_ref[2 * n :, 2 * n :] = low
    first = lax.rem(HALF * exp_index + sz, n)
    turned = jnp.concatenate([z_inv_ref[0, pl.ds(first, HALF), :], z_inv_ref[1, pl.ds(first, HALF), :]], axis=0)
    high, low = split(turned)
    col = lax.broadcasted_iota(jnp.int32, turned.shape, 1)
    zi_ref[...] = jnp.where(col < 2 * ROWS, high.astype(f32), low.astype(f32)).astype(bf16)

    def spread(e, first_lane, count):
        pieces = [pack_ref[e, :, pl.ds(first_lane + 128 * q, count)] for q in range(PAIRS)]
        pieces += [high_ref[e, :, pl.ds(first_lane + 128 * q, count)] for q in range(0, PAIRS, 2)]
        return jnp.concatenate(pieces, axis=0)

    def pack(e, ratio):
        lanes = ratio.shape[1]
        row = lax.broadcasted_iota(jnp.int32, ratio.shape, 0)
        both = jnp.where(row < 4, ratio, pltpu.roll(pltpu.roll(ratio, 4, 0), lanes - n, 1))
        high = both.astype(bf16).astype(f32)
        pack_ref[e, :, 0:lanes] = jnp.concatenate([high, both - high], axis=0).astype(bf16)
        high_ref[e, :, 0:lanes] = jnp.concatenate([high, pltpu.roll(high, lanes - 128, 1)], axis=0).astype(bf16)

    for e, (strip_ref, pad_ref) in enumerate(((own_ref, pad_own_ref), (other_ref, pad_other_ref))):
        raw_ref[e, 0:4, 0:pad] = pad_ref[0]
        raw_ref[e, 0:4, pad : pad + strip] = strip_ref[...]
        raw_ref[e, 0:4, pad + strip :] = pad_ref[pad_ref.shape[0] - 1]
        raw_ref[e, 4:8, :] = jnp.ones((4, strip + 2 * pad), f32)
    for e in range(2):
        logs = jnp.log(raw_ref[e, :, pl.ds(pl.multiple_of(part * (n * n), n * n), window)])
        log_ref[e] = logs
        pack(e, logs - uniform)

    lo_x, hi_x = -REACH, n + REACH
    chunk = 1280
    back_w = back_ref[...]
    forward_w = forward_ref[...]

    def first_pass(i, _):
        start = pl.multiple_of(i * chunk, 256)
        for e in range(2):
            logv = dot(back_w, spread(e, start + (lo_x + SHIFT_LOW + MARGIN) * n, chunk))
            high, low = split(jnp.exp(logv))
            shifted_ref[e, :, pl.ds(start, chunk)] = dot(forward_w, jnp.concatenate([high, low, high], axis=0))
        return 0

    lax.fori_loop(0, (hi_x - lo_x) * n // chunk, first_pass, 0)

    lo_u, hi_u = -10, n + 10
    count = (hi_u - lo_u) * n
    for e in range(2):
        gathered = sum(
            shifted_ref[e, 8 * q : 8 * q + 8, (lo_u - SHIFT_LOW - 2 * q - lo_x) * n :][:, :count] for q in range(PAIRS)
        )
        proj = gathered + pltpu.roll(pltpu.roll(gathered, n, 1), 4, 0)
        logs = log_ref[e, :, (lo_u + 2 + MARGIN) * n : (hi_u + MARGIN) * n]
        second = logs - jnp.log(proj[:, 2 * n :])
        pack(e, (logs - uniform) + second)

    chunk2 = 1024
    per = chunk2 // (2 * n)

    def second_pass(i, _):
        start = pl.multiple_of(i * chunk2, chunk2)
        for e in range(2):
            logv = dot(back_w, spread(e, start, chunk2))
            high, low = split(jnp.exp(logv))
            spec = dot(z_fwd_ref[...], jnp.concatenate([high, low, high], axis=0))
            groups = []
            for j in range(per):
                piece = spec[:, 2 * n * j : 2 * n * (j + 1)]
                groups.append(jnp.concatenate([piece[:ROWS], piece[ROWS:]], axis=1))
            high, low = split(jnp.concatenate(groups, axis=0))
            lines = dot(jnp.concatenate([high, low, high], axis=1), y_fwd_ref[...])
            at = pl.multiple_of(i * (per * ROWS), per * ROWS)
            spec_ref[e, 0, pl.ds(at, per * ROWS), :] = lines[:, : 2 * n]
            spec_ref[e, 1, pl.ds(at, per * ROWS), :] = lines[:, 2 * n :]
        return 0

    lax.fori_loop(0, n * n // chunk2, second_pass, 0)

    lane = lax.broadcasted_iota(jnp.int32, (n, 2 * n), 1)
    row = lax.broadcasted_iota(jnp.int32, (n, 2 * n), 0)
    swap_sign = jnp.where(lane < n, 1.0, -1.0)
    exp_sign = jnp.where(lane < n, 1.0, jnp.where(exp_index == 0, 1.0, -1.0))
    anchor = ((lane % n) == 0) & (row == 0)
    swap = lambda v: pltpu.roll(v, n, 1)

    def stack(pieces):
        value = jnp.concatenate(pieces, axis=1)
        turned = jnp.concatenate([swap(v) * swap_sign for v in pieces], axis=1)
        high, low = split(jnp.concatenate([value, turned], axis=0))
        return jnp.concatenate([high, low], axis=0)

    def spectra(i, _):
        for pair in range(KZ_PER_STEP // 2):
            crosses = []
            for odd in range(2):
                kz = i * KZ_PER_STEP + 2 * pair + odd
                lines = [
                    jnp.concatenate([spec_ref[e, p, pl.ds(kz, HALF, stride=ROWS), :] for p in range(2)], axis=0)
                    for e in range(2)
                ]
                both = dot(x_fwd_ref[...], stack(lines))
                both = both[:n] + both[n:]
                one, two = both[:, : 2 * n], both[:, 2 * n :]
                power_one, power_two = one * one, two * two
                power = (power_one + swap(power_one)) * (power_two + swap(power_two))
                gain = lax.rsqrt(jnp.maximum(power, spectral_floor * spectral_floor))
                direct = one * two
                mixed = one * swap(two)
                cross = jnp.where(lane < n, direct + swap(direct), swap(mixed) - mixed) * (gain * exp_sign)
                crosses.append(jnp.where(anchor & (kz == 0), 0.0, cross))
            rows_x = dot(xi_ref[...], stack(crosses))
            rows_x = rows_x[:n] + rows_x[n:]
            high, low = split(jnp.concatenate([rows_x[:, : 2 * n], rows_x[:, 2 * n :]], axis=0))
            lines = dot(jnp.concatenate([high, low], axis=1), yi_ref[...])
            at = pl.multiple_of((i * KZ_PER_STEP + 2 * pair) * n, 2 * n)
            line_ref[pl.ds(at, 2 * n), :] = lines[:, : 2 * n] + lines[:, 2 * n :]
        return 0

    lax.fori_loop(0, KZ_STEPS, spectra, 0)
    done = KZ_STEPS * KZ_PER_STEP
    line_ref[done * n :, :] = jnp.zeros(((ROWS - done) * n, 2 * n), f32)

    pad_rows = jnp.zeros((2 * n - 3 * ROWS, 4 * n), f32)
    lane = lax.broadcasted_iota(jnp.int32, (HALF, 2 * n), 1)
    x_per_step = 8

    def planes(i, _):
        for t in range(x_per_step):
            pair = i * x_per_step + t
            cols = jnp.concatenate([line_ref[pl.ds(2 * pair + p, ROWS, stride=n), :] for p in range(2)], axis=1)
            high = cols.astype(bf16).astype(f32)
            weights = jnp.concatenate([high, cols - high, high, pad_rows], axis=0).astype(bf16)
            both = dot(zi_ref[...], weights)
            cos_part, sin_part = both[:HALF], both[HALF:]
            even_c, odd_c = cos_part[:, : 2 * n], cos_part[:, 2 * n :]
            even_s, odd_s = sin_part[:, : 2 * n], sin_part[:, 2 * n :]
            value = jnp.where(lane < n, even_c, odd_s) + swap(jnp.where(lane < n, odd_c, even_s))
            out_ref[:, pl.ds(pl.multiple_of(pair * 2 * n, 2 * n), 2 * n)] = value
        return 0

    lax.fori_loop(0, HALF // x_per_step, planes, 0)


def share_tables(offsets, fractions):
    both = jnp.concatenate([offsets.astype(f32), fractions], axis=0)
    count = lax.axis_size("depth")
    slab = both.shape[1]
    lane = jnp.arange(2 * count * slab, dtype=jnp.int32) % (count * slab)
    mine = (lane // slab == lax.axis_index("depth")).astype(f32)
    table = jnp.tile(both, (1, 2 * count)) * mine
    step = 1
    while step < count:
        table = table + lax.ppermute(table, "depth", [(i, i ^ step) for i in range(count)])
        step *= 2
    return table


def windows(images, bricks_x, bricks_y):
    exps, tiles, depths = (lax.axis_size(a) for a in ("exp", "tile", "depth"))
    depth_index = lax.axis_index("depth")
    cams = images.shape[1]
    strip = lax.dynamic_slice_in_dim(images[0], depth_index % bricks_y * BRICK, BRICK, axis=2).reshape(cams, -1)

    def linear(e, t, d):
        return ((e % exps) * tiles + t % tiles) * depths + d

    def edge(step, other):
        edge_part = 0 if step == 1 else bricks_x - 1
        return [
            (linear(e, t, d), linear(e + other, t + step, d))
            for e in range(exps)
            for t in range(tiles)
            for d in range(depths)
            if d // bricks_y == edge_part
        ]

    axes = ("exp", "tile", "depth")
    tail = strip[:, -MARGIN * BRICK :]
    head = strip[:, : MARGIN * BRICK]
    pads = []
    for other in (0, 1):
        if bricks_x > 1:
            sent = jnp.where(depth_index // bricks_y == 0, tail, head)
            pads.append(lax.ppermute(sent, axes, edge(1, other) + edge(-1, other))[None])
        else:
            pads.append(jnp.stack([lax.ppermute(tail, axes, edge(1, other)), lax.ppermute(head, axes, edge(-1, other))]))
    other_strip = lax.ppermute(strip, "exp", [(i, (i + 1) % exps) for i in range(exps)])
    return strip, other_strip, pads[0], pads[1]


def per_device(images, offsets, fractions, shifts):
    cams, width, rows_y = images.shape[1:]
    bricks_x, bricks_y = width // BRICK, rows_y // BRICK
    assert cams == 4 and width % BRICK == 0 and rows_y % BRICK == 0
    assert bricks_x * bricks_y == lax.axis_size("depth")
    assert offsets.shape[1] * lax.axis_size("depth") == BRICK
    n = BRICK
    table = share_tables(offsets, fractions)
    strips = windows(images, bricks_x, bricks_y)
    window = (n + 2 * MARGIN) * n
    extended = (width + 2 * MARGIN) * n
    vmem = pl.BlockSpec(memory_space=pltpu.VMEM)
    out = pl.pallas_call(
        functools.partial(kernel, bricks_y=bricks_y),
        out_shape=jax.ShapeDtypeStruct((HALF, n * n), f32),
        in_specs=[pl.BlockSpec(memory_space=pltpu.SMEM)] + [vmem] * 11,
        out_specs=vmem,
        scratch_shapes=[
            pltpu.VMEM((2, 8, extended), f32),
            pltpu.VMEM((2, 8, window), f32),
            pltpu.VMEM((2, 16, window), bf16),
            pltpu.VMEM((2, 16, window), bf16),
            pltpu.VMEM((2, 8 * PAIRS, (n + 2 * REACH) * n), f32),
            pltpu.VMEM((2, 2, HALF * ROWS, 2 * n), f32),
            pltpu.VMEM((ROWS * n, 2 * n), f32),
            pltpu.VMEM((n, 224), bf16),
            pltpu.VMEM((8 * PAIRS, 3 * n), bf16),
            pltpu.VMEM((2 * n, 4 * n), bf16),
            pltpu.VMEM((4 * n, 4 * n), bf16),
            pltpu.VMEM((n, 2 * n), bf16),
        ],
        compiler_params=pltpu.CompilerParams(vmem_limit_bytes=40 * 1024 * 1024),
    )(shifts, *strips, table, *(jnp.asarray(t) for t in constant_tables()))
    return out.reshape(1, HALF, n * n)


def solution(mesh):
    placed = (
        P("exp", None, "tile", None),
        P(None, "depth"),
        P(None, "depth"),
        P(("tile", "depth"), None),
    )
    return jax.shard_map(
        per_device,
        mesh=mesh,
        in_specs=placed,
        out_specs=P(("tile", "depth"), "exp", None),
        check_vma=False,
    )
```

profile of v0, /device:TPU:0, one launch (start us, length us, event | category | flops | bytes accessed | tf_op | source)
XLA Modules:
  0.0 38.7 jit_solution(2545975933305459543)
XLA Ops:
  0.0 0.0 copy-start
  0.0 0.0 copy-start.8
  0.0 0.7 %copy-done.8 = s32[4,8]{1,0:T(4,128)S(1)} copy-done((s32[4,8]{1,0:T(4,128)S(1)}, s32[4,8]{1,0:T(4,128)}, u32[]{:S(2)}) %copy-start.8) | copy-done | bytes 152
  0.7 0.7 %copy-done.9 = f32[4,8]{1,0:T(4,128)S(1)} copy-done((f32[4,8]{1,0:T(4,128)S(1)}, f32[4,8]{1,0:T(4,128)}, u32[]{:S(2)}) %copy-start.9) | copy-done | bytes 152
  1.4 0.1 tile.10
  1.5 3.1 %collective-permute-start.3 = (f32[8,128]{1,0:T(8,128)S(1)}, f32[8,128]{1,0:T(8,128)S(1)}, u32[]{:S(2)}, u32[]{:S(2)}) collective-permute-start(f32[8,128]{1,0:T(8,128)S(1)} %broadcast_multiply_fusion), channel_id=1, source_target_pairs={{0,1},{1,0},{2,3},{3,2},{4,5},{5,4},{6,7},{7,6},{8,9},{9,8},{10,11... | collective-permute-start | bytes 12296 | tf_op jit(solution)/shard_map/ppermute | solution.py:276
  4.6 0.0 copy-done
  4.6 0.0 copy-start.6
  4.6 0.1 constant_dynamic-slice_fusion
  4.8 0.0 copy-start.1
  4.8 0.1 reshape.38.own_ref
  4.9 0.0 copy-start.2
  5.0 0.7 %collective-permute-start.2 = (f32[4,2048]{1,0:T(4,128)S(1)}, f32[4,2048]{1,0:T(4,128)S(1)}, u32[]{:S(2)}, u32[]{:S(2)}) collective-permute-start(f32[4,2048]{1,0:T(4,128)S(1)} %slice_select_fusion), channel_id=1, source_target_pairs={{0,24},{1,25},{2,26},{3,27},{8,16},{9,17},{10,18},{11,19},{16,8},{... | collective-permute-start | bytes 98312 | tf_op jit(solution)/shard_map/ppermute | solution.py:307
  5.7 1.0 %collective-permute-start.1 = (f32[4,2048]{1,0:T(4,128)S(1)}, f32[4,2048]{1,0:T(4,128)S(1)}, u32[]{:S(2)}, u32[]{:S(2)}) collective-permute-start(f32[4,2048]{1,0:T(4,128)S(1)} %slice_select_fusion), channel_id=1, source_target_pairs={{0,8},{1,9},{2,10},{3,11},{8,0},{9,1},{10,2},{11,3},{16,24},{17,25... | collective-permute-start | bytes 98312 | tf_op jit(solution)/shard_map/ppermute | solution.py:307
  6.6 0.5 %collective-permute-start = (f32[4,8192]{1,0:T(4,128)S(1)}, f32[4,8192]{1,0:T(4,128)S(1)}, u32[]{:S(2)}, u32[]{:S(2)}) collective-permute-start(f32[4,8192]{1,0:T(4,128)S(1)} %reshape.38.own_ref), channel_id=1, source_target_pairs={{0,16},{16,0},{1,17},{17,1},{2,18},{18,2},{3,19},{19,3},{4,20},{20... | collective-permute-start | bytes 393224 | tf_op jit(solution)/shard_map/ppermute | solution.py:310
  7.2 0.0 collective-permute-done.3
  7.2 1.6 %collective-permute-start.4 = (f32[8,128]{1,0:T(8,128)S(1)}, f32[8,128]{1,0:T(8,128)S(1)}, u32[]{:S(2)}, u32[]{:S(2)}) collective-permute-start(f32[8,128]{1,0:T(8,128)S(1)} %fusion), channel_id=1, source_target_pairs={{0,2},{1,3},{2,0},{3,1},{4,6},{5,7},{6,4},{7,5},{8,10},{9,11},{10,... | collective-permute-start | bytes 12296 | tf_op jit(solution)/shard_map/ppermute | solution.py:276
  8.8 2.0 %collective-permute-done.4 = f32[8,128]{1,0:T(8,128)S(1)} collective-permute-done((f32[8,128]{1,0:T(8,128)S(1)}, f32[8,128]{1,0:T(8,128)S(1)}, u32[]{:S(2)}, u32[]{:S(2)}) %collective-permute-start.4) | collective-permute-done | bytes 4128 | tf_op jit(solution)/shard_map/ppermute | solution.py:276
  10.8 2.6 %collective-permute-start.5 = (f32[8,128]{1,0:T(8,128)S(1)}, f32[8,128]{1,0:T(8,128)S(1)}, u32[]{:S(2)}, u32[]{:S(2)}) collective-permute-start(f32[8,128]{1,0:T(8,128)S(1)} %add.36), channel_id=1, source_target_pairs={{0,4},{1,5},{2,6},{3,7},{4,0},{5,1},{6,2},{7,3},{8,12},{9,13},{10,... | collective-permute-start | bytes 12296 | tf_op jit(solution)/shard_map/ppermute | solution.py:276
  13.4 1.9 %collective-permute-done.5 = f32[8,128]{1,0:T(8,128)S(1)} collective-permute-done((f32[8,128]{1,0:T(8,128)S(1)}, f32[8,128]{1,0:T(8,128)S(1)}, u32[]{:S(2)}, u32[]{:S(2)}) %collective-permute-start.5) | collective-permute-done | bytes 4128 | tf_op jit(solution)/shard_map/ppermute | solution.py:276
  15.3 0.0 collective-permute-done.2
  15.3 0.0 collective-permute-done.1
  15.3 0.0 collective-permute-done.other_ref
  15.3 0.0 copy-start.7
  15.3 0.0 copy-done.3
  15.3 0.0 copy-done.4
  15.3 0.0 copy-done.5
  15.4 0.0 copy-done.6
  15.4 0.0 copy-done.1
  15.4 0.0 copy-done.2
  15.4 0.6 %copy-done.7 = s32[1,3]{1,0:T(1,128)S(1)} copy-done((s32[1,3]{1,0:T(1,128)S(1)}, s32[1,3]{1,0:T(1,128)}, u32[]{:S(2)}) %copy-start.7) | copy-done | bytes 36
  16.0 22.7 %shard_map.100 = f32[32,4096]{1,0:T(8,128)} custom-call(s32[1,3]{1,0:T(1,128)S(1)} %copy-done.7, f32[4,8192]{1,0:T(4,128)S(1)} %reshape.38.own_ref, f32[4,8192]{1,0:T(4,128)S(1)} %collective-permute-done.other_ref, f32[1,4,2048]{2,1,0:T(4,128)S(1)} %bitcast.6, f32[1,4,2048]{2,1,0:T(4,128)S(1)} %bitcast.5, f32[8,128]{1,0:T(8,128)S(1)} %add.37.tab_ref, ...), custom_call_target="tpu_custom_call" | custom-call | tf_op jit(solution)/shard_map/pallas_call | solution.py:326
  (13 shorter events, 0.1 us)
Async XLA Ops:
  0.0 4.6 %copy-start = (f32[1,4,128,256]{3,2,1,0:T(8,128)S(1)}, f32[1,4,128,256]{3,2,1,0:T(8,128)}, u32[]{:S(2)}) copy-start(f32[1,4,128,256]{3,2,1,0:T(8,128)} %param.10) | copy-start | bytes 1572868
  0.0 0.7 %copy-start.8 = (s32[4,8]{1,0:T(4,128)S(1)}, s32[4,8]{1,0:T(4,128)}, u32[]{:S(2)}) copy-start(s32[4,8]{1,0:T(4,128)} %param.11) | copy-start | bytes 388
  0.7 0.7 %copy-start.9 = (f32[4,8]{1,0:T(4,128)S(1)}, f32[4,8]{1,0:T(4,128)}, u32[]{:S(2)}) copy-start(f32[4,8]{1,0:T(4,128)} %param.12) | copy-start | bytes 388
  1.5 5.6 %collective-permute-start.3 = (f32[8,128]{1,0:T(8,128)S(1)}, f32[8,128]{1,0:T(8,128)S(1)}, u32[]{:S(2)}, u32[]{:S(2)}) collective-permute-start(f32[8,128]{1,0:T(8,128)S(1)} %broadcast_multiply_fusion), channel_id=1, source_target_pairs={{0,1},{1,0},{2,3},{3,2},{4,5},{5,4},{6,7},{7,6},{8,9},{9,8},{10,11... | collective-permute-start | bytes 12296 | tf_op jit(solution)/shard_map/ppermute | solution.py:276
  4.6 10.7 %copy-start.3 = (f32[2,128,128]{2,1,0:T(8,128)S(1)}, f32[2,128,128]{2,1,0:T(8,128)}, u32[]{:S(2)}) copy-start(f32[2,128,128]{2,1,0:T(8,128)} %constant.79.clone.y_inv_ref) | copy-start | bytes 393220
  4.6 10.7 %copy-start.4 = (f32[128,128]{1,0:T(8,128)S(1)}, f32[128,128]{1,0:T(8,128)}, u32[]{:S(2)}) copy-start(f32[128,128]{1,0:T(8,128)} %constant.78.clone.x_inv_ref) | copy-start | bytes 196612
  4.6 10.7 %copy-start.5 = (bf16[128,256]{1,0:T(8,128)(2,1)S(1)}, bf16[128,256]{1,0:T(8,128)(2,1)}, u32[]{:S(2)}) copy-start(bf16[128,256]{1,0:T(8,128)(2,1)} %constant.77.clone.x_fwd_ref) | copy-start | bytes 196612
  4.6 10.7 %copy-start.6 = (bf16[80,192]{1,0:T(8,128)(2,1)S(1)}, bf16[80,192]{1,0:T(8,128)(2,1)}, u32[]{:S(2)}) copy-start(bf16[80,192]{1,0:T(8,128)(2,1)} %constant.75.clone.z_fwd_ref) | copy-start | bytes 92164
  4.8 10.6 %copy-start.1 = (bf16[768,256]{1,0:T(8,128)(2,1)S(1)}, bf16[768,256]{1,0:T(8,128)(2,1)}, u32[]{:S(2)}) copy-start(bf16[768,256]{1,0:T(8,128)(2,1)} %constant.76.clone.y_fwd_ref) | copy-start | bytes 1179652
  4.9 10.5 %copy-start.2 = (f32[2,128,128]{2,1,0:T(8,128)S(1)}, f32[2,128,128]{2,1,0:T(8,128)}, u32[]{:S(2)}) copy-start(f32[2,128,128]{2,1,0:T(8,128)} %constant.80.clone.z_inv_ref) | copy-start | bytes 393220
  5.0 10.3 %collective-permute-start.2 = (f32[4,2048]{1,0:T(4,128)S(1)}, f32[4,2048]{1,0:T(4,128)S(1)}, u32[]{:S(2)}, u32[]{:S(2)}) collective-permute-start(f32[4,2048]{1,0:T(4,128)S(1)} %slice_select_fusion), channel_id=1, source_target_pairs={{0,24},{1,25},{2,26},{3,27},{8,16},{9,17},{10,18},{11,19},{16,8},{... | collective-permute-start | bytes 98312 | tf_op jit(solution)/shard_map/ppermute | solution.py:307
  5.7 9.6 %collective-permute-start.1 = (f32[4,2048]{1,0:T(4,128)S(1)}, f32[4,2048]{1,0:T(4,128)S(1)}, u32[]{:S(2)}, u32[]{:S(2)}) collective-permute-start(f32[4,2048]{1,0:T(4,128)S(1)} %slice_select_fusion), channel_id=1, source_target_pairs={{0,8},{1,9},{2,10},{3,11},{8,0},{9,1},{10,2},{11,3},{16,24},{17,25... | collective-permute-start | bytes 98312 | tf_op jit(solution)/shard_map/ppermute | solution.py:307
  6.6 8.7 %collective-permute-start = (f32[4,8192]{1,0:T(4,128)S(1)}, f32[4,8192]{1,0:T(4,128)S(1)}, u32[]{:S(2)}, u32[]{:S(2)}) collective-permute-start(f32[4,8192]{1,0:T(4,128)S(1)} %reshape.38.own_ref), channel_id=1, source_target_pairs={{0,16},{16,0},{1,17},{17,1},{2,18},{18,2},{3,19},{19,3},{4,20},{20... | collective-permute-start | bytes 393224 | tf_op jit(solution)/shard_map/ppermute | solution.py:310
  7.2 3.6 %collective-permute-start.4 = (f32[8,128]{1,0:T(8,128)S(1)}, f32[8,128]{1,0:T(8,128)S(1)}, u32[]{:S(2)}, u32[]{:S(2)}) collective-permute-start(f32[8,128]{1,0:T(8,128)S(1)} %fusion), channel_id=1, source_target_pairs={{0,2},{1,3},{2,0},{3,1},{4,6},{5,7},{6,4},{7,5},{8,10},{9,11},{10,... | collective-permute-start | bytes 12296 | tf_op jit(solution)/shard_map/ppermute | solution.py:276
  10.8 4.5 %collective-permute-start.5 = (f32[8,128]{1,0:T(8,128)S(1)}, f32[8,128]{1,0:T(8,128)S(1)}, u32[]{:S(2)}, u32[]{:S(2)}) collective-permute-start(f32[8,128]{1,0:T(8,128)S(1)} %add.36), channel_id=1, source_target_pairs={{0,4},{1,5},{2,6},{3,7},{4,0},{5,1},{6,2},{7,3},{8,12},{9,13},{10,... | collective-permute-start | bytes 12296 | tf_op jit(solution)/shard_map/ppermute | solution.py:276
  15.3 0.7 %copy-start.7 = (s32[1,3]{1,0:T(1,128)S(1)}, s32[1,3]{1,0:T(1,128)}, u32[]{:S(2)}) copy-start(s32[1,3]{1,0:T(1,128)} %shift_ref.1) | copy-start | bytes 40
where the time goes:
time: 38.8 us; the launch traced here: 38.7 us
  Pallas kernels  22.7 us (59%)
  starting transfers between devices  9.43 us (24%)
  waiting for transfers between devices  3.96 us (10%)
  local copies, waits for them, and re-layouts  2.4 us (6%)
    pallas_call x1, Pallas kernels, per_device(): pl.pallas_call(functools.partial(kernel, bricks_y=bricks_y), out_shape=ja...  22.7 us
    ppermute x3, starting transfers between devices, share_tables(): lax.ppermute(table, 'depth', [(i, i ^ step) for i in range(count)])  7.23 us
    ppermute x3, waiting for transfers between devices, share_tables(): lax.ppermute(table, 'depth', [(i, i ^ step) for i in range(count)])  3.95 us
    unnamed x20, local copies, waits for them, and re-layouts  2.03 us
    ppermute x2, starting transfers between devices, windows(): lax.ppermute(sent, axes, edge(1, other) + edge(-1, other))[None]  1.67 us
  transfers between devices with their start and end apart: 6, of which 2 were waited for; matrix products, arithmetic and copies ran while one was open for 1% of the time, Pallas kernels for 0%

commit v1 on v0

v1 whole, which is shorter than its diff:
```python
import functools
import math

import jax
import jax.numpy as jnp
import numpy as np
from jax import lax
from jax.experimental import pallas as pl
from jax.experimental.pallas import tpu as pltpu
from jax.sharding import PartitionSpec as P

BRICK = 64
HALF = BRICK // 2
ROWS = 40
MARGIN = 32
SHIFT_LOW = -8
PAIRS = 9
REACH = 18
UNROLL = 2
STEPS = 9
GROUPS = 24
GAP = 72
spectral_floor = 0.01
f32, bf16 = jnp.float32, jnp.bfloat16


def split(value):
    high = value.astype(bf16)
    return high, (value - high.astype(f32)).astype(bf16)


def dot(a, b):
    return jnp.dot(a, b, preferred_element_type=f32)


def tent_value(distance, fraction):
    return jnp.maximum(0.0, 1.0 - jnp.abs(distance - fraction) / 1.5)


def dft_parts():
    wave = np.arange(BRICK)
    angle = (wave[:, None] * wave[None, :] % BRICK) * (2.0 * math.pi / BRICK)
    return np.cos(angle) / math.sqrt(BRICK), np.sin(angle) / math.sqrt(BRICK)


def host_split(value):
    high = value.astype(np.float32).astype(bf16)
    return high, (value - high.astype(np.float64)).astype(np.float32).astype(bf16)


def constant_tables():
    c, s = dft_parts()
    n = BRICK
    zt = np.zeros((2 * ROWS, n))
    zt[: HALF + 1], zt[ROWS : ROWS + HALF + 1] = c[: HALF + 1], -s[: HALF + 1]
    high, low = host_split(zt)
    z_fwd = np.concatenate([high, high, low], axis=1)
    yt = np.zeros((2, 2, n, 2, 2, n))
    for e in range(2):
        yt[0, e, :, 0, e], yt[0, e, :, 1, e] = c, -s
        yt[1, e, :, 0, e], yt[1, e, :, 1, e] = s, c
    high, low = host_split(yt.reshape(4 * n, 4 * n))
    y_fwd = np.concatenate([high, high, low], axis=0)
    high, low = host_split(np.concatenate([c, s], axis=0))
    x_fwd = np.concatenate([high, high, low], axis=1)
    twice = lambda t: np.concatenate([t, t], axis=0)
    x_inv = np.stack([np.tile(twice(t), (1, 2)) for t in (c, s)]).astype(np.float32)
    y_inv = np.stack([np.concatenate([twice(c), twice(-s)], 1).T, np.concatenate([twice(s), twice(c)], 1).T])
    y_inv = y_inv.astype(np.float32)
    weight = np.zeros(2 * GROUPS)
    weight[: HALF + 1] = 2.0
    weight[0] = weight[HALF] = 1.0
    z_inv = []
    for odd in range(2):
        pick = np.concatenate([(t[:, : 2 * GROUPS] * weight)[:, odd::2] for t in (c, -s)], axis=1)
        whole = twice(np.pad(np.tile(pick, (1, 3)), ((0, 0), (0, 4 * n - 6 * GROUPS))))
        z_inv.append(np.stack([whole[:, : 2 * n], whole[:, 2 * n :]]))
    return z_fwd, y_fwd, x_fwd, x_inv, y_inv, np.stack(z_inv).astype(np.float32)


def kernel(
    shift_ref, own_ref, other_ref, pad_own_ref, pad_other_ref, tab_ref,
    z_fwd_ref, y_fwd_ref, x_fwd_ref, x_inv_ref, y_inv_ref, z_inv_ref,
    out_ref,
    raw_ref, first_ref, pack_ref, high_ref, shifted_ref, spec_ref, freq_ref, cross_ref,
    wave_ref, line_ref, back_ref, forward_ref, xi_ref, yi_ref, zi_ref,
    *, bricks_y,
):
    n = BRICK
    w = 2 * n
    exp_index = lax.axis_index("exp")
    part = lax.axis_index("depth") // bricks_y
    columns = n + 2 * MARGIN
    pad = MARGIN * n
    strip = own_ref.shape[1]

    tab = tab_ref[...]
    rows = lax.broadcasted_iota(jnp.int32, (8, w), 0)
    offs = jnp.where(rows < 4, tab, pltpu.roll(tab, 4, 0))
    frac = jnp.where(rows < 4, pltpu.roll(tab, 4, 0), tab)
    total = sum(tent_value(float(d), frac) for d in range(-2, 4))
    parity = (rows >= 4).astype(f32)
    blocks = [tent_value(SHIFT_LOW + 2 * q + parity - offs, frac) / total for q in range(PAIRS)]
    sums = jnp.sum(sum(blocks)[:, :n], axis=1, keepdims=True) / n
    uniform = jnp.log(sums + pltpu.roll(jnp.broadcast_to(sums, (8, w)), 4, 0)[:, :1])
    both_high, back_low = [], []
    for block in blocks:
        high, low = split(block / 4.0)
        both_high += [high.astype(f32)] * 2
        back_low.append(low.astype(f32))
    stacked = jnp.concatenate(both_high + back_low + [jnp.zeros((40, w), f32)], axis=0)
    back_ref[...] = jnp.transpose(stacked)[:n, :224].astype(bf16)
    high, low = split(jnp.concatenate(blocks, axis=0) / n)
    forward_ref[...] = jnp.concatenate([high, low], axis=1)[:, : 3 * n]

    sz, sx, sy = (shift_ref[0, i] + n for i in range(3))
    moved = lax.rem(sx, n)
    turned = jnp.concatenate([x_inv_ref[0, pl.ds(moved, n), :], x_inv_ref[1, pl.ds(moved, n), :]], axis=0)
    high, low = split(turned)
    xi_ref[...] = jnp.concatenate([high, low], axis=1)[:, : 3 * n]
    lane = lax.broadcasted_iota(jnp.int32, (n, w), 1)
    back = lax.rem(w - lax.rem(sy, n), w)
    for ri_out in range(2):
        turned = pltpu.roll(y_inv_ref[ri_out], back, 1)
        pieces = []
        for ri in range(2):
            piece = turned[ri * n : (ri + 1) * n]
            pieces += [jnp.where(lane < n, piece, 0.0), jnp.where(lane < n, 0.0, piece)]
        high, low = split(jnp.concatenate(pieces, axis=0))
        at = slice(ri_out * w, (ri_out + 1) * w)
        yi_ref[0 : 2 * w, at] = high
        yi_ref[2 * w : 4 * w, at] = high
        yi_ref[4 * w :, at] = low
    first = lax.rem(HALF * exp_index + sz, n)
    turned = [jnp.concatenate([z_inv_ref[p, h, pl.ds(first, HALF), :] for h in range(2)], axis=1) for p in range(2)]
    turned = jnp.concatenate(turned, axis=0)
    high, low = split(turned)
    col = lax.broadcasted_iota(jnp.int32, turned.shape, 1)
    zi_ref[...] = jnp.where(col < 4 * GROUPS, high.astype(f32), low.astype(f32)).astype(bf16)[:, : 6 * GROUPS]

    def spread(first_lane, count):
        pieces = [pack_ref[:, pl.ds(first_lane + 2 * w * q, count)] for q in range(PAIRS)]
        pieces += [high_ref[:, pl.ds(first_lane + 2 * w * q, count)] for q in range(0, PAIRS, 2)]
        return jnp.concatenate(pieces, axis=0)

    def pack(both):
        lanes = both.shape[1]
        high = both.astype(bf16).astype(f32)
        pack_ref[:, 0:lanes] = jnp.concatenate([high, both - high], axis=0).astype(bf16)
        later = jnp.concatenate([high[:, 2 * w :], high[:, : 2 * w]], axis=1)
        high_ref[:, 0:lanes] = jnp.concatenate([high, later], axis=0).astype(bf16)

    raw_ref[0:4, 0:pad] = pad_own_ref[0]
    raw_ref[4:8, 0:pad] = pad_other_ref[0]
    raw_ref[0:4, pad : pad + strip] = own_ref[...]
    raw_ref[4:8, pad : pad + strip] = other_ref[...]
    raw_ref[0:4, pad + strip :] = pad_own_ref[pad_own_ref.shape[0] - 1]
    raw_ref[4:8, pad + strip :] = pad_other_ref[pad_other_ref.shape[0] - 1]
    row = lax.broadcasted_iota(jnp.int32, (8, w), 0)
    lane = lax.broadcasted_iota(jnp.int32, (8, w), 1)
    same = (row < 4) == (lane < n)
    swap = lambda v: pltpu.roll(v, n, 1)
    ratio = jnp.log(raw_ref[:, pl.ds(pl.multiple_of(part * (n * n), n * n), columns * n)]) - uniform
    even, odd = [], []
    for k in range(columns // 2):
        here = ratio[:, k * w : (k + 1) * w]
        flipped = pltpu.roll(here, 4, 0)
        even.append(jnp.where(same, here, swap(flipped)))
        odd.append(jnp.where(same, swap(here), flipped))
    cols = []
    for k in range(columns // 2):
        cols += [even[k], jnp.where(row < 4, odd[k], odd[(k + 1) % (columns // 2)])]
    cols = jnp.concatenate(cols, axis=1)
    first_ref[...] = cols
    pack(cols)

    lo_x, hi_x = -REACH, n + REACH
    chunk = 20 * w
    back_w = back_ref[...]
    forward_w = forward_ref[...]

    def first_pass(i, _):
        start = pl.multiple_of(i * chunk, 2 * w)
        logv = dot(back_w, spread(start + (lo_x + SHIFT_LOW + MARGIN) * w, chunk))
        high, low = split(jnp.exp(logv))
        shifted_ref[:, pl.ds(start, chunk)] = dot(forward_w, jnp.concatenate([high, low, high], axis=0))
        return 0

    lax.fori_loop(0, (hi_x - lo_x) * w // chunk, first_pass, 0)

    lo_u, hi_u = -10, n + 10
    count = (hi_u - lo_u) * w
    gathered = sum(
        shifted_ref[8 * q : 8 * q + 8, pl.ds((lo_u - SHIFT_LOW - 2 * q - lo_x) * w, count)] for q in range(PAIRS)
    )
    proj = gathered[:, 2 * w :] + pltpu.roll(gathered[:, w : count - w], 4, 0)
    ratio = first_ref[:, (lo_u + 2 + MARGIN) * w : (hi_u + MARGIN) * w]
    ratio = ratio + (ratio + uniform - jnp.log(proj))
    later = pltpu.roll(jnp.concatenate([ratio[:, w:], ratio[:, :w]], axis=1), 4, 0)
    pack(jnp.where(lax.broadcasted_iota(jnp.int32, ratio.shape, 0) < 4, ratio, later))

    per = 16
    chunk2 = per * w

    def second_pass(i, _):
        start = pl.multiple_of(i * chunk2, chunk2)
        logv = dot(back_w, spread(start, chunk2))
        high, low = split(jnp.exp(logv))
        spec = dot(z_fwd_ref[...], jnp.concatenate([high, low, high], axis=0))
        groups = []
        for j in range(per):
            piece = spec[:, w * j : w * (j + 1)]
            groups.append(jnp.concatenate([piece[:ROWS], piece[ROWS:]], axis=1))
        high, low = split(jnp.concatenate(groups, axis=0))
        lines = dot(jnp.concatenate([high, low, high], axis=1), y_fwd_ref[...])
        at = pl.multiple_of(i * (per * ROWS), per * ROWS)
        spec_ref[0, pl.ds(at, per * ROWS), :] = lines[:, :w]
        spec_ref[1, pl.ds(at, per * ROWS), :] = lines[:, w:]
        return 0

    lax.fori_loop(0, n // per, second_pass, 0)

    lane = lax.broadcasted_iota(jnp.int32, (n, w), 1)
    row = lax.broadcasted_iota(jnp.int32, (n, w), 0)
    own_sign = jnp.where(exp_index == 0, 1.0, -1.0)
    exp_sign = jnp.where(lane < n, own_sign, -own_sign)
    anchor = (lane == 0) & (row == 0)

    def three(value):
        high, low = split(value)
        return jnp.concatenate([high, low, high], axis=0)

    def spectra(i, _):
        for t in range(UNROLL):
            at = jnp.maximum(i - 2, 0) * UNROLL + t
            both = dot(xi_ref[...], cross_ref[t])
            re = both[:n, :w] - both[n:, w:]
            im = both[:n, w:] + both[n:, :w]
            high, low = split(jnp.concatenate([re, im], axis=1))
            wave_ref[0, pl.ds(pl.multiple_of(at * n, n), n), :] = high
            wave_ref[1, pl.ds(pl.multiple_of(at * n, n), n), :] = low
        for t in range(UNROLL):
            re_a, im_a = freq_ref[t, 0, 0], freq_ref[t, 0, 1]
            re_b, im_b = freq_ref[t, 1, 0], freq_ref[t, 1, 1]
            re_one = jnp.where(lane < n, re_a, re_b)
            im_one = jnp.where(lane < n, im_a, im_b)
            re_two = swap(jnp.where(lane < n, re_b, re_a))
            im_two = swap(jnp.where(lane < n, im_b, im_a))
            power = (re_one * re_one + im_one * im_one) * (re_two * re_two + im_two * im_two)
            gain = lax.rsqrt(jnp.maximum(power, spectral_floor * spectral_floor))
            if t == 0:
                gain = jnp.where(anchor & (i == 1), 0.0, gain)
            cross_re = (re_one * re_two + im_one * im_two) * gain
            cross_im = (re_one * im_two - im_one * re_two) * (gain * exp_sign)
            cross_ref[t] = three(jnp.concatenate([cross_re, cross_im], axis=1))
        for t in range(UNROLL):
            for odd in range(2):
                kz = jnp.minimum(i, STEPS - 1) * (2 * UNROLL) + 2 * t + odd
                lines = [spec_ref[ri, pl.ds(kz, n, stride=ROWS), :] for ri in range(2)]
                both = dot(x_fwd_ref[...], three(jnp.concatenate(lines, axis=1)))
                freq_ref[t, odd, 0] = both[:n, :w] + both[n:, w:]
                freq_ref[t, odd, 1] = both[:n, w:] - both[n:, :w]
        return 0

    lax.fori_loop(0, STEPS + 2, spectra, 0)

    done = STEPS * UNROLL
    per = done // 2

    def inverse_y(i, _):
        at = pl.multiple_of(i * (per * n), per * n)
        high, low = wave_ref[0, pl.ds(at, per * n), :], wave_ref[1, pl.ds(at, per * n), :]
        lines = dot(jnp.concatenate([high, low, high], axis=1), yi_ref[...])
        for t in range(per):
            to = pl.multiple_of((i * per + t) * GAP, 8)
            line_ref[0, pl.ds(to, n), :] = lines[t * n : (t + 1) * n, :w]
            line_ref[1, pl.ds(to, n), :] = lines[t * n : (t + 1) * n, w:]
        return 0

    lax.fori_loop(0, 2, inverse_y, 0)
    line_ref[:, done * GAP :, :] = jnp.zeros((2, (GROUPS - done) * GAP, w), f32)

    lane = lax.broadcasted_iota(jnp.int32, (HALF, w), 1)
    x_per_step = 8

    def planes(i, _):
        for t in range(x_per_step):
            pair = i * x_per_step + t
            cols = jnp.concatenate(
                [
                    jnp.concatenate([line_ref[ri, pl.ds(2 * pair + p, GROUPS, stride=GAP), :] for ri in range(2)], axis=0)
                    for p in range(2)
                ],
                axis=1,
            )
            both = dot(zi_ref[...], three(cols))
            a_even, a_odd = both[:HALF, :w], both[:HALF, w:]
            b_even, b_odd = both[HALF:, :w], both[HALF:, w:]
            value = jnp.where(lane < n, a_even, b_odd) + swap(jnp.where(lane < n, a_odd, b_even))
            out_ref[:, pl.ds(pl.multiple_of(pair * w, w), w)] = value
        return 0

    lax.fori_loop(0, HALF // x_per_step, planes, 0)


def share_tables(offsets, fractions):
    both = jnp.concatenate([offsets.astype(f32), fractions], axis=0)
    count = lax.axis_size("depth")
    slab = both.shape[1]
    lane = jnp.arange(2 * count * slab, dtype=jnp.int32) % (count * slab)
    mine = (lane // slab == lax.axis_index("depth")).astype(f32)
    table = jnp.tile(both, (1, 2 * count)) * mine
    step = 1
    while step < count:
        table = table + lax.ppermute(table, "depth", [(i, i ^ step) for i in range(count)])
        step *= 2
    return table


def windows(images, bricks_x, bricks_y):
    exps, tiles, depths = (lax.axis_size(a) for a in ("exp", "tile", "depth"))
    depth_index = lax.axis_index("depth")
    cams = images.shape[1]
    strip = lax.dynamic_slice_in_dim(images[0], depth_index % bricks_y * BRICK, BRICK, axis=2).reshape(cams, -1)

    def linear(e, t, d):
        return ((e % exps) * tiles + t % tiles) * depths + d

    def edge(step, other):
        edge_part = 0 if step == 1 else bricks_x - 1
        return [
            (linear(e, t, d), linear(e + other, t + step, d))
            for e in range(exps)
            for t in range(tiles)
            for d in range(depths)
            if d // bricks_y == edge_part
        ]

    axes = ("exp", "tile", "depth")
    tail = strip[:, -MARGIN * BRICK :]
    head = strip[:, : MARGIN * BRICK]
    pads = []
    for other in (0, 1):
        if bricks_x > 1:
            sent = jnp.where(depth_index // bricks_y == 0, tail, head)
            pads.append(lax.ppermute(sent, axes, edge(1, other) + edge(-1, other))[None])
        else:
            pads.append(jnp.stack([lax.ppermute(tail, axes, edge(1, other)), lax.ppermute(head, axes, edge(-1, other))]))
    other_strip = lax.ppermute(strip, "exp", [(i, (i + 1) % exps) for i in range(exps)])
    return strip, other_strip, pads[0], pads[1]


def per_device(images, offsets, fractions, shifts):
    cams, width, rows_y = images.shape[1:]
    bricks_x, bricks_y = width // BRICK, rows_y // BRICK
    assert cams == 4 and width % BRICK == 0 and rows_y % BRICK == 0
    assert bricks_x * bricks_y == lax.axis_size("depth")
    assert offsets.shape[1] * lax.axis_size("depth") == BRICK
    n = BRICK
    table = share_tables(offsets, fractions)
    strips = windows(images, bricks_x, bricks_y)
    window = (n + 2 * MARGIN) * n
    extended = (width + 2 * MARGIN) * n
    vmem = pl.BlockSpec(memory_space=pltpu.VMEM)
    out = pl.pallas_call(
        functools.partial(kernel, bricks_y=bricks_y),
        out_shape=jax.ShapeDtypeStruct((HALF, n * n), f32),
        in_specs=[pl.BlockSpec(memory_space=pltpu.SMEM)] + [vmem] * 11,
        out_specs=vmem,
        scratch_shapes=[
            pltpu.VMEM((8, extended), f32),
            pltpu.VMEM((8, 2 * window), f32),
            pltpu.VMEM((16, 2 * window), bf16),
            pltpu.VMEM((16, 2 * window), bf16),
            pltpu.VMEM((8 * PAIRS, (n + 2 * REACH) * 2 * n), f32),
            pltpu.VMEM((2, n * ROWS, 2 * n), f32),
            pltpu.VMEM((UNROLL, 2, 2, n, 2 * n), f32),
            pltpu.VMEM((UNROLL, 3 * n, 4 * n), bf16),
            pltpu.VMEM((2, STEPS * UNROLL * n, 4 * n), bf16),
            pltpu.VMEM((2, GROUPS * GAP, 2 * n), f32),
            pltpu.VMEM((n, 224), bf16),
            pltpu.VMEM((8 * PAIRS, 3 * n), bf16),
            pltpu.VMEM((2 * n, 3 * n), bf16),
            pltpu.VMEM((12 * n, 4 * n), bf16),
            pltpu.VMEM((n, 6 * GROUPS), bf16),
        ],
        compiler_params=pltpu.CompilerParams(vmem_limit_bytes=40 * 1024 * 1024),
    )(shifts, *strips, table, *(jnp.asarray(t) for t in constant_tables()))
    return out.reshape(1, HALF, n * n)


def solution(mesh):
    placed = (
        P("exp", None, "tile", None),
        P(None, "depth"),
        P(None, "depth"),
        P(("tile", "depth"), None),
    )
    return jax.shard_map(
        per_device,
        mesh=mesh,
        in_specs=placed,
        out_specs=P(("tile", "depth"), "exp", None),
        check_vma=False,
    )
```

time: 38.8 us -> 29.1 us (0.75)
  Pallas kernels: 22.7 us -> 12.9 us
    pallas_call x1, Pallas kernels: 22.7 us -> 12.9 us  [per_device(): pl.pallas_call(functools.partial(kernel, bricks_y=bricks_y), out_shape=ja...]
where the time goes in v1:
time: 29.1 us; the launch traced here: 28.9 us
  Pallas kernels  12.9 us (44%)
  starting transfers between devices  9.43 us (32%)
  waiting for transfers between devices  3.96 us (14%)
  local copies, waits for them, and re-layouts  2.4 us (8%)
    pallas_call x1, Pallas kernels, per_device(): pl.pallas_call(functools.partial(kernel, bricks_y=bricks_y), out_shape=ja...  12.9 us
    ppermute x3, starting transfers between devices, share_tables(): lax.ppermute(table, 'depth', [(i, i ^ step) for i in range(count)])  7.23 us
    ppermute x3, waiting for transfers between devices, share_tables(): lax.ppermute(table, 'depth', [(i, i ^ step) for i in range(count)])  3.95 us
    unnamed x20, local copies, waits for them, and re-layouts  2.03 us
    ppermute x2, starting transfers between devices, windows(): lax.ppermute(sent, axes, edge(1, other) + edge(-1, other))[None]  1.67 us
  transfers between devices with their start and end apart: 6, of which 2 were waited for; matrix products, arithmetic and copies ran while one was open for 1% of the time, Pallas kernels for 0%

profile of v1, /device:TPU:0, one launch (start us, length us, event | category | flops | bytes accessed | tf_op | source)
XLA Modules:
  0.0 28.9 jit_solution(3314287893310487595)
XLA Ops:
  0.0 0.0 copy-start
  0.0 0.0 copy-start.8
  0.0 0.7 %copy-done.8 = s32[4,8]{1,0:T(4,128)S(1)} copy-done((s32[4,8]{1,0:T(4,128)S(1)}, s32[4,8]{1,0:T(4,128)}, u32[]{:S(2)}) %copy-start.8) | copy-done | bytes 152
  0.7 0.7 %copy-done.9 = f32[4,8]{1,0:T(4,128)S(1)} copy-done((f32[4,8]{1,0:T(4,128)S(1)}, f32[4,8]{1,0:T(4,128)}, u32[]{:S(2)}) %copy-start.9) | copy-done | bytes 152
  1.4 0.1 tile.10
  1.5 3.1 %collective-permute-start.3 = (f32[8,128]{1,0:T(8,128)S(1)}, f32[8,128]{1,0:T(8,128)S(1)}, u32[]{:S(2)}, u32[]{:S(2)}) collective-permute-start(f32[8,128]{1,0:T(8,128)S(1)} %broadcast_multiply_fusion), channel_id=1, source_target_pairs={{0,1},{1,0},{2,3},{3,2},{4,5},{5,4},{6,7},{7,6},{8,9},{9,8},{10,11... | collective-permute-start | bytes 12296 | tf_op jit(solution)/shard_map/ppermute | solution.py:315
  4.6 0.0 copy-done
  4.6 0.0 copy-start.6
  4.6 0.1 constant_dynamic-slice_fusion
  4.8 0.0 copy-start.1
  4.8 0.1 reshape.38.own_ref
  4.9 0.0 copy-start.3
  5.0 0.7 %collective-permute-start.2 = (f32[4,2048]{1,0:T(4,128)S(1)}, f32[4,2048]{1,0:T(4,128)S(1)}, u32[]{:S(2)}, u32[]{:S(2)}) collective-permute-start(f32[4,2048]{1,0:T(4,128)S(1)} %slice_select_fusion), channel_id=1, source_target_pairs={{0,24},{1,25},{2,26},{3,27},{8,16},{9,17},{10,18},{11,19},{16,8},{... | collective-permute-start | bytes 98312 | tf_op jit(solution)/shard_map/ppermute | solution.py:346
  5.7 1.0 %collective-permute-start.1 = (f32[4,2048]{1,0:T(4,128)S(1)}, f32[4,2048]{1,0:T(4,128)S(1)}, u32[]{:S(2)}, u32[]{:S(2)}) collective-permute-start(f32[4,2048]{1,0:T(4,128)S(1)} %slice_select_fusion), channel_id=1, source_target_pairs={{0,8},{1,9},{2,10},{3,11},{8,0},{9,1},{10,2},{11,3},{16,24},{17,25... | collective-permute-start | bytes 98312 | tf_op jit(solution)/shard_map/ppermute | solution.py:346
  6.6 0.5 %collective-permute-start = (f32[4,8192]{1,0:T(4,128)S(1)}, f32[4,8192]{1,0:T(4,128)S(1)}, u32[]{:S(2)}, u32[]{:S(2)}) collective-permute-start(f32[4,8192]{1,0:T(4,128)S(1)} %reshape.38.own_ref), channel_id=1, source_target_pairs={{0,16},{16,0},{1,17},{17,1},{2,18},{18,2},{3,19},{19,3},{4,20},{20... | collective-permute-start | bytes 393224 | tf_op jit(solution)/shard_map/ppermute | solution.py:349
  7.2 0.0 collective-permute-done.3
  7.2 1.6 %collective-permute-start.4 = (f32[8,128]{1,0:T(8,128)S(1)}, f32[8,128]{1,0:T(8,128)S(1)}, u32[]{:S(2)}, u32[]{:S(2)}) collective-permute-start(f32[8,128]{1,0:T(8,128)S(1)} %fusion), channel_id=1, source_target_pairs={{0,2},{1,3},{2,0},{3,1},{4,6},{5,7},{6,4},{7,5},{8,10},{9,11},{10,... | collective-permute-start | bytes 12296 | tf_op jit(solution)/shard_map/ppermute | solution.py:315
  8.8 2.0 %collective-permute-done.4 = f32[8,128]{1,0:T(8,128)S(1)} collective-permute-done((f32[8,128]{1,0:T(8,128)S(1)}, f32[8,128]{1,0:T(8,128)S(1)}, u32[]{:S(2)}, u32[]{:S(2)}) %collective-permute-start.4) | collective-permute-done | bytes 4128 | tf_op jit(solution)/shard_map/ppermute | solution.py:315
  10.8 2.6 %collective-permute-start.5 = (f32[8,128]{1,0:T(8,128)S(1)}, f32[8,128]{1,0:T(8,128)S(1)}, u32[]{:S(2)}, u32[]{:S(2)}) collective-permute-start(f32[8,128]{1,0:T(8,128)S(1)} %add.36), channel_id=1, source_target_pairs={{0,4},{1,5},{2,6},{3,7},{4,0},{5,1},{6,2},{7,3},{8,12},{9,13},{10,... | collective-permute-start | bytes 12296 | tf_op jit(solution)/shard_map/ppermute | solution.py:315
  13.4 1.9 %collective-permute-done.5 = f32[8,128]{1,0:T(8,128)S(1)} collective-permute-done((f32[8,128]{1,0:T(8,128)S(1)}, f32[8,128]{1,0:T(8,128)S(1)}, u32[]{:S(2)}, u32[]{:S(2)}) %collective-permute-start.5) | collective-permute-done | bytes 4128 | tf_op jit(solution)/shard_map/ppermute | solution.py:315
  15.3 0.0 collective-permute-done.2
  15.3 0.0 collective-permute-done.1
  15.3 0.0 collective-permute-done.other_ref
  15.3 0.0 copy-start.7
  15.3 0.0 copy-done.2
  15.3 0.0 copy-done.4
  15.3 0.0 copy-done.5
  15.4 0.0 copy-done.6
  15.4 0.0 copy-done.1
  15.4 0.0 copy-done.3
  15.4 0.6 %copy-done.7 = s32[1,3]{1,0:T(1,128)S(1)} copy-done((s32[1,3]{1,0:T(1,128)S(1)}, s32[1,3]{1,0:T(1,128)}, u32[]{:S(2)}) %copy-start.7) | copy-done | bytes 36
  16.0 12.9 %shard_map.100 = f32[32,4096]{1,0:T(8,128)} custom-call(s32[1,3]{1,0:T(1,128)S(1)} %copy-done.7, f32[4,8192]{1,0:T(4,128)S(1)} %reshape.38.own_ref, f32[4,8192]{1,0:T(4,128)S(1)} %collective-permute-done.other_ref, f32[1,4,2048]{2,1,0:T(4,128)S(1)} %bitcast.6, f32[1,4,2048]{2,1,0:T(4,128)S(1)} %bitcast.5, f32[8,128]{1,0:T(8,128)S(1)} %add.37.tab_ref, ...), custom_call_target="tpu_custom_call" | custom-call | tf_op jit(solution)/shard_map/pallas_call | solution.py:365
  (13 shorter events, 0.1 us)
Async XLA Ops:
  0.0 4.6 %copy-start = (f32[1,4,128,256]{3,2,1,0:T(8,128)S(1)}, f32[1,4,128,256]{3,2,1,0:T(8,128)}, u32[]{:S(2)}) copy-start(f32[1,4,128,256]{3,2,1,0:T(8,128)} %param.10) | copy-start | bytes 1572868
  0.0 0.7 %copy-start.8 = (s32[4,8]{1,0:T(4,128)S(1)}, s32[4,8]{1,0:T(4,128)}, u32[]{:S(2)}) copy-start(s32[4,8]{1,0:T(4,128)} %param.11) | copy-start | bytes 388
  0.7 0.7 %copy-start.9 = (f32[4,8]{1,0:T(4,128)S(1)}, f32[4,8]{1,0:T(4,128)}, u32[]{:S(2)}) copy-start(f32[4,8]{1,0:T(4,128)} %param.12) | copy-start | bytes 388
  1.5 5.6 %collective-permute-start.3 = (f32[8,128]{1,0:T(8,128)S(1)}, f32[8,128]{1,0:T(8,128)S(1)}, u32[]{:S(2)}, u32[]{:S(2)}) collective-permute-start(f32[8,128]{1,0:T(8,128)S(1)} %broadcast_multiply_fusion), channel_id=1, source_target_pairs={{0,1},{1,0},{2,3},{3,2},{4,5},{5,4},{6,7},{7,6},{8,9},{9,8},{10,11... | collective-permute-start | bytes 12296 | tf_op jit(solution)/shard_map/ppermute | solution.py:315
  4.6 10.7 %copy-start.2 = (f32[2,2,128,128]{3,2,1,0:T(8,128)S(1)}, f32[2,2,128,128]{3,2,1,0:T(8,128)}, u32[]{:S(2)}) copy-start(f32[2,2,128,128]{3,2,1,0:T(8,128)} %constant.80.clone.z_inv_ref) | copy-start | bytes 786436
  4.6 10.7 %copy-start.4 = (f32[2,128,128]{2,1,0:T(8,128)S(1)}, f32[2,128,128]{2,1,0:T(8,128)}, u32[]{:S(2)}) copy-start(f32[2,128,128]{2,1,0:T(8,128)} %constant.78.clone.x_inv_ref) | copy-start | bytes 393220
  4.6 10.7 %copy-start.5 = (bf16[128,192]{1,0:T(8,128)(2,1)S(1)}, bf16[128,192]{1,0:T(8,128)(2,1)}, u32[]{:S(2)}) copy-start(bf16[128,192]{1,0:T(8,128)(2,1)} %constant.77.clone.x_fwd_ref) | copy-start | bytes 147460
  4.6 10.7 %copy-start.6 = (bf16[80,192]{1,0:T(8,128)(2,1)S(1)}, bf16[80,192]{1,0:T(8,128)(2,1)}, u32[]{:S(2)}) copy-start(bf16[80,192]{1,0:T(8,128)(2,1)} %constant.75.clone.z_fwd_ref) | copy-start | bytes 92164
  4.8 10.6 %copy-start.1 = (bf16[768,256]{1,0:T(8,128)(2,1)S(1)}, bf16[768,256]{1,0:T(8,128)(2,1)}, u32[]{:S(2)}) copy-start(bf16[768,256]{1,0:T(8,128)(2,1)} %constant.76.clone.y_fwd_ref) | copy-start | bytes 1179652
  4.9 10.5 %copy-start.3 = (f32[2,128,128]{2,1,0:T(8,128)S(1)}, f32[2,128,128]{2,1,0:T(8,128)}, u32[]{:S(2)}) copy-start(f32[2,128,128]{2,1,0:T(8,128)} %constant.79.clone.y_inv_ref) | copy-start | bytes 393220
  5.0 10.3 %collective-permute-start.2 = (f32[4,2048]{1,0:T(4,128)S(1)}, f32[4,2048]{1,0:T(4,128)S(1)}, u32[]{:S(2)}, u32[]{:S(2)}) collective-permute-start(f32[4,2048]{1,0:T(4,128)S(1)} %slice_select_fusion), channel_id=1, source_target_pairs={{0,24},{1,25},{2,26},{3,27},{8,16},{9,17},{10,18},{11,19},{16,8},{... | collective-permute-start | bytes 98312 | tf_op jit(solution)/shard_map/ppermute | solution.py:346
  5.7 9.6 %collective-permute-start.1 = (f32[4,2048]{1,0:T(4,128)S(1)}, f32[4,2048]{1,0:T(4,128)S(1)}, u32[]{:S(2)}, u32[]{:S(2)}) collective-permute-start(f32[4,2048]{1,0:T(4,128)S(1)} %slice_select_fusion), channel_id=1, source_target_pairs={{0,8},{1,9},{2,10},{3,11},{8,0},{9,1},{10,2},{11,3},{16,24},{17,25... | collective-permute-start | bytes 98312 | tf_op jit(solution)/shard_map/ppermute | solution.py:346
  6.6 8.7 %collective-permute-start = (f32[4,8192]{1,0:T(4,128)S(1)}, f32[4,8192]{1,0:T(4,128)S(1)}, u32[]{:S(2)}, u32[]{:S(2)}) collective-permute-start(f32[4,8192]{1,0:T(4,128)S(1)} %reshape.38.own_ref), channel_id=1, source_target_pairs={{0,16},{16,0},{1,17},{17,1},{2,18},{18,2},{3,19},{19,3},{4,20},{20... | collective-permute-start | bytes 393224 | tf_op jit(solution)/shard_map/ppermute | solution.py:349
  7.2 3.6 %collective-permute-start.4 = (f32[8,128]{1,0:T(8,128)S(1)}, f32[8,128]{1,0:T(8,128)S(1)}, u32[]{:S(2)}, u32[]{:S(2)}) collective-permute-start(f32[8,128]{1,0:T(8,128)S(1)} %fusion), channel_id=1, source_target_pairs={{0,2},{1,3},{2,0},{3,1},{4,6},{5,7},{6,4},{7,5},{8,10},{9,11},{10,... | collective-permute-start | bytes 12296 | tf_op jit(solution)/shard_map/ppermute | solution.py:315
  10.8 4.5 %collective-permute-start.5 = (f32[8,128]{1,0:T(8,128)S(1)}, f32[8,128]{1,0:T(8,128)S(1)}, u32[]{:S(2)}, u32[]{:S(2)}) collective-permute-start(f32[8,128]{1,0:T(8,128)S(1)} %add.36), channel_id=1, source_target_pairs={{0,4},{1,5},{2,6},{3,7},{4,0},{5,1},{6,2},{7,3},{8,12},{9,13},{10,... | collective-permute-start | bytes 12296 | tf_op jit(solution)/shard_map/ppermute | solution.py:315
  15.3 0.7 %copy-start.7 = (s32[1,3]{1,0:T(1,128)S(1)}, s32[1,3]{1,0:T(1,128)}, u32[]{:S(2)}) copy-start(s32[1,3]{1,0:T(1,128)} %shift_ref.1) | copy-start | bytes 40

commit v2 on v1

--- a/solution.py
+++ b/solution.py
@@ -8,6 +8,7 @@
 from jax.experimental import pallas as pl
 from jax.experimental.pallas import tpu as pltpu
 from jax.sharding import PartitionSpec as P
+
 
 BRICK = 64
 HALF = BRICK // 2
@@ -79,11 +80,12 @@
 
 
 def kernel(
-    shift_ref, own_ref, other_ref, pad_own_ref, pad_other_ref, tab_ref,
+    shift_hbm, own_ref, other_ref, pad_own_ref, pad_other_ref, tab_ref,
     z_fwd_ref, y_fwd_ref, x_fwd_ref, x_inv_ref, y_inv_ref, z_inv_ref,
-    out_ref,
+    out_hbm,
     raw_ref, first_ref, pack_ref, high_ref, shifted_ref, spec_ref, freq_ref, cross_ref,
     wave_ref, line_ref, back_ref, forward_ref, xi_ref, yi_ref, zi_ref,
+    out_ref, shift_ref, shift_sem, out_sem,
     *, bricks_y,
 ):
     n = BRICK
@@ -93,6 +95,8 @@
     columns = n + 2 * MARGIN
     pad = MARGIN * n
     strip = own_ref.shape[1]
+    shift_copy = pltpu.make_async_copy(shift_hbm, shift_ref, shift_sem)
+    shift_copy.start()
 
     tab = tab_ref[...]
     rows = lax.broadcasted_iota(jnp.int32, (8, w), 0)
@@ -113,6 +117,68 @@
     high, low = split(jnp.concatenate(blocks, axis=0) / n)
     forward_ref[...] = jnp.concatenate([high, low], axis=1)[:, : 3 * n]
 
+    def spread(first_lane, count):
+        pieces = [pack_ref[:, pl.ds(first_lane + 2 * w * q, count)] for q in range(PAIRS)]
+        pieces += [high_ref[:, pl.ds(first_lane + 2 * w * q, count)] for q in range(0, PAIRS, 2)]
+        return jnp.concatenate(pieces, axis=0)
+
+    def pack(both):
+        lanes = both.shape[1]
+        high = both.astype(bf16).astype(f32)
+        pack_ref[:, 0:lanes] = jnp.concatenate([high, both - high], axis=0).astype(bf16)
+        later = jnp.concatenate([high[:, 2 * w :], high[:, : 2 * w]], axis=1)
+        high_ref[:, 0:lanes] = jnp.concatenate([high, later], axis=0).astype(bf16)
+
+    raw_ref[0:4, 0:pad] = pad_own_ref[0]
+    raw_ref[4:8, 0:pad] = pad_other_ref[0]
+    raw_ref[0:4, pad : pad + strip] = own_ref[...]
+    raw_ref[4:8, pad : pad + strip] = other_ref[...]
+    raw_ref[0:4, pad + strip :] = pad_own_ref[pad_own_ref.shape[0] - 1]
+    raw_ref[4:8, pad + strip :] = pad_other_ref[pad_other_ref.shape[0] - 1]
+    row = lax.broadcasted_iota(jnp.int32, (8, w), 0)
+    lane = lax.broadcasted_iota(jnp.int32, (8, w), 1)
+    same = (row < 4) == (lane < n)
+    swap = lambda v: pltpu.roll(v, n, 1)
+    ratio = jnp.log(raw_ref[:, pl.ds(pl.multiple_of(part * (n * n), n * n), columns * n)]) - uniform
+    even, odd = [], []
+    for k in range(columns // 2):
+        here = ratio[:, k * w : (k + 1) * w]
+        flipped = pltpu.roll(here, 4, 0)
+        even.append(jnp.where(same, here, swap(flipped)))
+        odd.append(jnp.where(same, swap(here), flipped))
+    cols = []
+    for k in range(columns // 2):
+        cols += [even[k], jnp.where(row < 4, odd[k], odd[(k + 1) % (columns // 2)])]
+    cols = jnp.concatenate(cols, axis=1)
+    first_ref[...] = cols
+    pack(cols)
+
+    lo_x, hi_x = -REACH, n + REACH
+    chunk = 20 * w
+    back_w = back_ref[...]
+    forward_w = forward_ref[...]
+
+    def first_pass(i, _):
+        start = pl.multiple_of(i * chunk, 2 * w)
+        logv = dot(back_w, spread(start + (lo_x + SHIFT_LOW + MARGIN) * w, chunk))
+        high, low = split(jnp.exp(logv))
+        shifted_ref[:, pl.ds(start, chunk)] = dot(forward_w, jnp.concatenate([high, low, high], axis=0))
+        return 0
+
+    lax.fori_loop(0, (hi_x - lo_x) * w // chunk, first_pass, 0)
+
+    lo_u, hi_u = -10, n + 10
+    count = (hi_u - lo_u) * w
+    gathered = sum(
+        shifted_ref[8 * q : 8 * q + 8, pl.ds((lo_u - SHIFT_LOW - 2 * q - lo_x) * w, count)] for q in range(PAIRS)
+    )
+    proj = gathered[:, 2 * w :] + pltpu.roll(gathered[:, w : count - w], 4, 0)
+    ratio = first_ref[:, (lo_u + 2 + MARGIN) * w : (hi_u + MARGIN) * w]
+    ratio = ratio + (ratio + uniform - jnp.log(proj))
+    later = pltpu.roll(jnp.concatenate([ratio[:, w:], ratio[:, :w]], axis=1), 4, 0)
+    pack(jnp.where(lax.broadcasted_iota(jnp.int32, ratio.shape, 0) < 4, ratio, later))
+
+    shift_copy.wait()
     sz, sx, sy = (shift_ref[0, i] + n for i in range(3))
     moved = lax.rem(sx, n)
     turned = jnp.concatenate([x_inv_ref[0, pl.ds(moved, n), :], x_inv_ref[1, pl.ds(moved, n), :]], axis=0)
@@ -137,67 +203,6 @@
     high, low = split(turned)
     col = lax.broadcasted_iota(jnp.int32, turned.shape, 1)
     zi_ref[...] = jnp.where(col < 4 * GROUPS, high.astype(f32), low.astype(f32)).astype(bf16)[:, : 6 * GROUPS]
-
-    def spread(first_lane, count):
-        pieces = [pack_ref[:, pl.ds(first_lane + 2 * w * q, count)] for q in range(PAIRS)]
-        pieces += [high_ref[:, pl.ds(first_lane + 2 * w * q, count)] for q in range(0, PAIRS, 2)]
-        return jnp.concatenate(pieces, axis=0)
-
-    def pack(both):
-        lanes = both.shape[1]
-        high = both.astype(bf16).astype(f32)
-        pack_ref[:, 0:lanes] = jnp.concatenate([high, both - high], axis=0).astype(bf16)
-        later = jnp.concatenate([high[:, 2 * w :], high[:, : 2 * w]], axis=1)
-        high_ref[:, 0:lanes] = jnp.concatenate([high, later], axis=0).astype(bf16)
-
-    raw_ref[0:4, 0:pad] = pad_own_ref[0]
-    raw_ref[4:8, 0:pad] = pad_other_ref[0]
-    raw_ref[0:4, pad : pad + strip] = own_ref[...]
-    raw_ref[4:8, pad : pad + strip] = other_ref[...]
-    raw_ref[0:4, pad + strip :] = pad_own_ref[pad_own_ref.shape[0] - 1]
-    raw_ref[4:8, pad + strip :] = pad_other_ref[pad_other_ref.shape[0] - 1]
-    row = lax.broadcasted_iota(jnp.int32, (8, w), 0)
-    lane = lax.broadcasted_iota(jnp.int32, (8, w), 1)
-    same = (row < 4) == (lane < n)
-    swap = lambda v: pltpu.roll(v, n, 1)
-    ratio = jnp.log(raw_ref[:, pl.ds(pl.multiple_of(part * (n * n), n * n), columns * n)]) - uniform
-    even, odd = [], []
-    for k in range(columns // 2):
-        here = ratio[:, k * w : (k + 1) * w]
-        flipped = pltpu.roll(here, 4, 0)
-        even.append(jnp.where(same, here, swap(flipped)))
-        odd.append(jnp.where(same, swap(here), flipped))
-    cols = []
-    for k in range(columns // 2):
-        cols += [even[k], jnp.where(row < 4, odd[k], odd[(k + 1) % (columns // 2)])]
-    cols = jnp.concatenate(cols, axis=1)
-    first_ref[...] = cols
-    pack(cols)
-
-    lo_x, hi_x = -REACH, n + REACH
-    chunk = 20 * w
-    back_w = back_ref[...]
-    forward_w = forward_ref[...]
-
-    def first_pass(i, _):
-        start = pl.multiple_of(i * chunk, 2 * w)
-        logv = dot(back_w, spread(start + (lo_x + SHIFT_LOW + MARGIN) * w, chunk))
-        high, low = split(jnp.exp(logv))
-        shifted_ref[:, pl.ds(start, chunk)] = dot(forward_w, jnp.concatenate([high, low, high], axis=0))
-        return 0
-
-    lax.fori_loop(0, (hi_x - lo_x) * w // chunk, first_pass, 0)
-
-    lo_u, hi_u = -10, n + 10
-    count = (hi_u - lo_u) * w
-    gathered = sum(
-        shifted_ref[8 * q : 8 * q + 8, pl.ds((lo_u - SHIFT_LOW - 2 * q - lo_x) * w, count)] for q in range(PAIRS)
-    )
-    proj = gathered[:, 2 * w :] + pltpu.roll(gathered[:, w : count - w], 4, 0)
-    ratio = first_ref[:, (lo_u + 2 + MARGIN) * w : (hi_u + MARGIN) * w]
-    ratio = ratio + (ratio + uniform - jnp.log(proj))
-    later = pltpu.roll(jnp.concatenate([ratio[:, w:], ratio[:, :w]], axis=1), 4, 0)
-    pack(jnp.where(lax.broadcasted_iota(jnp.int32, ratio.shape, 0) < 4, ratio, later))
 
     per = 16
     chunk2 = per * w
@@ -298,9 +303,16 @@
             b_even, b_odd = both[HALF:, :w], both[HALF:, w:]
             value = jnp.where(lane < n, a_even, b_odd) + swap(jnp.where(lane < n, a_odd, b_even))
             out_ref[:, pl.ds(pl.multiple_of(pair * w, w), w)] = value
+        out_copy(i).start()
         return 0
 
+    def out_copy(i):
+        at = pl.ds(pl.multiple_of(i * (x_per_step * w), x_per_step * w), x_per_step * w)
+        return pltpu.make_async_copy(out_ref.at[:, at], out_hbm.at[:, at], out_sem.at[i])
+
     lax.fori_loop(0, HALF // x_per_step, planes, 0)
+    for i in range(HALF // x_per_step):
+        out_copy(i).wait()
 
 
 def share_tables(offsets, fractions):
@@ -310,11 +322,14 @@
     lane = jnp.arange(2 * count * slab, dtype=jnp.int32) % (count * slab)
     mine = (lane // slab == lax.axis_index("depth")).astype(f32)
     table = jnp.tile(both, (1, 2 * count)) * mine
-    step = 1
-    while step < count:
+    step = count // 2
+    while step > 2:
         table = table + lax.ppermute(table, "depth", [(i, i ^ step) for i in range(count)])
-        step *= 2
-    return table
+        step //= 2
+    total = table
+    for k in (1, 2, 3):
+        total = total + lax.ppermute(table, "depth", [(i, i ^ k) for i in range(count)])
+    return total
 
 
 def windows(images, bricks_x, bricks_y):
@@ -345,7 +360,8 @@
             sent = jnp.where(depth_index // bricks_y == 0, tail, head)
             pads.append(lax.ppermute(sent, axes, edge(1, other) + edge(-1, other))[None])
         else:
-            pads.append(jnp.stack([lax.ppermute(tail, axes, edge(1, other)), lax.ppermute(head, axes, edge(-1, other))]))
+            sides = ((tail, 1), (head, -1))
+            pads.append(jnp.stack([lax.ppermute(v, axes, edge(step, other)) for v, step in sides]))
     other_strip = lax.ppermute(strip, "exp", [(i, (i + 1) % exps) for i in range(exps)])
     return strip, other_strip, pads[0], pads[1]
 
@@ -365,8 +381,8 @@
     out = pl.pallas_call(
         functools.partial(kernel, bricks_y=bricks_y),
         out_shape=jax.ShapeDtypeStruct((HALF, n * n), f32),
-        in_specs=[pl.BlockSpec(memory_space=pltpu.SMEM)] + [vmem] * 11,
-        out_specs=vmem,
+        in_specs=[pl.BlockSpec(memory_space=pltpu.HBM)] + [vmem] * 11,
+        out_specs=pl.BlockSpec(memory_space=pl.ANY),
         scratch_shapes=[
             pltpu.VMEM((8, extended), f32),
             pltpu.VMEM((8, 2 * window), f32),
@@ -383,6 +399,10 @@
             pltpu.VMEM((2 * n, 3 * n), bf16),
             pltpu.VMEM((12 * n, 4 * n), bf16),
             pltpu.VMEM((n, 6 * GROUPS), bf16),
+            pltpu.VMEM((HALF, n * n), f32),
+            pltpu.SMEM(shifts.shape, jnp.int32),
+            pltpu.SemaphoreType.DMA(()),
+            pltpu.SemaphoreType.DMA((4,)),
         ],
         compiler_params=pltpu.CompilerParams(vmem_limit_bytes=40 * 1024 * 1024),
     )(shifts, *strips, table, *(jnp.asarray(t) for t in constant_tables()))

time: 29.1 us -> 31.4 us (1.079)
  waiting for transfers between devices: 3.96 us -> 5.81 us
  starting transfers between devices: 9.43 us -> 10.4 us
  Pallas kernels: 12.9 us -> 12.4 us
    ppermute x1, waiting for transfers between devices: 0.01 us -> 3.97 us  [windows(): lax.ppermute(strip, 'exp', [(i, (i + 1) % exps) for i in range(exps)])]
    ppermute x0 -> x3, starting transfers between devices: none -> 3.49 us  [share_tables(): lax.ppermute(table, 'depth', [(i, i ^ k) for i in range(count)])]
    ppermute x3 -> x1, starting transfers between devices: 7.23 us -> 4.13 us  [share_tables(): lax.ppermute(table, 'depth', [(i, i ^ step) for i in range(count)])]
    ppermute x3 -> x1, waiting for transfers between devices: 3.95 us -> 1.24 us  [share_tables(): lax.ppermute(table, 'depth', [(i, i ^ step) for i in range(count)])]
    ppermute x0 -> x3, waiting for transfers between devices: none -> 0.59 us  [share_tables(): lax.ppermute(table, 'depth', [(i, i ^ k) for i in range(count)])]
    pallas_call x1, Pallas kernels: 12.9 us -> 12.4 us  [per_device(): pl.pallas_call(functools.partial(kernel, bricks_y=bricks_y), out_shape=ja...]
    ppermute x2, starting transfers between devices: 1.67 us -> 1.99 us  [windows(): lax.ppermute(sent, axes, edge(1, other) + edge(-1, other))[None]]
  transfers between devices with their start and end apart: 6 -> 7, of which waited for: 2 -> 4; matrix products, arithmetic and copies ran while one was open for 1% -> 1% of each run, Pallas kernels for 0% -> 0%
where the time goes in v2:
time: 31.4 us; the launch traced here: 31.2 us
  Pallas kernels  12.4 us (39%)
  starting transfers between devices  10.4 us (33%)
  waiting for transfers between devices  5.81 us (19%)
  local copies, waits for them, and re-layouts  2.43 us (8%)
    pallas_call x1, Pallas kernels, per_device(): pl.pallas_call(functools.partial(kernel, bricks_y=bricks_y), out_shape=ja...  12.4 us
    ppermute x1, starting transfers between devices, share_tables(): lax.ppermute(table, 'depth', [(i, i ^ step) for i in range(count)])  4.13 us
    ppermute x1, waiting for transfers between devices, windows(): lax.ppermute(strip, 'exp', [(i, (i + 1) % exps) for i in range(exps)])  3.97 us
    ppermute x3, starting transfers between devices, share_tables(): lax.ppermute(table, 'depth', [(i, i ^ k) for i in range(count)])  3.49 us
    unnamed x20, local copies, waits for them, and re-layouts  2.06 us
    ppermute x2, starting transfers between devices, windows(): lax.ppermute(sent, axes, edge(1, other) + edge(-1, other))[None]  1.99 us
    ppermute x1, waiting for transfers between devices, share_tables(): lax.ppermute(table, 'depth', [(i, i ^ step) for i in range(count)])  1.24 us
    ppermute x1, starting transfers between devices, windows(): lax.ppermute(strip, 'exp', [(i, (i + 1) % exps) for i in range(exps)])  0.82 us
  transfers between devices with their start and end apart: 7, of which 4 were waited for; matrix products, arithmetic and copies ran while one was open for 1% of the time, Pallas kernels for 0%

profile of v2, /device:TPU:0, one launch (start us, length us, event | category | flops | bytes accessed | tf_op | source)
XLA Modules:
  0.0 31.2 jit_solution(11982581715426341862)
XLA Ops:
  0.0 0.0 copy-start
  0.0 0.7 %copy-done.8 = s32[4,8]{1,0:T(4,128)S(1)} copy-done((s32[4,8]{1,0:T(4,128)S(1)}, s32[4,8]{1,0:T(4,128)}, u32[]{:S(2)}) %copy-start.8) | copy-done | bytes 152
  0.7 0.7 %copy-done.9 = f32[4,8]{1,0:T(4,128)S(1)} copy-done((f32[4,8]{1,0:T(4,128)S(1)}, f32[4,8]{1,0:T(4,128)}, u32[]{:S(2)}) %copy-start.9) | copy-done | bytes 152
  1.4 0.1 tile.10
  1.5 4.1 %collective-permute-start.3 = (f32[8,128]{1,0:T(8,128)S(1)}, f32[8,128]{1,0:T(8,128)S(1)}, u32[]{:S(2)}, u32[]{:S(2)}) collective-permute-start(f32[8,128]{1,0:T(8,128)S(1)} %broadcast_multiply_fusion), channel_id=1, source_target_pairs={{0,4},{1,5},{2,6},{3,7},{4,0},{5,1},{6,2},{7,3},{8,12},{9,13},{10,... | collective-permute-start | bytes 12296 | tf_op jit(solution)/shard_map/ppermute | solution.py:327
  5.7 0.0 copy-done
  5.7 0.0 copy-start.6
  5.7 0.1 constant_dynamic-slice_fusion
  5.8 0.0 copy-start.1
  5.9 0.1 reshape.38.own_ref
  6.0 0.0 copy-start.3
  6.0 1.2 %collective-permute-done.3 = f32[8,128]{1,0:T(8,128)S(1)} collective-permute-done((f32[8,128]{1,0:T(8,128)S(1)}, f32[8,128]{1,0:T(8,128)S(1)}, u32[]{:S(2)}, u32[]{:S(2)}) %collective-permute-start.3) | collective-permute-done | bytes 4128 | tf_op jit(solution)/shard_map/ppermute | solution.py:327
  7.3 2.9 %collective-permute-start.6 = (f32[8,128]{1,0:T(8,128)S(1)}, f32[8,128]{1,0:T(8,128)S(1)}, u32[]{:S(2)}, u32[]{:S(2)}) collective-permute-start(f32[8,128]{1,0:T(8,128)S(1)} %fusion), channel_id=1, source_target_pairs={{0,3},{1,2},{2,1},{3,0},{4,7},{5,6},{6,5},{7,4},{8,11},{9,10},{10,... | collective-permute-start | bytes 12296 | tf_op jit(solution)/shard_map/ppermute | solution.py:331
  10.1 0.4 %collective-permute-start.5 = (f32[8,128]{1,0:T(8,128)S(1)}, f32[8,128]{1,0:T(8,128)S(1)}, u32[]{:S(2)}, u32[]{:S(2)}) collective-permute-start(f32[8,128]{1,0:T(8,128)S(1)} %fusion), channel_id=1, source_target_pairs={{0,2},{1,3},{2,0},{3,1},{4,6},{5,7},{6,4},{7,5},{8,10},{9,11},{10,... | collective-permute-start | bytes 12296 | tf_op jit(solution)/shard_map/ppermute | solution.py:331
  10.6 0.2 collective-permute-start.4
  10.8 0.1 collective-permute-start.2
  10.9 1.9 %collective-permute-start.1 = (f32[4,2048]{1,0:T(4,128)S(1)}, f32[4,2048]{1,0:T(4,128)S(1)}, u32[]{:S(2)}, u32[]{:S(2)}) collective-permute-start(f32[4,2048]{1,0:T(4,128)S(1)} %slice_select_fusion), channel_id=1, source_target_pairs={{0,8},{1,9},{2,10},{3,11},{8,0},{9,1},{10,2},{11,3},{16,24},{17,25... | collective-permute-start | bytes 98312 | tf_op jit(solution)/shard_map/ppermute | solution.py:361
  12.8 0.0 collective-permute-done.6
  12.8 0.8 %collective-permute-start = (f32[4,8192]{1,0:T(4,128)S(1)}, f32[4,8192]{1,0:T(4,128)S(1)}, u32[]{:S(2)}, u32[]{:S(2)}) collective-permute-start(f32[4,8192]{1,0:T(4,128)S(1)} %reshape.38.own_ref), channel_id=1, source_target_pairs={{0,16},{16,0},{1,17},{17,1},{2,18},{18,2},{3,19},{19,3},{4,20},{20... | collective-permute-start | bytes 393224 | tf_op jit(solution)/shard_map/ppermute | solution.py:365
  13.6 0.1 collective-permute-done.5
  13.7 0.4 %collective-permute-done.4 = f32[8,128]{1,0:T(8,128)S(1)} collective-permute-done((f32[8,128]{1,0:T(8,128)S(1)}, f32[8,128]{1,0:T(8,128)S(1)}, u32[]{:S(2)}, u32[]{:S(2)}) %collective-permute-start.4) | collective-permute-done | bytes 4128 | tf_op jit(solution)/shard_map/ppermute | solution.py:331
  14.2 0.0 collective-permute-done.2
  14.2 0.0 collective-permute-done.1
  14.2 4.0 %collective-permute-done.other_ref = f32[4,8192]{1,0:T(4,128)S(1)} collective-permute-done((f32[4,8192]{1,0:T(4,128)S(1)}, f32[4,8192]{1,0:T(4,128)S(1)}, u32[]{:S(2)}, u32[]{:S(2)}) %collective-permute-start) | collective-permute-done | bytes 131104 | tf_op jit(solution)/shard_map/ppermute | solution.py:365
  18.2 0.0 copy-done.2
  18.2 0.0 copy-done.4
  18.2 0.0 copy-done.5
  18.2 0.0 copy-done.6
  18.2 0.0 copy-done.1
  18.2 0.0 copy-done.3
  18.2 0.6 %copy-done.7 = s32[1,3]{1,0:T(1,128)S(1)} copy-done((s32[1,3]{1,0:T(1,128)S(1)}, s32[1,3]{1,0:T(1,128)}, u32[]{:S(2)}) %copy-start.7) | copy-done | bytes 36
  18.8 12.4 %shard_map.100 = f32[32,4096]{1,0:T(8,128)} custom-call(s32[1,3]{1,0:T(1,128)S(1)} %copy-done.7, f32[4,8192]{1,0:T(4,128)S(1)} %reshape.38.own_ref, f32[4,8192]{1,0:T(4,128)S(1)} %collective-permute-done.other_ref, f32[1,4,2048]{2,1,0:T(4,128)S(1)} %bitcast.6, f32[1,4,2048]{2,1,0:T(4,128)S(1)} %bitcast.5, f32[8,128]{1,0:T(8,128)S(1)} %add_add_fusion.tab_ref, ...), custom_call_target="tpu_custom_call" | custom-call | tf_op jit(solution)/shard_map/pallas_call | solution.py:381
  (14 shorter events, 0.1 us)
Async XLA Ops:
  0.0 5.7 %copy-start = (f32[1,4,128,256]{3,2,1,0:T(8,128)S(1)}, f32[1,4,128,256]{3,2,1,0:T(8,128)}, u32[]{:S(2)}) copy-start(f32[1,4,128,256]{3,2,1,0:T(8,128)} %param.10) | copy-start | bytes 1572868
  0.0 0.7 %copy-start.8 = (s32[4,8]{1,0:T(4,128)S(1)}, s32[4,8]{1,0:T(4,128)}, u32[]{:S(2)}) copy-start(s32[4,8]{1,0:T(4,128)} %param.11) | copy-start | bytes 388
  0.7 0.7 %copy-start.9 = (f32[4,8]{1,0:T(4,128)S(1)}, f32[4,8]{1,0:T(4,128)}, u32[]{:S(2)}) copy-start(f32[4,8]{1,0:T(4,128)} %param.12) | copy-start | bytes 388
  1.5 5.7 %collective-permute-start.3 = (f32[8,128]{1,0:T(8,128)S(1)}, f32[8,128]{1,0:T(8,128)S(1)}, u32[]{:S(2)}, u32[]{:S(2)}) collective-permute-start(f32[8,128]{1,0:T(8,128)S(1)} %broadcast_multiply_fusion), channel_id=1, source_target_pairs={{0,4},{1,5},{2,6},{3,7},{4,0},{5,1},{6,2},{7,3},{8,12},{9,13},{10,... | collective-permute-start | bytes 12296 | tf_op jit(solution)/shard_map/ppermute | solution.py:327
  5.7 12.5 %copy-start.2 = (f32[2,2,128,128]{3,2,1,0:T(8,128)S(1)}, f32[2,2,128,128]{3,2,1,0:T(8,128)}, u32[]{:S(2)}) copy-start(f32[2,2,128,128]{3,2,1,0:T(8,128)} %constant.80.clone.z_inv_ref) | copy-start | bytes 786436
  5.7 12.5 %copy-start.4 = (f32[2,128,128]{2,1,0:T(8,128)S(1)}, f32[2,128,128]{2,1,0:T(8,128)}, u32[]{:S(2)}) copy-start(f32[2,128,128]{2,1,0:T(8,128)} %constant.78.clone.x_inv_ref) | copy-start | bytes 393220
  5.7 12.5 %copy-start.5 = (bf16[128,192]{1,0:T(8,128)(2,1)S(1)}, bf16[128,192]{1,0:T(8,128)(2,1)}, u32[]{:S(2)}) copy-start(bf16[128,192]{1,0:T(8,128)(2,1)} %constant.77.clone.x_fwd_ref) | copy-start | bytes 147460
  5.7 12.5 %copy-start.6 = (bf16[80,192]{1,0:T(8,128)(2,1)S(1)}, bf16[80,192]{1,0:T(8,128)(2,1)}, u32[]{:S(2)}) copy-start(bf16[80,192]{1,0:T(8,128)(2,1)} %constant.75.clone.z_fwd_ref) | copy-start | bytes 92164
  5.8 12.4 %copy-start.1 = (bf16[768,256]{1,0:T(8,128)(2,1)S(1)}, bf16[768,256]{1,0:T(8,128)(2,1)}, u32[]{:S(2)}) copy-start(bf16[768,256]{1,0:T(8,128)(2,1)} %constant.76.clone.y_fwd_ref) | copy-start | bytes 1179652
  6.0 12.2 %copy-start.3 = (f32[2,128,128]{2,1,0:T(8,128)S(1)}, f32[2,128,128]{2,1,0:T(8,128)}, u32[]{:S(2)}) copy-start(f32[2,128,128]{2,1,0:T(8,128)} %constant.79.clone.y_inv_ref) | copy-start | bytes 393220
  7.3 5.5 %collective-permute-start.6 = (f32[8,128]{1,0:T(8,128)S(1)}, f32[8,128]{1,0:T(8,128)S(1)}, u32[]{:S(2)}, u32[]{:S(2)}) collective-permute-start(f32[8,128]{1,0:T(8,128)S(1)} %fusion), channel_id=1, source_target_pairs={{0,3},{1,2},{2,1},{3,0},{4,7},{5,6},{6,5},{7,4},{8,11},{9,10},{10,... | collective-permute-start | bytes 12296 | tf_op jit(solution)/shard_map/ppermute | solution.py:331
  10.1 3.6 %collective-permute-start.5 = (f32[8,128]{1,0:T(8,128)S(1)}, f32[8,128]{1,0:T(8,128)S(1)}, u32[]{:S(2)}, u32[]{:S(2)}) collective-permute-start(f32[8,128]{1,0:T(8,128)S(1)} %fusion), channel_id=1, source_target_pairs={{0,2},{1,3},{2,0},{3,1},{4,6},{5,7},{6,4},{7,5},{8,10},{9,11},{10,... | collective-permute-start | bytes 12296 | tf_op jit(solution)/shard_map/ppermute | solution.py:331
  10.6 3.6 %collective-permute-start.4 = (f32[8,128]{1,0:T(8,128)S(1)}, f32[8,128]{1,0:T(8,128)S(1)}, u32[]{:S(2)}, u32[]{:S(2)}) collective-permute-start(f32[8,128]{1,0:T(8,128)S(1)} %fusion), channel_id=1, source_target_pairs={{0,1},{1,0},{2,3},{3,2},{4,5},{5,4},{6,7},{7,6},{8,9},{9,8},{10,11... | collective-permute-start | bytes 12296 | tf_op jit(solution)/shard_map/ppermute | solution.py:331
  10.8 3.4 %collective-permute-start.2 = (f32[4,2048]{1,0:T(4,128)S(1)}, f32[4,2048]{1,0:T(4,128)S(1)}, u32[]{:S(2)}, u32[]{:S(2)}) collective-permute-start(f32[4,2048]{1,0:T(4,128)S(1)} %slice_select_fusion), channel_id=1, source_target_pairs={{0,24},{1,25},{2,26},{3,27},{8,16},{9,17},{10,18},{11,19},{16,8},{... | collective-permute-start | bytes 98312 | tf_op jit(solution)/shard_map/ppermute | solution.py:361
  10.9 3.4 %collective-permute-start.1 = (f32[4,2048]{1,0:T(4,128)S(1)}, f32[4,2048]{1,0:T(4,128)S(1)}, u32[]{:S(2)}, u32[]{:S(2)}) collective-permute-start(f32[4,2048]{1,0:T(4,128)S(1)} %slice_select_fusion), channel_id=1, source_target_pairs={{0,8},{1,9},{2,10},{3,11},{8,0},{9,1},{10,2},{11,3},{16,24},{17,25... | collective-permute-start | bytes 98312 | tf_op jit(solution)/shard_map/ppermute | solution.py:361
  12.8 5.4 %collective-permute-start = (f32[4,8192]{1,0:T(4,128)S(1)}, f32[4,8192]{1,0:T(4,128)S(1)}, u32[]{:S(2)}, u32[]{:S(2)}) collective-permute-start(f32[4,8192]{1,0:T(4,128)S(1)} %reshape.38.own_ref), channel_id=1, source_target_pairs={{0,16},{16,0},{1,17},{17,1},{2,18},{18,2},{3,19},{19,3},{4,20},{20... | collective-permute-start | bytes 393224 | tf_op jit(solution)/shard_map/ppermute | solution.py:365
  18.2 0.7 %copy-start.7 = (s32[1,3]{1,0:T(1,128)S(1)}, s32[1,3]{1,0:T(1,128)}, u32[]{:S(2)}) copy-start(s32[1,3]{1,0:T(1,128)} %shift_hbm.1) | copy-start | bytes 40

commit v3 on v1

--- a/solution.py
+++ b/solution.py
@@ -8,6 +8,7 @@
 from jax.experimental import pallas as pl
 from jax.experimental.pallas import tpu as pltpu
 from jax.sharding import PartitionSpec as P
+
 
 BRICK = 64
 HALF = BRICK // 2
@@ -78,40 +79,18 @@
     return z_fwd, y_fwd, x_fwd, x_inv, y_inv, np.stack(z_inv).astype(np.float32)
 
 
-def kernel(
-    shift_ref, own_ref, other_ref, pad_own_ref, pad_other_ref, tab_ref,
-    z_fwd_ref, y_fwd_ref, x_fwd_ref, x_inv_ref, y_inv_ref, z_inv_ref,
-    out_ref,
-    raw_ref, first_ref, pack_ref, high_ref, shifted_ref, spec_ref, freq_ref, cross_ref,
-    wave_ref, line_ref, back_ref, forward_ref, xi_ref, yi_ref, zi_ref,
-    *, bricks_y,
-):
+def pack(both, pack_ref, high_ref):
+    w = 2 * BRICK
+    high = both.astype(bf16).astype(f32)
+    pack_ref[...] = jnp.concatenate([high, both - high], axis=0).astype(bf16)
+    later = jnp.concatenate([high[:, 2 * w :], high[:, : 2 * w]], axis=1)
+    high_ref[...] = jnp.concatenate([high, later], axis=0).astype(bf16)
+
+
+def turn(shift_ref, x_inv_ref, y_inv_ref, z_inv_ref, xi_ref, yi_ref, zi_ref):
     n = BRICK
     w = 2 * n
     exp_index = lax.axis_index("exp")
-    part = lax.axis_index("depth") // bricks_y
-    columns = n + 2 * MARGIN
-    pad = MARGIN * n
-    strip = own_ref.shape[1]
-
-    tab = tab_ref[...]
-    rows = lax.broadcasted_iota(jnp.int32, (8, w), 0)
-    offs = jnp.where(rows < 4, tab, pltpu.roll(tab, 4, 0))
-    frac = jnp.where(rows < 4, pltpu.roll(tab, 4, 0), tab)
-    total = sum(tent_value(float(d), frac) for d in range(-2, 4))
-    parity = (rows >= 4).astype(f32)
-    blocks = [tent_value(SHIFT_LOW + 2 * q + parity - offs, frac) / total for q in range(PAIRS)]
-    sums = jnp.sum(sum(blocks)[:, :n], axis=1, keepdims=True) / n
-    uniform = jnp.log(sums + pltpu.roll(jnp.broadcast_to(sums, (8, w)), 4, 0)[:, :1])
-    both_high, back_low = [], []
-    for block in blocks:
-        high, low = split(block / 4.0)
-        both_high += [high.astype(f32)] * 2
-        back_low.append(low.astype(f32))
-    stacked = jnp.concatenate(both_high + back_low + [jnp.zeros((40, w), f32)], axis=0)
-    back_ref[...] = jnp.transpose(stacked)[:n, :224].astype(bf16)
-    high, low = split(jnp.concatenate(blocks, axis=0) / n)
-    forward_ref[...] = jnp.concatenate([high, low], axis=1)[:, : 3 * n]
 
     sz, sx, sy = (shift_ref[0, i] + n for i in range(3))
     moved = lax.rem(sx, n)
@@ -138,29 +117,31 @@
     col = lax.broadcasted_iota(jnp.int32, turned.shape, 1)
     zi_ref[...] = jnp.where(col < 4 * GROUPS, high.astype(f32), low.astype(f32)).astype(bf16)[:, : 6 * GROUPS]
 
-    def spread(first_lane, count):
-        pieces = [pack_ref[:, pl.ds(first_lane + 2 * w * q, count)] for q in range(PAIRS)]
-        pieces += [high_ref[:, pl.ds(first_lane + 2 * w * q, count)] for q in range(0, PAIRS, 2)]
-        return jnp.concatenate(pieces, axis=0)
-
-    def pack(both):
-        lanes = both.shape[1]
-        high = both.astype(bf16).astype(f32)
-        pack_ref[:, 0:lanes] = jnp.concatenate([high, both - high], axis=0).astype(bf16)
-        later = jnp.concatenate([high[:, 2 * w :], high[:, : 2 * w]], axis=1)
-        high_ref[:, 0:lanes] = jnp.concatenate([high, later], axis=0).astype(bf16)
+
+def prepare(
+    own_ref, other_ref, pad_own_ref, pad_other_ref, first_ref, pack_ref, high_ref, raw_ref,
+    *, bricks_y,
+):
+    n = BRICK
+    w = 2 * n
+    part = lax.axis_index("depth") // bricks_y
+    columns = n + 2 * MARGIN
+    pad = MARGIN * n
+    strip = own_ref.shape[1]
 
     raw_ref[0:4, 0:pad] = pad_own_ref[0]
     raw_ref[4:8, 0:pad] = pad_other_ref[0]
     raw_ref[0:4, pad : pad + strip] = own_ref[...]
-    raw_ref[4:8, pad : pad + strip] = other_ref[...]
+    reach = other_ref.shape[1]
+    at = pad + part * (strip - reach) if reach < strip else pad
+    raw_ref[4:8, pl.ds(pl.multiple_of(at, pad), reach)] = other_ref[...]
     raw_ref[0:4, pad + strip :] = pad_own_ref[pad_own_ref.shape[0] - 1]
     raw_ref[4:8, pad + strip :] = pad_other_ref[pad_other_ref.shape[0] - 1]
     row = lax.broadcasted_iota(jnp.int32, (8, w), 0)
     lane = lax.broadcasted_iota(jnp.int32, (8, w), 1)
     same = (row < 4) == (lane < n)
     swap = lambda v: pltpu.roll(v, n, 1)
-    ratio = jnp.log(raw_ref[:, pl.ds(pl.multiple_of(part * (n * n), n * n), columns * n)]) - uniform
+    ratio = jnp.log(raw_ref[:, pl.ds(pl.multiple_of(part * (n * n), n * n), columns * n)])
     even, odd = [], []
     for k in range(columns // 2):
         here = ratio[:, k * w : (k + 1) * w]
@@ -172,7 +153,46 @@
         cols += [even[k], jnp.where(row < 4, odd[k], odd[(k + 1) % (columns // 2)])]
     cols = jnp.concatenate(cols, axis=1)
     first_ref[...] = cols
-    pack(cols)
+    pack(cols, pack_ref, high_ref)
+
+
+def kernel(
+    tab_ref, first_ref, pack_in_ref, high_in_ref, xi_ref, yi_ref, zi_ref, z_fwd_ref, y_fwd_ref, x_fwd_ref,
+    out_hbm,
+    pack_ref, high_ref, shifted_ref, spec_ref, freq_ref, cross_ref,
+    wave_ref, line_ref, back_ref, forward_ref,
+    out_ref, out_sem,
+):
+    n = BRICK
+    w = 2 * n
+    exp_index = lax.axis_index("exp")
+
+    tab = tab_ref[...]
+    rows = lax.broadcasted_iota(jnp.int32, (8, w), 0)
+    offs = jnp.where(rows < 4, tab, pltpu.roll(tab, 4, 0))
+    frac = jnp.where(rows < 4, pltpu.roll(tab, 4, 0), tab)
+    total = sum(tent_value(float(d), frac) for d in range(-2, 4))
+    parity = (rows >= 4).astype(f32)
+    blocks = [tent_value(SHIFT_LOW + 2 * q + parity - offs, frac) / total for q in range(PAIRS)]
+    sums = jnp.sum(sum(blocks)[:, :n], axis=1, keepdims=True) / n
+    uniform = jnp.log(sums + pltpu.roll(jnp.broadcast_to(sums, (8, w)), 4, 0)[:, :1])
+    faint = jnp.exp(-jnp.sum(sum(blocks) * uniform, axis=0, keepdims=True) / 4.0)
+    both_high, back_low = [], []
+    for block in blocks:
+        high, low = split(block / 4.0)
+        both_high += [high.astype(f32)] * 2
+        back_low.append(low.astype(f32))
+    stacked = jnp.concatenate(both_high + back_low + [jnp.zeros((40, w), f32)], axis=0)
+    back_ref[...] = jnp.transpose(stacked)[:n, :224].astype(bf16)
+    high, low = split(jnp.concatenate(blocks, axis=0) * (faint / n))
+    forward_ref[...] = jnp.concatenate([high, low], axis=1)[:, : 3 * n]
+
+    swap = lambda v: pltpu.roll(v, n, 1)
+
+    def spread(pack_from, high_from, first_lane, count):
+        pieces = [pack_from[:, pl.ds(first_lane + 2 * w * q, count)] for q in range(PAIRS)]
+        pieces += [high_from[:, pl.ds(first_lane + 2 * w * q, count)] for q in range(0, PAIRS, 2)]
+        return jnp.concatenate(pieces, axis=0)
 
     lo_x, hi_x = -REACH, n + REACH
     chunk = 20 * w
@@ -181,7 +201,7 @@
 
     def first_pass(i, _):
         start = pl.multiple_of(i * chunk, 2 * w)
-        logv = dot(back_w, spread(start + (lo_x + SHIFT_LOW + MARGIN) * w, chunk))
+        logv = dot(back_w, spread(pack_in_ref, high_in_ref, start + (lo_x + SHIFT_LOW + MARGIN) * w, chunk))
         high, low = split(jnp.exp(logv))
         shifted_ref[:, pl.ds(start, chunk)] = dot(forward_w, jnp.concatenate([high, low, high], axis=0))
         return 0
@@ -195,16 +215,16 @@
     )
     proj = gathered[:, 2 * w :] + pltpu.roll(gathered[:, w : count - w], 4, 0)
     ratio = first_ref[:, (lo_u + 2 + MARGIN) * w : (hi_u + MARGIN) * w]
-    ratio = ratio + (ratio + uniform - jnp.log(proj))
+    ratio = (ratio - uniform) + (ratio - jnp.log(proj))
     later = pltpu.roll(jnp.concatenate([ratio[:, w:], ratio[:, :w]], axis=1), 4, 0)
-    pack(jnp.where(lax.broadcasted_iota(jnp.int32, ratio.shape, 0) < 4, ratio, later))
+    pack(jnp.where(lax.broadcasted_iota(jnp.int32, ratio.shape, 0) < 4, ratio, later), pack_ref, high_ref)
 
     per = 16
     chunk2 = per * w
 
     def second_pass(i, _):
         start = pl.multiple_of(i * chunk2, chunk2)
-        logv = dot(back_w, spread(start, chunk2))
+        logv = dot(back_w, spread(pack_ref, high_ref, start, chunk2))
         high, low = split(jnp.exp(logv))
         spec = dot(z_fwd_ref[...], jnp.concatenate([high, low, high], axis=0))
         groups = []
@@ -298,9 +318,16 @@
             b_even, b_odd = both[HALF:, :w], both[HALF:, w:]
             value = jnp.where(lane < n, a_even, b_odd) + swap(jnp.where(lane < n, a_odd, b_even))
             out_ref[:, pl.ds(pl.multiple_of(pair * w, w), w)] = value
+        out_copy(i).start()
         return 0
 
+    def out_copy(i):
+        at = pl.ds(pl.multiple_of(i * (x_per_step * w), x_per_step * w), x_per_step * w)
+        return pltpu.make_async_copy(out_ref.at[:, at], out_hbm.at[:, at], out_sem.at[i])
+
     lax.fori_loop(0, HALF // x_per_step, planes, 0)
+    for i in range(HALF // x_per_step):
+        out_copy(i).wait()
 
 
 def share_tables(offsets, fractions):
@@ -310,11 +337,14 @@
     lane = jnp.arange(2 * count * slab, dtype=jnp.int32) % (count * slab)
     mine = (lane // slab == lax.axis_index("depth")).astype(f32)
     table = jnp.tile(both, (1, 2 * count)) * mine
-    step = 1
-    while step < count:
+    step = count // 2
+    while step > 2:
         table = table + lax.ppermute(table, "depth", [(i, i ^ step) for i in range(count)])
-        step *= 2
-    return table
+        step //= 2
+    total = table
+    for k in (1, 2, 3):
+        total = total + lax.ppermute(table, "depth", [(i, i ^ k) for i in range(count)])
+    return total
 
 
 def windows(images, bricks_x, bricks_y):
@@ -345,8 +375,13 @@
             sent = jnp.where(depth_index // bricks_y == 0, tail, head)
             pads.append(lax.ppermute(sent, axes, edge(1, other) + edge(-1, other))[None])
         else:
-            pads.append(jnp.stack([lax.ppermute(tail, axes, edge(1, other)), lax.ppermute(head, axes, edge(-1, other))]))
-    other_strip = lax.ppermute(strip, "exp", [(i, (i + 1) % exps) for i in range(exps)])
+            sides = ((tail, 1), (head, -1))
+            pads.append(jnp.stack([lax.ppermute(v, axes, edge(step, other)) for v, step in sides]))
+    piece = strip
+    if bricks_x == 2:
+        near = strip.shape[1] - MARGIN * BRICK
+        piece = jnp.where(depth_index // bricks_y == 0, strip[:, :near], strip[:, -near:])
+    other_strip = lax.ppermute(piece, "exp", [(i, (i + 1) % exps) for i in range(exps)])
     return strip, other_strip, pads[0], pads[1]
 
 
@@ -362,16 +397,39 @@
     window = (n + 2 * MARGIN) * n
     extended = (width + 2 * MARGIN) * n
     vmem = pl.BlockSpec(memory_space=pltpu.VMEM)
+    z_fwd, y_fwd, x_fwd, *inverses = (jnp.asarray(v) for v in constant_tables())
+    turned = pl.pallas_call(
+        turn,
+        out_shape=[
+            jax.ShapeDtypeStruct((2 * n, 3 * n), bf16),
+            jax.ShapeDtypeStruct((12 * n, 4 * n), bf16),
+            jax.ShapeDtypeStruct((n, 6 * GROUPS), bf16),
+        ],
+        in_specs=[pl.BlockSpec(memory_space=pltpu.SMEM)] + [vmem] * 3,
+        out_specs=[vmem] * 3,
+        compiler_params=pltpu.CompilerParams(vmem_limit_bytes=8 * 1024 * 1024),
+    )(shifts, *inverses)
+    ready = pl.pallas_call(
+        functools.partial(prepare, bricks_y=bricks_y),
+        out_shape=[
+            jax.ShapeDtypeStruct((8, 2 * window), f32),
+            jax.ShapeDtypeStruct((16, 2 * window), bf16),
+            jax.ShapeDtypeStruct((16, 2 * window), bf16),
+        ],
+        in_specs=[vmem] * 4,
+        out_specs=[vmem] * 3,
+        scratch_shapes=[pltpu.VMEM((8, extended), f32)],
+        compiler_params=pltpu.CompilerParams(vmem_limit_bytes=16 * 1024 * 1024),
+    )(*strips)
+    second = (n + 18) * 2 * n
     out = pl.pallas_call(
-        functools.partial(kernel, bricks_y=bricks_y),
+        kernel,
         out_shape=jax.ShapeDtypeStruct((HALF, n * n), f32),
-        in_specs=[pl.BlockSpec(memory_space=pltpu.SMEM)] + [vmem] * 11,
-        out_specs=vmem,
+        in_specs=[vmem] * 10,
+        out_specs=pl.BlockSpec(memory_space=pl.ANY),
         scratch_shapes=[
-            pltpu.VMEM((8, extended), f32),
-            pltpu.VMEM((8, 2 * window), f32),
-            pltpu.VMEM((16, 2 * window), bf16),
-            pltpu.VMEM((16, 2 * window), bf16),
+            pltpu.VMEM((16, second), bf16),
+            pltpu.VMEM((16, second), bf16),
             pltpu.VMEM((8 * PAIRS, (n + 2 * REACH) * 2 * n), f32),
             pltpu.VMEM((2, n * ROWS, 2 * n), f32),
             pltpu.VMEM((UNROLL, 2, 2, n, 2 * n), f32),
@@ -380,12 +438,11 @@
             pltpu.VMEM((2, GROUPS * GAP, 2 * n), f32),
             pltpu.VMEM((n, 224), bf16),
             pltpu.VMEM((8 * PAIRS, 3 * n), bf16),
-            pltpu.VMEM((2 * n, 3 * n), bf16),
-            pltpu.VMEM((12 * n, 4 * n), bf16),
-            pltpu.VMEM((n, 6 * GROUPS), bf16),
+            pltpu.VMEM((HALF, n * n), f32),
+            pltpu.SemaphoreType.DMA((4,)),
         ],
         compiler_params=pltpu.CompilerParams(vmem_limit_bytes=40 * 1024 * 1024),
-    )(shifts, *strips, table, *(jnp.asarray(t) for t in constant_tables()))
+    )(table, *ready, *turned, z_fwd, y_fwd, x_fwd)
     return out.reshape(1, HALF, n * n)
 
 

time: 29.1 us -> 29.9 us (1.027)
  starting transfers between devices: 9.43 us -> 10.8 us
  waiting for transfers between devices: 3.96 us -> 3.47 us
    ppermute x1 -> x4, starting transfers between devices: 0.53 us -> 4.95 us  [the longest x3 3.55 us: share_tables(): lax.ppermute(table, 'depth', [(i, i ^ k) for i in range(count)])]
    ppermute x3 -> x1, waiting for transfers between devices: 3.95 us -> 0.01 us  [share_tables(): lax.ppermute(table, 'depth', [(i, i ^ step) for i in range(count)])]
    ppermute x1 -> x4, waiting for transfers between devices: 0.01 us -> 3.46 us  [the longest x1 2.51 us: windows(): lax.ppermute(piece, 'exp', [(i, (i + 1) % exps) for i in range(exps)])]
    ppermute x3 -> x1, starting transfers between devices: 7.23 us -> 4.13 us  [share_tables(): lax.ppermute(table, 'depth', [(i, i ^ step) for i in range(count)])]
    pallas_call x1 -> x3, Pallas kernels: 12.9 us -> 12.9 us  [the longest x1 12 us: per_device(): pl.pallas_call(kernel, out_shape=jax.ShapeDtypeStruct((HALF, n * n), f32)...]
  transfers between devices with their start and end apart: 6 -> 7, of which waited for: 2 -> 4; matrix products, arithmetic and copies ran while one was open for 1% -> 1% of each run, Pallas kernels for 0% -> 2%
where the time goes in v3:
time: 29.9 us; the launch traced here: 29.7 us
  Pallas kernels  12.9 us (43%)
  starting transfers between devices  10.8 us (36%)
  waiting for transfers between devices  3.47 us (12%)
  local copies, waits for them, and re-layouts  2.36 us (8%)
    pallas_call x1, Pallas kernels, per_device(): pl.pallas_call(kernel, out_shape=jax.ShapeDtypeStruct((HALF, n * n), f32)...  12 us
    ppermute x1, starting transfers between devices, share_tables(): lax.ppermute(table, 'depth', [(i, i ^ step) for i in range(count)])  4.13 us
    ppermute x3, starting transfers between devices, share_tables(): lax.ppermute(table, 'depth', [(i, i ^ k) for i in range(count)])  3.55 us
    ppermute x1, waiting for transfers between devices, windows(): lax.ppermute(piece, 'exp', [(i, (i + 1) % exps) for i in range(exps)])  2.51 us
    unnamed x20, local copies, waits for them, and re-layouts  2 us
    ppermute x2, starting transfers between devices, windows(): lax.ppermute(sent, axes, edge(1, other) + edge(-1, other))[None]  1.67 us
    ppermute x1, starting transfers between devices, windows(): lax.ppermute(piece, 'exp', [(i, (i + 1) % exps) for i in range(exps)])  1.4 us
    ppermute x3, waiting for transfers between devices, share_tables(): lax.ppermute(table, 'depth', [(i, i ^ k) for i in range(count)])  0.95 us
  transfers between devices with their start and end apart: 7, of which 4 were waited for; matrix products, arithmetic and copies ran while one was open for 1% of the time, Pallas kernels for 2%

profile of v3, /device:TPU:0, one launch (start us, length us, event | category | flops | bytes accessed | tf_op | source)
XLA Modules:
  0.0 29.7 jit_solution(8928316569533884677)
XLA Ops:
  0.0 0.0 copy-start
  0.0 0.7 %copy-done.8 = s32[4,8]{1,0:T(4,128)S(1)} copy-done((s32[4,8]{1,0:T(4,128)S(1)}, s32[4,8]{1,0:T(4,128)}, u32[]{:S(2)}) %copy-start.8) | copy-done | bytes 152
  0.7 0.7 %copy-done.9 = f32[4,8]{1,0:T(4,128)S(1)} copy-done((f32[4,8]{1,0:T(4,128)S(1)}, f32[4,8]{1,0:T(4,128)}, u32[]{:S(2)}) %copy-start.9) | copy-done | bytes 152
  1.4 0.1 tile.10
  1.5 4.1 %collective-permute-start = (f32[8,128]{1,0:T(8,128)S(1)}, f32[8,128]{1,0:T(8,128)S(1)}, u32[]{:S(2)}, u32[]{:S(2)}) collective-permute-start(f32[8,128]{1,0:T(8,128)S(1)} %broadcast_multiply_fusion), channel_id=1, source_target_pairs={{0,4},{1,5},{2,6},{3,7},{4,0},{5,1},{6,2},{7,3},{8,12},{9,13},{10,... | collective-permute-start | bytes 12296 | tf_op jit(solution)/shard_map/ppermute | solution.py:342
  5.7 0.0 copy-done
  5.7 0.1 constant_dynamic-slice_fusion
  5.8 0.0 copy-start.4
  5.8 0.1 reshape.38.own_ref
  6.0 0.0 copy-start.2
  6.0 0.7 %collective-permute-start.6 = (f32[4,2048]{1,0:T(4,128)S(1)}, f32[4,2048]{1,0:T(4,128)S(1)}, u32[]{:S(2)}, u32[]{:S(2)}) collective-permute-start(f32[4,2048]{1,0:T(4,128)S(1)} %slice_select_fusion.1), channel_id=1, source_target_pairs={{0,24},{1,25},{2,26},{3,27},{8,16},{9,17},{10,18},{11,19},{16,8},{... | collective-permute-start | bytes 98312 | tf_op jit(solution)/shard_map/ppermute | solution.py:376
  6.7 1.0 %collective-permute-start.5 = (f32[4,2048]{1,0:T(4,128)S(1)}, f32[4,2048]{1,0:T(4,128)S(1)}, u32[]{:S(2)}, u32[]{:S(2)}) collective-permute-start(f32[4,2048]{1,0:T(4,128)S(1)} %slice_select_fusion.1), channel_id=1, source_target_pairs={{0,8},{1,9},{2,10},{3,11},{8,0},{9,1},{10,2},{11,3},{16,24},{17,25... | collective-permute-start | bytes 98312 | tf_op jit(solution)/shard_map/ppermute | solution.py:376
  7.7 0.0 collective-permute-done
  7.7 0.0 copy-start.7
  7.7 2.6 %collective-permute-start.3 = (f32[8,128]{1,0:T(8,128)S(1)}, f32[8,128]{1,0:T(8,128)S(1)}, u32[]{:S(2)}, u32[]{:S(2)}) collective-permute-start(f32[8,128]{1,0:T(8,128)S(1)} %fusion), channel_id=1, source_target_pairs={{0,3},{1,2},{2,1},{3,0},{4,7},{5,6},{6,5},{7,4},{8,11},{9,10},{10,... | collective-permute-start | bytes 12296 | tf_op jit(solution)/shard_map/ppermute | solution.py:346
  10.3 0.4 %collective-permute-start.2 = (f32[8,128]{1,0:T(8,128)S(1)}, f32[8,128]{1,0:T(8,128)S(1)}, u32[]{:S(2)}, u32[]{:S(2)}) collective-permute-start(f32[8,128]{1,0:T(8,128)S(1)} %fusion), channel_id=1, source_target_pairs={{0,2},{1,3},{2,0},{3,1},{4,6},{5,7},{6,4},{7,5},{8,10},{9,11},{10,... | collective-permute-start | bytes 12296 | tf_op jit(solution)/shard_map/ppermute | solution.py:346
  10.7 0.5 %collective-permute-start.1 = (f32[8,128]{1,0:T(8,128)S(1)}, f32[8,128]{1,0:T(8,128)S(1)}, u32[]{:S(2)}, u32[]{:S(2)}) collective-permute-start(f32[8,128]{1,0:T(8,128)S(1)} %fusion), channel_id=1, source_target_pairs={{0,1},{1,0},{2,3},{3,2},{4,5},{5,4},{6,7},{7,6},{8,9},{9,8},{10,11... | collective-permute-start | bytes 12296 | tf_op jit(solution)/shard_map/ppermute | solution.py:346
  11.3 0.0 copy-done.4
  11.3 0.0 copy-done.2
  11.3 0.0 copy-done.3
  11.3 0.0 copy-start.1
  11.3 0.7 %shard_map.101 = (bf16[128,192]{1,0:T(8,128)(2,1)S(1)}, bf16[768,256]{1,0:T(8,128)(2,1)S(1)}, bf16[64,144]{1,0:T(8,128)(2,1)S(1)}) custom-call(s32[1,3]{1,0:T(1,128)S(1)} %copy-done.7, f32[2,128,128]{2,1,0:T(8,128)S(1)} %copy-done.4, f32[2,128,128]{2,1,0:T(8,128)S(1)} %copy-done.3, f32[2,2,128,128]{3,2,1,0:T(8,128)S(1)} %copy-done.2), custom_call_target="tpu_custom_call" | custom-call | tf_op jit(solution)/shard_map/pallas_call | solution.py:401
  12.0 0.3 collective-permute-done.3
  12.3 1.4 %collective-permute-start.4 = (f32[4,6144]{1,0:T(4,128)S(1)}, f32[4,6144]{1,0:T(4,128)S(1)}, u32[]{:S(2)}, u32[]{:S(2)}) collective-permute-start(f32[4,6144]{1,0:T(4,128)S(1)} %slice_select_fusion), channel_id=1, source_target_pairs={{0,16},{16,0},{1,17},{17,1},{2,18},{18,2},{3,19},{19,3},{4,20},{20... | collective-permute-start | bytes 294920 | tf_op jit(solution)/shard_map/ppermute | solution.py:384
  13.7 0.2 collective-permute-done.2
  13.9 0.4 %collective-permute-done.1 = f32[8,128]{1,0:T(8,128)S(1)} collective-permute-done((f32[8,128]{1,0:T(8,128)S(1)}, f32[8,128]{1,0:T(8,128)S(1)}, u32[]{:S(2)}, u32[]{:S(2)}) %collective-permute-start.1) | collective-permute-done | bytes 4128 | tf_op jit(solution)/shard_map/ppermute | solution.py:346
  14.4 0.0 collective-permute-done.6
  14.4 0.0 collective-permute-done.5
  14.4 2.5 %collective-permute-done.4.other_ref = f32[4,6144]{1,0:T(4,128)S(1)} collective-permute-done((f32[4,6144]{1,0:T(4,128)S(1)}, f32[4,6144]{1,0:T(4,128)S(1)}, u32[]{:S(2)}, u32[]{:S(2)}) %collective-permute-start.4) | collective-permute-done | bytes 98336 | tf_op jit(solution)/shard_map/ppermute | solution.py:384
  16.9 0.3 shard_map.100
  17.2 0.6 %copy-done.5 = bf16[128,192]{1,0:T(8,128)(2,1)S(1)} copy-done((bf16[128,192]{1,0:T(8,128)(2,1)S(1)}, bf16[128,192]{1,0:T(8,128)(2,1)}, u32[]{:S(2)}) %copy-start.5) | copy-done | bytes 49176
  17.7 12.0 %shard_map.102 = f32[32,4096]{1,0:T(8,128)} custom-call(f32[8,128]{1,0:T(8,128)S(1)} %add_add_fusion.tab_ref, f32[8,16384]{1,0:T(8,128)S(1)} %get-tuple-element.11.first_ref, bf16[16,16384]{1,0:T(8,128)(2,1)S(1)} %get-tuple-element.12.pack_in_ref, bf16[16,16384]{1,0:T(8,128)(2,1)S(1)} %get-tuple-element.13.high_in_ref, ...), custom_call_target="tpu_custom_call" | custom-call | tf_op jit(solution)/shard_map/pallas_call | solution.py:425
  (17 shorter events, 0.1 us)
Async XLA Ops:
  0.0 5.7 %copy-start = (f32[1,4,128,256]{3,2,1,0:T(8,128)S(1)}, f32[1,4,128,256]{3,2,1,0:T(8,128)}, u32[]{:S(2)}) copy-start(f32[1,4,128,256]{3,2,1,0:T(8,128)} %param.10) | copy-start | bytes 1572868
  0.0 0.7 %copy-start.8 = (s32[4,8]{1,0:T(4,128)S(1)}, s32[4,8]{1,0:T(4,128)}, u32[]{:S(2)}) copy-start(s32[4,8]{1,0:T(4,128)} %param.11) | copy-start | bytes 388
  0.7 0.7 %copy-start.9 = (f32[4,8]{1,0:T(4,128)S(1)}, f32[4,8]{1,0:T(4,128)}, u32[]{:S(2)}) copy-start(f32[4,8]{1,0:T(4,128)} %param.12) | copy-start | bytes 388
  1.5 6.1 %collective-permute-start = (f32[8,128]{1,0:T(8,128)S(1)}, f32[8,128]{1,0:T(8,128)S(1)}, u32[]{:S(2)}, u32[]{:S(2)}) collective-permute-start(f32[8,128]{1,0:T(8,128)S(1)} %broadcast_multiply_fusion), channel_id=1, source_target_pairs={{0,4},{1,5},{2,6},{3,7},{4,0},{5,1},{6,2},{7,3},{8,12},{9,13},{10,... | collective-permute-start | bytes 12296 | tf_op jit(solution)/shard_map/ppermute | solution.py:342
  5.8 5.5 %copy-start.4 = (f32[2,128,128]{2,1,0:T(8,128)S(1)}, f32[2,128,128]{2,1,0:T(8,128)}, u32[]{:S(2)}) copy-start(f32[2,128,128]{2,1,0:T(8,128)} %constant.80.clone.x_inv_ref) | copy-start | bytes 393220
  6.0 5.3 %copy-start.2 = (f32[2,2,128,128]{3,2,1,0:T(8,128)S(1)}, f32[2,2,128,128]{3,2,1,0:T(8,128)}, u32[]{:S(2)}) copy-start(f32[2,2,128,128]{3,2,1,0:T(8,128)} %constant.82.clone.z_inv_ref) | copy-start | bytes 786436
  6.0 8.4 %collective-permute-start.6 = (f32[4,2048]{1,0:T(4,128)S(1)}, f32[4,2048]{1,0:T(4,128)S(1)}, u32[]{:S(2)}, u32[]{:S(2)}) collective-permute-start(f32[4,2048]{1,0:T(4,128)S(1)} %slice_select_fusion.1), channel_id=1, source_target_pairs={{0,24},{1,25},{2,26},{3,27},{8,16},{9,17},{10,18},{11,19},{16,8},{... | collective-permute-start | bytes 98312 | tf_op jit(solution)/shard_map/ppermute | solution.py:376
  6.7 7.6 %collective-permute-start.5 = (f32[4,2048]{1,0:T(4,128)S(1)}, f32[4,2048]{1,0:T(4,128)S(1)}, u32[]{:S(2)}, u32[]{:S(2)}) collective-permute-start(f32[4,2048]{1,0:T(4,128)S(1)} %slice_select_fusion.1), channel_id=1, source_target_pairs={{0,8},{1,9},{2,10},{3,11},{8,0},{9,1},{10,2},{11,3},{16,24},{17,25... | collective-permute-start | bytes 98312 | tf_op jit(solution)/shard_map/ppermute | solution.py:376
  7.7 3.6 %copy-start.3 = (f32[2,128,128]{2,1,0:T(8,128)S(1)}, f32[2,128,128]{2,1,0:T(8,128)}, u32[]{:S(2)}) copy-start(f32[2,128,128]{2,1,0:T(8,128)} %constant.81.clone.y_inv_ref) | copy-start | bytes 393220
  7.7 3.6 %copy-start.7 = (s32[1,3]{1,0:T(1,128)S(1)}, s32[1,3]{1,0:T(1,128)}, u32[]{:S(2)}) copy-start(s32[1,3]{1,0:T(1,128)} %shift_ref.1) | copy-start | bytes 40
  7.7 4.6 %collective-permute-start.3 = (f32[8,128]{1,0:T(8,128)S(1)}, f32[8,128]{1,0:T(8,128)S(1)}, u32[]{:S(2)}, u32[]{:S(2)}) collective-permute-start(f32[8,128]{1,0:T(8,128)S(1)} %fusion), channel_id=1, source_target_pairs={{0,3},{1,2},{2,1},{3,0},{4,7},{5,6},{6,5},{7,4},{8,11},{9,10},{10,... | collective-permute-start | bytes 12296 | tf_op jit(solution)/shard_map/ppermute | solution.py:346
  10.3 3.6 %collective-permute-start.2 = (f32[8,128]{1,0:T(8,128)S(1)}, f32[8,128]{1,0:T(8,128)S(1)}, u32[]{:S(2)}, u32[]{:S(2)}) collective-permute-start(f32[8,128]{1,0:T(8,128)S(1)} %fusion), channel_id=1, source_target_pairs={{0,2},{1,3},{2,0},{3,1},{4,6},{5,7},{6,4},{7,5},{8,10},{9,11},{10,... | collective-permute-start | bytes 12296 | tf_op jit(solution)/shard_map/ppermute | solution.py:346
  10.7 3.6 %collective-permute-start.1 = (f32[8,128]{1,0:T(8,128)S(1)}, f32[8,128]{1,0:T(8,128)S(1)}, u32[]{:S(2)}, u32[]{:S(2)}) collective-permute-start(f32[8,128]{1,0:T(8,128)S(1)} %fusion), channel_id=1, source_target_pairs={{0,1},{1,0},{2,3},{3,2},{4,5},{5,4},{6,7},{7,6},{8,9},{9,8},{10,11... | collective-permute-start | bytes 12296 | tf_op jit(solution)/shard_map/ppermute | solution.py:346
  11.3 5.9 %copy-start.1 = (bf16[768,256]{1,0:T(8,128)(2,1)S(1)}, bf16[768,256]{1,0:T(8,128)(2,1)}, u32[]{:S(2)}) copy-start(bf16[768,256]{1,0:T(8,128)(2,1)} %constant.78.clone.y_fwd_ref) | copy-start | bytes 1179652
  12.3 4.6 %collective-permute-start.4 = (f32[4,6144]{1,0:T(4,128)S(1)}, f32[4,6144]{1,0:T(4,128)S(1)}, u32[]{:S(2)}, u32[]{:S(2)}) collective-permute-start(f32[4,6144]{1,0:T(4,128)S(1)} %slice_select_fusion), channel_id=1, source_target_pairs={{0,16},{16,0},{1,17},{17,1},{2,18},{18,2},{3,19},{19,3},{4,20},{20... | collective-permute-start | bytes 294920 | tf_op jit(solution)/shard_map/ppermute | solution.py:384
  16.9 0.8 %copy-start.5 = (bf16[128,192]{1,0:T(8,128)(2,1)S(1)}, bf16[128,192]{1,0:T(8,128)(2,1)}, u32[]{:S(2)}) copy-start(bf16[128,192]{1,0:T(8,128)(2,1)} %constant.79.clone.x_fwd_ref) | copy-start | bytes 147460
  16.9 0.8 %copy-start.6 = (bf16[80,192]{1,0:T(8,128)(2,1)S(1)}, bf16[80,192]{1,0:T(8,128)(2,1)}, u32[]{:S(2)}) copy-start(bf16[80,192]{1,0:T(8,128)(2,1)} %constant.77.clone.z_fwd_ref) | copy-start | bytes 92164

commit v4 on v3

--- a/solution.py
+++ b/solution.py
@@ -18,7 +18,8 @@
 PAIRS = 9
 REACH = 18
 UNROLL = 2
-STEPS = 9
+STEPS = 8
+PLANES = 18
 GROUPS = 24
 GAP = 72
 spectral_floor = 0.01
@@ -52,9 +53,7 @@
 def constant_tables():
     c, s = dft_parts()
     n = BRICK
-    zt = np.zeros((2 * ROWS, n))
-    zt[: HALF + 1], zt[ROWS : ROWS + HALF + 1] = c[: HALF + 1], -s[: HALF + 1]
-    high, low = host_split(zt)
+    high, low = host_split(np.concatenate([c[: HALF + 1], -s[1:HALF]], axis=0))
     z_fwd = np.concatenate([high, high, low], axis=1)
     yt = np.zeros((2, 2, n, 2, 2, n))
     for e in range(2):
@@ -62,10 +61,13 @@
         yt[1, e, :, 0, e], yt[1, e, :, 1, e] = s, c
     high, low = host_split(yt.reshape(4 * n, 4 * n))
     y_fwd = np.concatenate([high, high, low], axis=0)
-    high, low = host_split(np.concatenate([c, s], axis=0))
+    fold = np.zeros((n, n))
+    fold[:HALF, 1:HALF], fold[HALF, 1:HALF] = c[:HALF, 1:HALF], c[HALF, 1:HALF]
+    fold[HALF + 1 :, HALF + 1 :] = s[1:HALF, 1:HALF]
+    fold[0 : HALF + 1 : 2, 0] = fold[1:HALF:2, HALF] = c[0, 0]
+    high, low = host_split(fold)
     x_fwd = np.concatenate([high, high, low], axis=1)
     twice = lambda t: np.concatenate([t, t], axis=0)
-    x_inv = np.stack([np.tile(twice(t), (1, 2)) for t in (c, s)]).astype(np.float32)
     y_inv = np.stack([np.concatenate([twice(c), twice(-s)], 1).T, np.concatenate([twice(s), twice(c)], 1).T])
     y_inv = y_inv.astype(np.float32)
     weight = np.zeros(2 * GROUPS)
@@ -76,7 +78,7 @@
         pick = np.concatenate([(t[:, : 2 * GROUPS] * weight)[:, odd::2] for t in (c, -s)], axis=1)
         whole = twice(np.pad(np.tile(pick, (1, 3)), ((0, 0), (0, 4 * n - 6 * GROUPS))))
         z_inv.append(np.stack([whole[:, : 2 * n], whole[:, 2 * n :]]))
-    return z_fwd, y_fwd, x_fwd, x_inv, y_inv, np.stack(z_inv).astype(np.float32)
+    return z_fwd, y_fwd, x_fwd, y_inv, np.stack(z_inv).astype(np.float32)
 
 
 def pack(both, pack_ref, high_ref):
@@ -87,16 +89,12 @@
     high_ref[...] = jnp.concatenate([high, later], axis=0).astype(bf16)
 
 
-def turn(shift_ref, x_inv_ref, y_inv_ref, z_inv_ref, xi_ref, yi_ref, zi_ref):
+def turn(shift_ref, y_inv_ref, z_inv_ref, yi_ref, zi_ref):
     n = BRICK
     w = 2 * n
     exp_index = lax.axis_index("exp")
 
-    sz, sx, sy = (shift_ref[0, i] + n for i in range(3))
-    moved = lax.rem(sx, n)
-    turned = jnp.concatenate([x_inv_ref[0, pl.ds(moved, n), :], x_inv_ref[1, pl.ds(moved, n), :]], axis=0)
-    high, low = split(turned)
-    xi_ref[...] = jnp.concatenate([high, low], axis=1)[:, : 3 * n]
+    sz, sy = shift_ref[0, 0] + n, shift_ref[0, 2] + n
     lane = lax.broadcasted_iota(jnp.int32, (n, w), 1)
     back = lax.rem(w - lax.rem(sy, n), w)
     for ri_out in range(2):
@@ -157,15 +155,20 @@
 
 
 def kernel(
-    tab_ref, first_ref, pack_in_ref, high_in_ref, xi_ref, yi_ref, zi_ref, z_fwd_ref, y_fwd_ref, x_fwd_ref,
+    shift_any, tab_ref, first_ref, pack_in_ref, high_in_ref, yi_ref, zi_ref, z_fwd_ref, y_fwd_ref, x_fwd_ref,
     out_hbm,
-    pack_ref, high_ref, shifted_ref, spec_ref, freq_ref, cross_ref,
+    pack_ref, high_ref, shifted_ref, spec_ref, edge_ref, freq_ref, cross_ref,
     wave_ref, line_ref, back_ref, forward_ref,
-    out_ref, out_sem,
+    out_ref, out_sem, shift_ref, shift_sem, place_ref,
 ):
     n = BRICK
     w = 2 * n
     exp_index = lax.axis_index("exp")
+
+    shift_copy = pltpu.make_async_copy(shift_any, shift_ref, shift_sem)
+    shift_copy.start()
+    line_ref[:, PLANES * GAP :, :] = jnp.zeros((2, (GROUPS - PLANES) * GAP, w), f32)
+    wave_ref[:, (PLANES - 1) * n :, :] = jnp.zeros((2, n, 2 * w), bf16)
 
     tab = tab_ref[...]
     rows = lax.broadcasted_iota(jnp.int32, (8, w), 0)
@@ -219,6 +222,9 @@
     later = pltpu.roll(jnp.concatenate([ratio[:, w:], ratio[:, :w]], axis=1), 4, 0)
     pack(jnp.where(lax.broadcasted_iota(jnp.int32, ratio.shape, 0) < 4, ratio, later), pack_ref, high_ref)
 
+    top = lax.broadcasted_iota(jnp.int32, (8, w), 0) == 0
+    place = lambda x: jnp.where(x <= HALF, x, n + HALF - x)
+
     per = 16
     chunk2 = per * w
 
@@ -230,15 +236,21 @@
         groups = []
         for j in range(per):
             piece = spec[:, w * j : w * (j + 1)]
-            groups.append(jnp.concatenate([piece[:ROWS], piece[ROWS:]], axis=1))
+            imag = jnp.concatenate([jnp.where(top, 0.0, piece[HALF : HALF + 8]), piece[HALF + 8 :]], axis=0)
+            groups.append(jnp.concatenate([piece[:HALF], imag], axis=1))
+            edge_ref[0, pl.ds(place(i * per + j), 1), :] = piece[HALF : HALF + 1]
         high, low = split(jnp.concatenate(groups, axis=0))
         lines = dot(jnp.concatenate([high, low, high], axis=1), y_fwd_ref[...])
-        at = pl.multiple_of(i * (per * ROWS), per * ROWS)
-        spec_ref[0, pl.ds(at, per * ROWS), :] = lines[:, :w]
-        spec_ref[1, pl.ds(at, per * ROWS), :] = lines[:, w:]
+        for j in range(per):
+            at = pl.multiple_of(place(i * per + j) * ROWS, ROWS)
+            spec_ref[0, pl.ds(at, HALF), :] = lines[j * HALF : (j + 1) * HALF, :w]
+            spec_ref[1, pl.ds(at, HALF), :] = lines[j * HALF : (j + 1) * HALF, w:]
         return 0
 
     lax.fori_loop(0, n // per, second_pass, 0)
+    high, low = split(jnp.concatenate([edge_ref[0], jnp.zeros((n, w), f32)], axis=1))
+    lines = dot(jnp.concatenate([high, low, high], axis=1), y_fwd_ref[...])
+    edge_ref[0], edge_ref[1] = lines[:, :w], lines[:, w:]
 
     lane = lax.broadcasted_iota(jnp.int32, (n, w), 1)
     row = lax.broadcasted_iota(jnp.int32, (n, w), 0)
@@ -250,41 +262,78 @@
         high, low = split(value)
         return jnp.concatenate([high, low, high], axis=0)
 
-    def spectra(i, _):
+    def folded(pieces):
+        value = jnp.concatenate(pieces, axis=1)
+        return three(jnp.concatenate([value[:HALF] + value[HALF:], value[:HALF] - value[HALF:]], axis=0))
+
+    def unfolded(both, sign):
+        cos_re, cos_im, sin_re, sin_im = (both[r : r + HALF, c : c + w] for r in (0, HALF) for c in (0, w))
+        re, re_mirror = cos_re - sin_im, cos_re + sin_im
+        im, im_mirror = cos_im + sin_re, cos_im - sin_re
+        if sign < 0:
+            re, re_mirror, im, im_mirror = re_mirror, re, im_mirror, im
+        pieces = []
+        for plain, mirror, cos_part, sin_part in ((re, re_mirror, cos_re, sin_re), (im, im_mirror, cos_im, sin_im)):
+            first = [jnp.where(top, cos_part[:8], plain[:8]), plain[8:]]
+            pieces.append(jnp.concatenate(first + [jnp.where(top, sin_part[:8], mirror[:8]), mirror[8:]], axis=0))
+        return pieces
+
+    def columns_to_spectrum(i):
         for t in range(UNROLL):
-            at = jnp.maximum(i - 2, 0) * UNROLL + t
-            both = dot(xi_ref[...], cross_ref[t])
-            re = both[:n, :w] - both[n:, w:]
-            im = both[:n, w:] + both[n:, :w]
-            high, low = split(jnp.concatenate([re, im], axis=1))
-            wave_ref[0, pl.ds(pl.multiple_of(at * n, n), n), :] = high
-            wave_ref[1, pl.ds(pl.multiple_of(at * n, n), n), :] = low
-        for t in range(UNROLL):
+            for odd in range(2):
+                kz = i * (2 * UNROLL) + 2 * t + odd
+                lines = [spec_ref[ri, pl.ds(kz, n, stride=ROWS), :] for ri in range(2)]
+                freq_ref[t, odd, 0], freq_ref[t, odd, 1] = unfolded(dot(x_fwd_ref[...], folded(lines)), -1.0)
+
+    def last_to_spectrum():
+        freq_ref[0, 0, 0], freq_ref[0, 0, 1] = unfolded(dot(x_fwd_ref[...], folded([edge_ref[0], edge_ref[1]])), -1.0)
+        freq_ref[0, 1] = jnp.zeros((2, n, w), f32)
+
+    def spectrum_to_cross(holds_anchor, count=UNROLL):
+        for t in range(count):
             re_a, im_a = freq_ref[t, 0, 0], freq_ref[t, 0, 1]
             re_b, im_b = freq_ref[t, 1, 0], freq_ref[t, 1, 1]
             re_one = jnp.where(lane < n, re_a, re_b)
             im_one = jnp.where(lane < n, im_a, im_b)
             re_two = swap(jnp.where(lane < n, re_b, re_a))
             im_two = swap(jnp.where(lane < n, im_b, im_a))
-            power = (re_one * re_one + im_one * im_one) * (re_two * re_two + im_two * im_two)
+            cross_re = re_one * re_two + im_one * im_two
+            cross_im = re_one * im_two - im_one * re_two
+            power = cross_re * cross_re + cross_im * cross_im
             gain = lax.rsqrt(jnp.maximum(power, spectral_floor * spectral_floor))
-            if t == 0:
-                gain = jnp.where(anchor & (i == 1), 0.0, gain)
-            cross_re = (re_one * re_two + im_one * im_two) * gain
-            cross_im = (re_one * im_two - im_one * re_two) * (gain * exp_sign)
-            cross_ref[t] = three(jnp.concatenate([cross_re, cross_im], axis=1))
-        for t in range(UNROLL):
-            for odd in range(2):
-                kz = jnp.minimum(i, STEPS - 1) * (2 * UNROLL) + 2 * t + odd
-                lines = [spec_ref[ri, pl.ds(kz, n, stride=ROWS), :] for ri in range(2)]
-                both = dot(x_fwd_ref[...], three(jnp.concatenate(lines, axis=1)))
-                freq_ref[t, odd, 0] = both[:n, :w] + both[n:, w:]
-                freq_ref[t, odd, 1] = both[:n, w:] - both[n:, :w]
+            if holds_anchor and t == 0:
+                gain = jnp.where(anchor, 0.0, gain)
+            cross_re, cross_im = cross_re * gain, cross_im * (gain * exp_sign)
+            cross_ref[t] = folded([cross_re, cross_im])
+
+    def cross_to_wave(i, count=UNROLL):
+        for t in range(count):
+            at = i * UNROLL + t
+            high, low = split(jnp.concatenate(unfolded(dot(x_fwd_ref[...], cross_ref[t]), 1.0), axis=1))
+            wave_ref[0, pl.ds(pl.multiple_of(at * n, n), n), :] = high
+            wave_ref[1, pl.ds(pl.multiple_of(at * n, n), n), :] = low
+
+    def spectra(i, _):
+        cross_to_wave(i - 2)
+        spectrum_to_cross(False)
+        columns_to_spectrum(i)
         return 0
 
-    lax.fori_loop(0, STEPS + 2, spectra, 0)
-
-    done = STEPS * UNROLL
+    shift_copy.wait()
+    for x in range(n):
+        place_ref[x] = place(lax.rem(shift_ref[0, 1] + (n + x), n))
+    columns_to_spectrum(0)
+    spectrum_to_cross(True)
+    columns_to_spectrum(1)
+    lax.fori_loop(2, STEPS, spectra, 0)
+    cross_to_wave(STEPS - 2)
+    spectrum_to_cross(False)
+    last_to_spectrum()
+    cross_to_wave(STEPS - 1)
+    spectrum_to_cross(False, 1)
+    cross_to_wave(STEPS, 1)
+
+    done = PLANES
     per = done // 2
 
     def inverse_y(i, _):
@@ -298,17 +347,16 @@
         return 0
 
     lax.fori_loop(0, 2, inverse_y, 0)
-    line_ref[:, done * GAP :, :] = jnp.zeros((2, (GROUPS - done) * GAP, w), f32)
 
     lane = lax.broadcasted_iota(jnp.int32, (HALF, w), 1)
-    x_per_step = 8
+    x_per_step = 16
 
     def planes(i, _):
         for t in range(x_per_step):
             pair = i * x_per_step + t
             cols = jnp.concatenate(
                 [
-                    jnp.concatenate([line_ref[ri, pl.ds(2 * pair + p, GROUPS, stride=GAP), :] for ri in range(2)], axis=0)
+                    jnp.concatenate([line_ref[ri, pl.ds(place_ref[2 * pair + p], GROUPS, stride=GAP), :] for ri in range(2)], axis=0)
                     for p in range(2)
                 ],
                 axis=1,
@@ -401,12 +449,11 @@
     turned = pl.pallas_call(
         turn,
         out_shape=[
-            jax.ShapeDtypeStruct((2 * n, 3 * n), bf16),
             jax.ShapeDtypeStruct((12 * n, 4 * n), bf16),
             jax.ShapeDtypeStruct((n, 6 * GROUPS), bf16),
         ],
-        in_specs=[pl.BlockSpec(memory_space=pltpu.SMEM)] + [vmem] * 3,
-        out_specs=[vmem] * 3,
+        in_specs=[pl.BlockSpec(memory_space=pltpu.SMEM)] + [vmem] * 2,
+        out_specs=[vmem] * 2,
         compiler_params=pltpu.CompilerParams(vmem_limit_bytes=8 * 1024 * 1024),
     )(shifts, *inverses)
     ready = pl.pallas_call(
@@ -425,24 +472,28 @@
     out = pl.pallas_call(
         kernel,
         out_shape=jax.ShapeDtypeStruct((HALF, n * n), f32),
-        in_specs=[vmem] * 10,
+        in_specs=[pl.BlockSpec(memory_space=pl.ANY)] + [vmem] * 9,
         out_specs=pl.BlockSpec(memory_space=pl.ANY),
         scratch_shapes=[
             pltpu.VMEM((16, second), bf16),
             pltpu.VMEM((16, second), bf16),
             pltpu.VMEM((8 * PAIRS, (n + 2 * REACH) * 2 * n), f32),
             pltpu.VMEM((2, n * ROWS, 2 * n), f32),
+            pltpu.VMEM((2, n, 2 * n), f32),
             pltpu.VMEM((UNROLL, 2, 2, n, 2 * n), f32),
             pltpu.VMEM((UNROLL, 3 * n, 4 * n), bf16),
-            pltpu.VMEM((2, STEPS * UNROLL * n, 4 * n), bf16),
+            pltpu.VMEM((2, PLANES * n, 4 * n), bf16),
             pltpu.VMEM((2, GROUPS * GAP, 2 * n), f32),
             pltpu.VMEM((n, 224), bf16),
             pltpu.VMEM((8 * PAIRS, 3 * n), bf16),
             pltpu.VMEM((HALF, n * n), f32),
-            pltpu.SemaphoreType.DMA((4,)),
+            pltpu.SemaphoreType.DMA((2,)),
+            pltpu.SMEM(shifts.shape, jnp.int32),
+            pltpu.SemaphoreType.DMA(()),
+            pltpu.SMEM((n,), jnp.int32),
         ],
         compiler_params=pltpu.CompilerParams(vmem_limit_bytes=40 * 1024 * 1024),
-    )(table, *ready, *turned, z_fwd, y_fwd, x_fwd)
+    )(shifts, table, *ready, *turned, z_fwd, y_fwd, x_fwd)
     return out.reshape(1, HALF, n * n)
 
 

time: 29.9 us -> 29 us (0.970)
  Pallas kernels: 12.9 us -> 12.1 us
    pallas_call x1, Pallas kernels: 12 us -> 11.1 us  [per_device(): pl.pallas_call(kernel, out_shape=jax.ShapeDtypeStruct((HALF, n * n), f32)...]
    unnamed x20 -> x18, local copies, waits for them, and re-layouts: 2 us -> 1.92 us
where the time goes in v4:
time: 29 us; the launch traced here: 28.8 us
  Pallas kernels  12.1 us (42%)
  starting transfers between devices  10.8 us (37%)
  waiting for transfers between devices  3.46 us (12%)
  local copies, waits for them, and re-layouts  2.29 us (8%)
    pallas_call x1, Pallas kernels, per_device(): pl.pallas_call(kernel, out_shape=jax.ShapeDtypeStruct((HALF, n * n), f32)...  11.1 us
    ppermute x1, starting transfers between devices, share_tables(): lax.ppermute(table, 'depth', [(i, i ^ step) for i in range(count)])  4.13 us
    ppermute x3, starting transfers between devices, share_tables(): lax.ppermute(table, 'depth', [(i, i ^ k) for i in range(count)])  3.55 us
    ppermute x1, waiting for transfers between devices, windows(): lax.ppermute(piece, 'exp', [(i, (i + 1) % exps) for i in range(exps)])  2.51 us
    unnamed x18, local copies, waits for them, and re-layouts  1.92 us
    ppermute x2, starting transfers between devices, windows(): lax.ppermute(sent, axes, edge(1, other) + edge(-1, other))[None]  1.67 us
    ppermute x1, starting transfers between devices, windows(): lax.ppermute(piece, 'exp', [(i, (i + 1) % exps) for i in range(exps)])  1.41 us
    ppermute x3, waiting for transfers between devices, share_tables(): lax.ppermute(table, 'depth', [(i, i ^ k) for i in range(count)])  0.94 us
  transfers between devices with their start and end apart: 7, of which 4 were waited for; matrix products, arithmetic and copies ran while one was open for 1% of the time, Pallas kernels for 2%

profile of v4, /device:TPU:0, one launch (start us, length us, event | category | flops | bytes accessed | tf_op | source)
XLA Modules:
  0.0 28.8 jit_solution(7297797052794673619)
XLA Ops:
  0.0 0.0 copy-start
  0.0 0.7 %copy-done.7 = s32[4,8]{1,0:T(4,128)S(1)} copy-done((s32[4,8]{1,0:T(4,128)S(1)}, s32[4,8]{1,0:T(4,128)}, u32[]{:S(2)}) %copy-start.7) | copy-done | bytes 152
  0.7 0.7 %copy-done.8 = f32[4,8]{1,0:T(4,128)S(1)} copy-done((f32[4,8]{1,0:T(4,128)S(1)}, f32[4,8]{1,0:T(4,128)}, u32[]{:S(2)}) %copy-start.8) | copy-done | bytes 152
  1.4 0.1 tile.10
  1.5 4.1 %collective-permute-start = (f32[8,128]{1,0:T(8,128)S(1)}, f32[8,128]{1,0:T(8,128)S(1)}, u32[]{:S(2)}, u32[]{:S(2)}) collective-permute-start(f32[8,128]{1,0:T(8,128)S(1)} %broadcast_multiply_fusion), channel_id=1, source_target_pairs={{0,4},{1,5},{2,6},{3,7},{4,0},{5,1},{6,2},{7,3},{8,12},{9,13},{10,... | collective-permute-start | bytes 12296 | tf_op jit(solution)/shard_map/ppermute | solution.py:390
  5.7 0.0 copy-done
  5.7 0.1 constant_dynamic-slice_fusion
  5.8 0.1 reshape.38.own_ref
  6.0 0.0 copy-start.2
  6.0 0.7 %collective-permute-start.6 = (f32[4,2048]{1,0:T(4,128)S(1)}, f32[4,2048]{1,0:T(4,128)S(1)}, u32[]{:S(2)}, u32[]{:S(2)}) collective-permute-start(f32[4,2048]{1,0:T(4,128)S(1)} %slice_select_fusion.1), channel_id=1, source_target_pairs={{0,24},{1,25},{2,26},{3,27},{8,16},{9,17},{10,18},{11,19},{16,8},{... | collective-permute-start | bytes 98312 | tf_op jit(solution)/shard_map/ppermute | solution.py:424
  6.7 1.0 %collective-permute-start.5 = (f32[4,2048]{1,0:T(4,128)S(1)}, f32[4,2048]{1,0:T(4,128)S(1)}, u32[]{:S(2)}, u32[]{:S(2)}) collective-permute-start(f32[4,2048]{1,0:T(4,128)S(1)} %slice_select_fusion.1), channel_id=1, source_target_pairs={{0,8},{1,9},{2,10},{3,11},{8,0},{9,1},{10,2},{11,3},{16,24},{17,25... | collective-permute-start | bytes 98312 | tf_op jit(solution)/shard_map/ppermute | solution.py:424
  7.7 0.0 collective-permute-done
  7.7 0.0 copy-start.6
  7.7 2.6 %collective-permute-start.3 = (f32[8,128]{1,0:T(8,128)S(1)}, f32[8,128]{1,0:T(8,128)S(1)}, u32[]{:S(2)}, u32[]{:S(2)}) collective-permute-start(f32[8,128]{1,0:T(8,128)S(1)} %fusion), channel_id=1, source_target_pairs={{0,3},{1,2},{2,1},{3,0},{4,7},{5,6},{6,5},{7,4},{8,11},{9,10},{10,... | collective-permute-start | bytes 12296 | tf_op jit(solution)/shard_map/ppermute | solution.py:394
  10.3 0.4 %collective-permute-start.2 = (f32[8,128]{1,0:T(8,128)S(1)}, f32[8,128]{1,0:T(8,128)S(1)}, u32[]{:S(2)}, u32[]{:S(2)}) collective-permute-start(f32[8,128]{1,0:T(8,128)S(1)} %fusion), channel_id=1, source_target_pairs={{0,2},{1,3},{2,0},{3,1},{4,6},{5,7},{6,4},{7,5},{8,10},{9,11},{10,... | collective-permute-start | bytes 12296 | tf_op jit(solution)/shard_map/ppermute | solution.py:394
  10.7 0.5 %collective-permute-start.1 = (f32[8,128]{1,0:T(8,128)S(1)}, f32[8,128]{1,0:T(8,128)S(1)}, u32[]{:S(2)}, u32[]{:S(2)}) collective-permute-start(f32[8,128]{1,0:T(8,128)S(1)} %fusion), channel_id=1, source_target_pairs={{0,1},{1,0},{2,3},{3,2},{4,5},{5,4},{6,7},{7,6},{8,9},{9,8},{10,11... | collective-permute-start | bytes 12296 | tf_op jit(solution)/shard_map/ppermute | solution.py:394
  11.3 0.0 copy-done.2
  11.3 0.0 copy-done.3
  11.3 0.0 copy-done.6
  11.3 0.0 copy-start.1
  11.3 0.7 %shard_map.92 = (bf16[768,256]{1,0:T(8,128)(2,1)S(1)}, bf16[64,144]{1,0:T(8,128)(2,1)S(1)}) custom-call(s32[1,3]{1,0:T(1,128)S(1)} %copy-done.6, f32[2,128,128]{2,1,0:T(8,128)S(1)} %copy-done.3, f32[2,2,128,128]{3,2,1,0:T(8,128)S(1)} %copy-done.2), custom_call_target="tpu_custom_call" | custom-call | tf_op jit(solution)/shard_map/pallas_call | solution.py:449
  12.0 0.3 collective-permute-done.3
  12.3 1.4 %collective-permute-start.4 = (f32[4,6144]{1,0:T(4,128)S(1)}, f32[4,6144]{1,0:T(4,128)S(1)}, u32[]{:S(2)}, u32[]{:S(2)}) collective-permute-start(f32[4,6144]{1,0:T(4,128)S(1)} %slice_select_fusion), channel_id=1, source_target_pairs={{0,16},{16,0},{1,17},{17,1},{2,18},{18,2},{3,19},{19,3},{4,20},{20... | collective-permute-start | bytes 294920 | tf_op jit(solution)/shard_map/ppermute | solution.py:432
  13.7 0.2 collective-permute-done.2
  13.9 0.4 %collective-permute-done.1 = f32[8,128]{1,0:T(8,128)S(1)} collective-permute-done((f32[8,128]{1,0:T(8,128)S(1)}, f32[8,128]{1,0:T(8,128)S(1)}, u32[]{:S(2)}, u32[]{:S(2)}) %collective-permute-start.1) | collective-permute-done | bytes 4128 | tf_op jit(solution)/shard_map/ppermute | solution.py:394
  14.3 0.0 collective-permute-done.6
  14.4 0.0 collective-permute-done.5
  14.4 2.5 %collective-permute-done.4.other_ref = f32[4,6144]{1,0:T(4,128)S(1)} collective-permute-done((f32[4,6144]{1,0:T(4,128)S(1)}, f32[4,6144]{1,0:T(4,128)S(1)}, u32[]{:S(2)}, u32[]{:S(2)}) %collective-permute-start.4) | collective-permute-done | bytes 98336 | tf_op jit(solution)/shard_map/ppermute | solution.py:432
  16.9 0.3 shard_map.91
  17.2 0.5 %copy-done.4 = bf16[64,192]{1,0:T(8,128)(2,1)S(1)} copy-done((bf16[64,192]{1,0:T(8,128)(2,1)S(1)}, bf16[64,192]{1,0:T(8,128)(2,1)}, u32[]{:S(2)}) %copy-start.4) | copy-done | bytes 24600
  17.6 0.0 copy-done.5
  17.6 11.1 %shard_map.93 = f32[32,4096]{1,0:T(8,128)} custom-call(s32[1,3]{1,0:T(1,128)S(1)} %copy-done.6, f32[8,128]{1,0:T(8,128)S(1)} %add_add_fusion.tab_ref, f32[8,16384]{1,0:T(8,128)S(1)} %get-tuple-element.10.first_ref, bf16[16,16384]{1,0:T(8,128)(2,1)S(1)} %get-tuple-element.11.pack_in_ref, bf16[16,16384]{1,0:T(8,128)(2,1)S(1)} %get-tuple-element.12.high_in_ref, ...), custom_call_target="tpu_custom_call" | custom-call | tf_op jit(solution)/shard_map/pallas_call | solution.py:472
  (15 shorter events, 0.1 us)
Async XLA Ops:
  0.0 5.7 %copy-start = (f32[1,4,128,256]{3,2,1,0:T(8,128)S(1)}, f32[1,4,128,256]{3,2,1,0:T(8,128)}, u32[]{:S(2)}) copy-start(f32[1,4,128,256]{3,2,1,0:T(8,128)} %param.9) | copy-start | bytes 1572868
  0.0 0.7 %copy-start.7 = (s32[4,8]{1,0:T(4,128)S(1)}, s32[4,8]{1,0:T(4,128)}, u32[]{:S(2)}) copy-start(s32[4,8]{1,0:T(4,128)} %param.10) | copy-start | bytes 388
  0.7 0.7 %copy-start.8 = (f32[4,8]{1,0:T(4,128)S(1)}, f32[4,8]{1,0:T(4,128)}, u32[]{:S(2)}) copy-start(f32[4,8]{1,0:T(4,128)} %param.11) | copy-start | bytes 388
  1.5 6.1 %collective-permute-start = (f32[8,128]{1,0:T(8,128)S(1)}, f32[8,128]{1,0:T(8,128)S(1)}, u32[]{:S(2)}, u32[]{:S(2)}) collective-permute-start(f32[8,128]{1,0:T(8,128)S(1)} %broadcast_multiply_fusion), channel_id=1, source_target_pairs={{0,4},{1,5},{2,6},{3,7},{4,0},{5,1},{6,2},{7,3},{8,12},{9,13},{10,... | collective-permute-start | bytes 12296 | tf_op jit(solution)/shard_map/ppermute | solution.py:390
  6.0 5.3 %copy-start.2 = (f32[2,2,128,128]{3,2,1,0:T(8,128)S(1)}, f32[2,2,128,128]{3,2,1,0:T(8,128)}, u32[]{:S(2)}) copy-start(f32[2,2,128,128]{3,2,1,0:T(8,128)} %constant.79.clone.z_inv_ref) | copy-start | bytes 786436
  6.0 8.4 %collective-permute-start.6 = (f32[4,2048]{1,0:T(4,128)S(1)}, f32[4,2048]{1,0:T(4,128)S(1)}, u32[]{:S(2)}, u32[]{:S(2)}) collective-permute-start(f32[4,2048]{1,0:T(4,128)S(1)} %slice_select_fusion.1), channel_id=1, source_target_pairs={{0,24},{1,25},{2,26},{3,27},{8,16},{9,17},{10,18},{11,19},{16,8},{... | collective-permute-start | bytes 98312 | tf_op jit(solution)/shard_map/ppermute | solution.py:424
  6.7 7.6 %collective-permute-start.5 = (f32[4,2048]{1,0:T(4,128)S(1)}, f32[4,2048]{1,0:T(4,128)S(1)}, u32[]{:S(2)}, u32[]{:S(2)}) collective-permute-start(f32[4,2048]{1,0:T(4,128)S(1)} %slice_select_fusion.1), channel_id=1, source_target_pairs={{0,8},{1,9},{2,10},{3,11},{8,0},{9,1},{10,2},{11,3},{16,24},{17,25... | collective-permute-start | bytes 98312 | tf_op jit(solution)/shard_map/ppermute | solution.py:424
  7.7 3.6 %copy-start.3 = (f32[2,128,128]{2,1,0:T(8,128)S(1)}, f32[2,128,128]{2,1,0:T(8,128)}, u32[]{:S(2)}) copy-start(f32[2,128,128]{2,1,0:T(8,128)} %constant.78.clone.y_inv_ref) | copy-start | bytes 393220
  7.7 3.6 %copy-start.6 = (s32[1,3]{1,0:T(1,128)S(1)}, s32[1,3]{1,0:T(1,128)}, u32[]{:S(2)}) copy-start(s32[1,3]{1,0:T(1,128)} %shift_any.1) | copy-start | bytes 40
  7.7 4.6 %collective-permute-start.3 = (f32[8,128]{1,0:T(8,128)S(1)}, f32[8,128]{1,0:T(8,128)S(1)}, u32[]{:S(2)}, u32[]{:S(2)}) collective-permute-start(f32[8,128]{1,0:T(8,128)S(1)} %fusion), channel_id=1, source_target_pairs={{0,3},{1,2},{2,1},{3,0},{4,7},{5,6},{6,5},{7,4},{8,11},{9,10},{10,... | collective-permute-start | bytes 12296 | tf_op jit(solution)/shard_map/ppermute | solution.py:394
  10.3 3.6 %collective-permute-start.2 = (f32[8,128]{1,0:T(8,128)S(1)}, f32[8,128]{1,0:T(8,128)S(1)}, u32[]{:S(2)}, u32[]{:S(2)}) collective-permute-start(f32[8,128]{1,0:T(8,128)S(1)} %fusion), channel_id=1, source_target_pairs={{0,2},{1,3},{2,0},{3,1},{4,6},{5,7},{6,4},{7,5},{8,10},{9,11},{10,... | collective-permute-start | bytes 12296 | tf_op jit(solution)/shard_map/ppermute | solution.py:394
  10.7 3.6 %collective-permute-start.1 = (f32[8,128]{1,0:T(8,128)S(1)}, f32[8,128]{1,0:T(8,128)S(1)}, u32[]{:S(2)}, u32[]{:S(2)}) collective-permute-start(f32[8,128]{1,0:T(8,128)S(1)} %fusion), channel_id=1, source_target_pairs={{0,1},{1,0},{2,3},{3,2},{4,5},{5,4},{6,7},{7,6},{8,9},{9,8},{10,11... | collective-permute-start | bytes 12296 | tf_op jit(solution)/shard_map/ppermute | solution.py:394
  11.3 5.9 %copy-start.1 = (bf16[768,256]{1,0:T(8,128)(2,1)S(1)}, bf16[768,256]{1,0:T(8,128)(2,1)}, u32[]{:S(2)}) copy-start(bf16[768,256]{1,0:T(8,128)(2,1)} %constant.76.clone.y_fwd_ref) | copy-start | bytes 1179652
  12.3 4.6 %collective-permute-start.4 = (f32[4,6144]{1,0:T(4,128)S(1)}, f32[4,6144]{1,0:T(4,128)S(1)}, u32[]{:S(2)}, u32[]{:S(2)}) collective-permute-start(f32[4,6144]{1,0:T(4,128)S(1)} %slice_select_fusion), channel_id=1, source_target_pairs={{0,16},{16,0},{1,17},{17,1},{2,18},{18,2},{3,19},{19,3},{4,20},{20... | collective-permute-start | bytes 294920 | tf_op jit(solution)/shard_map/ppermute | solution.py:432
  16.9 0.8 %copy-start.4 = (bf16[64,192]{1,0:T(8,128)(2,1)S(1)}, bf16[64,192]{1,0:T(8,128)(2,1)}, u32[]{:S(2)}) copy-start(bf16[64,192]{1,0:T(8,128)(2,1)} %constant.77.clone.x_fwd_ref) | copy-start | bytes 73732
  16.9 0.8 %copy-start.5 = (bf16[64,192]{1,0:T(8,128)(2,1)S(1)}, bf16[64,192]{1,0:T(8,128)(2,1)}, u32[]{:S(2)}) copy-start(bf16[64,192]{1,0:T(8,128)(2,1)} %constant.75.clone.z_fwd_ref) | copy-start | bytes 73732

commit v5 on v4

--- a/solution.py
+++ b/solution.py
@@ -198,7 +198,7 @@
         return jnp.concatenate(pieces, axis=0)
 
     lo_x, hi_x = -REACH, n + REACH
-    chunk = 20 * w
+    chunk = 100 * w
     back_w = back_ref[...]
     forward_w = forward_ref[...]
 
@@ -225,7 +225,7 @@
     top = lax.broadcasted_iota(jnp.int32, (8, w), 0) == 0
     place = lambda x: jnp.where(x <= HALF, x, n + HALF - x)
 
-    per = 16
+    per = 64
     chunk2 = per * w
 
     def second_pass(i, _):
@@ -349,7 +349,8 @@
     lax.fori_loop(0, 2, inverse_y, 0)
 
     lane = lax.broadcasted_iota(jnp.int32, (HALF, w), 1)
-    x_per_step = 16
+    x_per_step = 32
+    x_per_copy = 8
 
     def planes(i, _):
         for t in range(x_per_step):
@@ -366,15 +367,16 @@
             b_even, b_odd = both[HALF:, :w], both[HALF:, w:]
             value = jnp.where(lane < n, a_even, b_odd) + swap(jnp.where(lane < n, a_odd, b_even))
             out_ref[:, pl.ds(pl.multiple_of(pair * w, w), w)] = value
-        out_copy(i).start()
+            if t % x_per_copy == x_per_copy - 1:
+                out_copy(i * (x_per_step // x_per_copy) + t // x_per_copy).start()
         return 0
 
     def out_copy(i):
-        at = pl.ds(pl.multiple_of(i * (x_per_step * w), x_per_step * w), x_per_step * w)
+        at = pl.ds(pl.multiple_of(i * (x_per_copy * w), x_per_copy * w), x_per_copy * w)
         return pltpu.make_async_copy(out_ref.at[:, at], out_hbm.at[:, at], out_sem.at[i])
 
     lax.fori_loop(0, HALF // x_per_step, planes, 0)
-    for i in range(HALF // x_per_step):
+    for i in range(HALF // x_per_copy):
         out_copy(i).wait()
 
 
@@ -487,7 +489,7 @@
             pltpu.VMEM((n, 224), bf16),
             pltpu.VMEM((8 * PAIRS, 3 * n), bf16),
             pltpu.VMEM((HALF, n * n), f32),
-            pltpu.SemaphoreType.DMA((2,)),
+            pltpu.SemaphoreType.DMA((4,)),
             pltpu.SMEM(shifts.shape, jnp.int32),
             pltpu.SemaphoreType.DMA(()),
             pltpu.SMEM((n,), jnp.int32),

time: 29 us -> 26.9 us (0.928)
  Pallas kernels: 12.1 us -> 10 us
    pallas_call x1, Pallas kernels: 11.1 us -> 9.07 us  [per_device(): pl.pallas_call(kernel, out_shape=jax.ShapeDtypeStruct((HALF, n * n), f32)...]
  transfers between devices with their start and end apart: 7 -> 7, of which waited for: 4 -> 4; matrix products, arithmetic and copies ran while one was open for 1% -> 1% of each run, Pallas kernels for 2% -> 3%
where the time goes in v5:
time: 26.9 us; the launch traced here: 26.7 us
  starting transfers between devices  10.8 us (40%)
  Pallas kernels  10 us (37%)
  waiting for transfers between devices  3.46 us (13%)
  local copies, waits for them, and re-layouts  2.29 us (9%)
    pallas_call x1, Pallas kernels, per_device(): pl.pallas_call(kernel, out_shape=jax.ShapeDtypeStruct((HALF, n * n), f32)...  9.07 us
    ppermute x1, starting transfers between devices, share_tables(): lax.ppermute(table, 'depth', [(i, i ^ step) for i in range(count)])  4.13 us
    ppermute x3, starting transfers between devices, share_tables(): lax.ppermute(table, 'depth', [(i, i ^ k) for i in range(count)])  3.55 us
    ppermute x1, waiting for transfers between devices, windows(): lax.ppermute(piece, 'exp', [(i, (i + 1) % exps) for i in range(exps)])  2.51 us
    unnamed x18, local copies, waits for them, and re-layouts  1.92 us
    ppermute x2, starting transfers between devices, windows(): lax.ppermute(sent, axes, edge(1, other) + edge(-1, other))[None]  1.67 us
    ppermute x1, starting transfers between devices, windows(): lax.ppermute(piece, 'exp', [(i, (i + 1) % exps) for i in range(exps)])  1.41 us
    ppermute x3, waiting for transfers between devices, share_tables(): lax.ppermute(table, 'depth', [(i, i ^ k) for i in range(count)])  0.94 us
  transfers between devices with their start and end apart: 7, of which 4 were waited for; matrix products, arithmetic and copies ran while one was open for 1% of the time, Pallas kernels for 3%

profile of v5, /device:TPU:0, one launch (start us, length us, event | category | flops | bytes accessed | tf_op | source)
XLA Modules:
  0.0 26.7 jit_solution(16537364082492658490)
XLA Ops:
  0.0 0.0 copy-start
  0.0 0.7 %copy-done.7 = s32[4,8]{1,0:T(4,128)S(1)} copy-done((s32[4,8]{1,0:T(4,128)S(1)}, s32[4,8]{1,0:T(4,128)}, u32[]{:S(2)}) %copy-start.7) | copy-done | bytes 152
  0.7 0.7 %copy-done.8 = f32[4,8]{1,0:T(4,128)S(1)} copy-done((f32[4,8]{1,0:T(4,128)S(1)}, f32[4,8]{1,0:T(4,128)}, u32[]{:S(2)}) %copy-start.8) | copy-done | bytes 152
  1.4 0.1 tile.10
  1.5 4.1 %collective-permute-start = (f32[8,128]{1,0:T(8,128)S(1)}, f32[8,128]{1,0:T(8,128)S(1)}, u32[]{:S(2)}, u32[]{:S(2)}) collective-permute-start(f32[8,128]{1,0:T(8,128)S(1)} %broadcast_multiply_fusion), channel_id=1, source_target_pairs={{0,4},{1,5},{2,6},{3,7},{4,0},{5,1},{6,2},{7,3},{8,12},{9,13},{10,... | collective-permute-start | bytes 12296 | tf_op jit(solution)/shard_map/ppermute | solution.py:392
  5.7 0.0 copy-done
  5.7 0.1 constant_dynamic-slice_fusion
  5.8 0.1 reshape.38.own_ref
  6.0 0.0 copy-start.2
  6.0 0.7 %collective-permute-start.6 = (f32[4,2048]{1,0:T(4,128)S(1)}, f32[4,2048]{1,0:T(4,128)S(1)}, u32[]{:S(2)}, u32[]{:S(2)}) collective-permute-start(f32[4,2048]{1,0:T(4,128)S(1)} %slice_select_fusion.1), channel_id=1, source_target_pairs={{0,24},{1,25},{2,26},{3,27},{8,16},{9,17},{10,18},{11,19},{16,8},{... | collective-permute-start | bytes 98312 | tf_op jit(solution)/shard_map/ppermute | solution.py:426
  6.7 1.0 %collective-permute-start.5 = (f32[4,2048]{1,0:T(4,128)S(1)}, f32[4,2048]{1,0:T(4,128)S(1)}, u32[]{:S(2)}, u32[]{:S(2)}) collective-permute-start(f32[4,2048]{1,0:T(4,128)S(1)} %slice_select_fusion.1), channel_id=1, source_target_pairs={{0,8},{1,9},{2,10},{3,11},{8,0},{9,1},{10,2},{11,3},{16,24},{17,25... | collective-permute-start | bytes 98312 | tf_op jit(solution)/shard_map/ppermute | solution.py:426
  7.7 0.0 collective-permute-done
  7.7 0.0 copy-start.6
  7.7 2.6 %collective-permute-start.3 = (f32[8,128]{1,0:T(8,128)S(1)}, f32[8,128]{1,0:T(8,128)S(1)}, u32[]{:S(2)}, u32[]{:S(2)}) collective-permute-start(f32[8,128]{1,0:T(8,128)S(1)} %fusion), channel_id=1, source_target_pairs={{0,3},{1,2},{2,1},{3,0},{4,7},{5,6},{6,5},{7,4},{8,11},{9,10},{10,... | collective-permute-start | bytes 12296 | tf_op jit(solution)/shard_map/ppermute | solution.py:396
  10.3 0.4 %collective-permute-start.2 = (f32[8,128]{1,0:T(8,128)S(1)}, f32[8,128]{1,0:T(8,128)S(1)}, u32[]{:S(2)}, u32[]{:S(2)}) collective-permute-start(f32[8,128]{1,0:T(8,128)S(1)} %fusion), channel_id=1, source_target_pairs={{0,2},{1,3},{2,0},{3,1},{4,6},{5,7},{6,4},{7,5},{8,10},{9,11},{10,... | collective-permute-start | bytes 12296 | tf_op jit(solution)/shard_map/ppermute | solution.py:396
  10.7 0.5 %collective-permute-start.1 = (f32[8,128]{1,0:T(8,128)S(1)}, f32[8,128]{1,0:T(8,128)S(1)}, u32[]{:S(2)}, u32[]{:S(2)}) collective-permute-start(f32[8,128]{1,0:T(8,128)S(1)} %fusion), channel_id=1, source_target_pairs={{0,1},{1,0},{2,3},{3,2},{4,5},{5,4},{6,7},{7,6},{8,9},{9,8},{10,11... | collective-permute-start | bytes 12296 | tf_op jit(solution)/shard_map/ppermute | solution.py:396
  11.3 0.0 copy-done.2
  11.3 0.0 copy-done.3
  11.3 0.0 copy-done.6
  11.3 0.0 copy-start.1
  11.3 0.7 %shard_map.92 = (bf16[768,256]{1,0:T(8,128)(2,1)S(1)}, bf16[64,144]{1,0:T(8,128)(2,1)S(1)}) custom-call(s32[1,3]{1,0:T(1,128)S(1)} %copy-done.6, f32[2,128,128]{2,1,0:T(8,128)S(1)} %copy-done.3, f32[2,2,128,128]{3,2,1,0:T(8,128)S(1)} %copy-done.2), custom_call_target="tpu_custom_call" | custom-call | tf_op jit(solution)/shard_map/pallas_call | solution.py:451
  12.0 0.3 %collective-permute-done.3 = f32[8,128]{1,0:T(8,128)S(1)} collective-permute-done((f32[8,128]{1,0:T(8,128)S(1)}, f32[8,128]{1,0:T(8,128)S(1)}, u32[]{:S(2)}, u32[]{:S(2)}) %collective-permute-start.3) | collective-permute-done | bytes 4128 | tf_op jit(solution)/shard_map/ppermute | solution.py:396
  12.3 1.4 %collective-permute-start.4 = (f32[4,6144]{1,0:T(4,128)S(1)}, f32[4,6144]{1,0:T(4,128)S(1)}, u32[]{:S(2)}, u32[]{:S(2)}) collective-permute-start(f32[4,6144]{1,0:T(4,128)S(1)} %slice_select_fusion), channel_id=1, source_target_pairs={{0,16},{16,0},{1,17},{17,1},{2,18},{18,2},{3,19},{19,3},{4,20},{20... | collective-permute-start | bytes 294920 | tf_op jit(solution)/shard_map/ppermute | solution.py:434
  13.7 0.2 collective-permute-done.2
  13.9 0.4 %collective-permute-done.1 = f32[8,128]{1,0:T(8,128)S(1)} collective-permute-done((f32[8,128]{1,0:T(8,128)S(1)}, f32[8,128]{1,0:T(8,128)S(1)}, u32[]{:S(2)}, u32[]{:S(2)}) %collective-permute-start.1) | collective-permute-done | bytes 4128 | tf_op jit(solution)/shard_map/ppermute | solution.py:396
  14.3 0.0 collective-permute-done.6
  14.4 0.0 collective-permute-done.5
  14.4 2.5 %collective-permute-done.4.other_ref = f32[4,6144]{1,0:T(4,128)S(1)} collective-permute-done((f32[4,6144]{1,0:T(4,128)S(1)}, f32[4,6144]{1,0:T(4,128)S(1)}, u32[]{:S(2)}, u32[]{:S(2)}) %collective-permute-start.4) | collective-permute-done | bytes 98336 | tf_op jit(solution)/shard_map/ppermute | solution.py:434
  16.9 0.3 %shard_map.91 = (f32[8,16384]{1,0:T(8,128)S(1)}, bf16[16,16384]{1,0:T(8,128)(2,1)S(1)}, bf16[16,16384]{1,0:T(8,128)(2,1)S(1)}) custom-call(f32[4,8192]{1,0:T(4,128)S(1)} %reshape.38.own_ref, f32[4,6144]{1,0:T(4,128)S(1)} %collective-permute-done.4.other_ref, f32[1,4,2048]{2,1,0:T(4,128)S(1)} %bitcast.6, f32[1,4,2048]{2,1,0:T(4,128)S(1)} %bitcast.5), custom_call_target="tpu_custom_call" | custom-call | tf_op jit(solution)/shard_map/pallas_call | solution.py:461
  17.2 0.5 %copy-done.4 = bf16[64,192]{1,0:T(8,128)(2,1)S(1)} copy-done((bf16[64,192]{1,0:T(8,128)(2,1)S(1)}, bf16[64,192]{1,0:T(8,128)(2,1)}, u32[]{:S(2)}) %copy-start.4) | copy-done | bytes 24600
  17.6 0.0 copy-done.5
  17.6 9.1 %shard_map.93 = f32[32,4096]{1,0:T(8,128)} custom-call(s32[1,3]{1,0:T(1,128)S(1)} %copy-done.6, f32[8,128]{1,0:T(8,128)S(1)} %add_add_fusion.tab_ref, f32[8,16384]{1,0:T(8,128)S(1)} %get-tuple-element.10.first_ref, bf16[16,16384]{1,0:T(8,128)(2,1)S(1)} %get-tuple-element.11.pack_in_ref, bf16[16,16384]{1,0:T(8,128)(2,1)S(1)} %get-tuple-element.12.high_in_ref, ...), custom_call_target="tpu_custom_call" | custom-call | tf_op jit(solution)/shard_map/pallas_call | solution.py:474
  (15 shorter events, 0.1 us)
Async XLA Ops:
  0.0 5.7 %copy-start = (f32[1,4,128,256]{3,2,1,0:T(8,128)S(1)}, f32[1,4,128,256]{3,2,1,0:T(8,128)}, u32[]{:S(2)}) copy-start(f32[1,4,128,256]{3,2,1,0:T(8,128)} %param.9) | copy-start | bytes 1572868
  0.0 0.7 %copy-start.7 = (s32[4,8]{1,0:T(4,128)S(1)}, s32[4,8]{1,0:T(4,128)}, u32[]{:S(2)}) copy-start(s32[4,8]{1,0:T(4,128)} %param.10) | copy-start | bytes 388
  0.7 0.7 %copy-start.8 = (f32[4,8]{1,0:T(4,128)S(1)}, f32[4,8]{1,0:T(4,128)}, u32[]{:S(2)}) copy-start(f32[4,8]{1,0:T(4,128)} %param.11) | copy-start | bytes 388
  1.5 6.1 %collective-permute-start = (f32[8,128]{1,0:T(8,128)S(1)}, f32[8,128]{1,0:T(8,128)S(1)}, u32[]{:S(2)}, u32[]{:S(2)}) collective-permute-start(f32[8,128]{1,0:T(8,128)S(1)} %broadcast_multiply_fusion), channel_id=1, source_target_pairs={{0,4},{1,5},{2,6},{3,7},{4,0},{5,1},{6,2},{7,3},{8,12},{9,13},{10,... | collective-permute-start | bytes 12296 | tf_op jit(solution)/shard_map/ppermute | solution.py:392
  6.0 5.3 %copy-start.2 = (f32[2,2,128,128]{3,2,1,0:T(8,128)S(1)}, f32[2,2,128,128]{3,2,1,0:T(8,128)}, u32[]{:S(2)}) copy-start(f32[2,2,128,128]{3,2,1,0:T(8,128)} %constant.79.clone.z_inv_ref) | copy-start | bytes 786436
  6.0 8.4 %collective-permute-start.6 = (f32[4,2048]{1,0:T(4,128)S(1)}, f32[4,2048]{1,0:T(4,128)S(1)}, u32[]{:S(2)}, u32[]{:S(2)}) collective-permute-start(f32[4,2048]{1,0:T(4,128)S(1)} %slice_select_fusion.1), channel_id=1, source_target_pairs={{0,24},{1,25},{2,26},{3,27},{8,16},{9,17},{10,18},{11,19},{16,8},{... | collective-permute-start | bytes 98312 | tf_op jit(solution)/shard_map/ppermute | solution.py:426
  6.7 7.6 %collective-permute-start.5 = (f32[4,2048]{1,0:T(4,128)S(1)}, f32[4,2048]{1,0:T(4,128)S(1)}, u32[]{:S(2)}, u32[]{:S(2)}) collective-permute-start(f32[4,2048]{1,0:T(4,128)S(1)} %slice_select_fusion.1), channel_id=1, source_target_pairs={{0,8},{1,9},{2,10},{3,11},{8,0},{9,1},{10,2},{11,3},{16,24},{17,25... | collective-permute-start | bytes 98312 | tf_op jit(solution)/shard_map/ppermute | solution.py:426
  7.7 3.6 %copy-start.3 = (f32[2,128,128]{2,1,0:T(8,128)S(1)}, f32[2,128,128]{2,1,0:T(8,128)}, u32[]{:S(2)}) copy-start(f32[2,128,128]{2,1,0:T(8,128)} %constant.78.clone.y_inv_ref) | copy-start | bytes 393220
  7.7 3.6 %copy-start.6 = (s32[1,3]{1,0:T(1,128)S(1)}, s32[1,3]{1,0:T(1,128)}, u32[]{:S(2)}) copy-start(s32[1,3]{1,0:T(1,128)} %shift_any.1) | copy-start | bytes 40
  7.7 4.6 %collective-permute-start.3 = (f32[8,128]{1,0:T(8,128)S(1)}, f32[8,128]{1,0:T(8,128)S(1)}, u32[]{:S(2)}, u32[]{:S(2)}) collective-permute-start(f32[8,128]{1,0:T(8,128)S(1)} %fusion), channel_id=1, source_target_pairs={{0,3},{1,2},{2,1},{3,0},{4,7},{5,6},{6,5},{7,4},{8,11},{9,10},{10,... | collective-permute-start | bytes 12296 | tf_op jit(solution)/shard_map/ppermute | solution.py:396
  10.3 3.6 %collective-permute-start.2 = (f32[8,128]{1,0:T(8,128)S(1)}, f32[8,128]{1,0:T(8,128)S(1)}, u32[]{:S(2)}, u32[]{:S(2)}) collective-permute-start(f32[8,128]{1,0:T(8,128)S(1)} %fusion), channel_id=1, source_target_pairs={{0,2},{1,3},{2,0},{3,1},{4,6},{5,7},{6,4},{7,5},{8,10},{9,11},{10,... | collective-permute-start | bytes 12296 | tf_op jit(solution)/shard_map/ppermute | solution.py:396
  10.7 3.6 %collective-permute-start.1 = (f32[8,128]{1,0:T(8,128)S(1)}, f32[8,128]{1,0:T(8,128)S(1)}, u32[]{:S(2)}, u32[]{:S(2)}) collective-permute-start(f32[8,128]{1,0:T(8,128)S(1)} %fusion), channel_id=1, source_target_pairs={{0,1},{1,0},{2,3},{3,2},{4,5},{5,4},{6,7},{7,6},{8,9},{9,8},{10,11... | collective-permute-start | bytes 12296 | tf_op jit(solution)/shard_map/ppermute | solution.py:396
  11.3 5.9 %copy-start.1 = (bf16[768,256]{1,0:T(8,128)(2,1)S(1)}, bf16[768,256]{1,0:T(8,128)(2,1)}, u32[]{:S(2)}) copy-start(bf16[768,256]{1,0:T(8,128)(2,1)} %constant.76.clone.y_fwd_ref) | copy-start | bytes 1179652
  12.3 4.6 %collective-permute-start.4 = (f32[4,6144]{1,0:T(4,128)S(1)}, f32[4,6144]{1,0:T(4,128)S(1)}, u32[]{:S(2)}, u32[]{:S(2)}) collective-permute-start(f32[4,6144]{1,0:T(4,128)S(1)} %slice_select_fusion), channel_id=1, source_target_pairs={{0,16},{16,0},{1,17},{17,1},{2,18},{18,2},{3,19},{19,3},{4,20},{20... | collective-permute-start | bytes 294920 | tf_op jit(solution)/shard_map/ppermute | solution.py:434
  16.9 0.8 %copy-start.4 = (bf16[64,192]{1,0:T(8,128)(2,1)S(1)}, bf16[64,192]{1,0:T(8,128)(2,1)}, u32[]{:S(2)}) copy-start(bf16[64,192]{1,0:T(8,128)(2,1)} %constant.77.clone.x_fwd_ref) | copy-start | bytes 73732
  16.9 0.8 %copy-start.5 = (bf16[64,192]{1,0:T(8,128)(2,1)S(1)}, bf16[64,192]{1,0:T(8,128)(2,1)}, u32[]{:S(2)}) copy-start(bf16[64,192]{1,0:T(8,128)(2,1)} %constant.75.clone.z_fwd_ref) | copy-start | bytes 73732

commit v6 on v5

--- a/solution.py
+++ b/solution.py
@@ -387,14 +387,15 @@
     lane = jnp.arange(2 * count * slab, dtype=jnp.int32) % (count * slab)
     mine = (lane // slab == lax.axis_index("depth")).astype(f32)
     table = jnp.tile(both, (1, 2 * count)) * mine
-    step = count // 2
-    while step > 2:
-        table = table + lax.ppermute(table, "depth", [(i, i ^ step) for i in range(count)])
-        step //= 2
     total = table
     for k in (1, 2, 3):
         total = total + lax.ppermute(table, "depth", [(i, i ^ k) for i in range(count)])
-    return total
+    table = total
+    step = 4
+    while step < count:
+        table = table + lax.ppermute(table, "depth", [(i, i ^ step) for i in range(count)])
+        step *= 2
+    return table
 
 
 def windows(images, bricks_x, bricks_y):

time: 26.9 us -> 24.3 us (0.903)
  waiting for transfers between devices: 3.46 us -> 2.07 us
  starting transfers between devices: 10.8 us -> 9.52 us
    ppermute x1, waiting for transfers between devices: 2.51 us -> 0.01 us  [windows(): lax.ppermute(piece, 'exp', [(i, (i + 1) % exps) for i in range(exps)])]
    ppermute x1, starting transfers between devices: 4.13 us -> 2.59 us  [share_tables(): lax.ppermute(table, 'depth', [(i, i ^ step) for i in range(count)])]
    ppermute x1, waiting for transfers between devices: 0.01 us -> 1.23 us  [share_tables(): lax.ppermute(table, 'depth', [(i, i ^ step) for i in range(count)])]
    ppermute x1, starting transfers between devices: 1.41 us -> 0.23 us  [windows(): lax.ppermute(piece, 'exp', [(i, (i + 1) % exps) for i in range(exps)])]
    ppermute x3, starting transfers between devices: 3.55 us -> 4.66 us  [share_tables(): lax.ppermute(table, 'depth', [(i, i ^ k) for i in range(count)])]
    ppermute x2, starting transfers between devices: 1.67 us -> 2.04 us  [windows(): lax.ppermute(sent, axes, edge(1, other) + edge(-1, other))[None]]
  transfers between devices with their start and end apart: 7 -> 7, of which waited for: 4 -> 3; matrix products, arithmetic and copies ran while one was open for 1% -> 1% of each run, Pallas kernels for 3% -> 3%
where the time goes in v6:
time: 24.3 us; the launch traced here: 24.1 us
  Pallas kernels  10 us (41%)
  starting transfers between devices  9.52 us (39%)
  local copies, waits for them, and re-layouts  2.28 us (9%)
  waiting for transfers between devices  2.07 us (9%)
    pallas_call x1, Pallas kernels, per_device(): pl.pallas_call(kernel, out_shape=jax.ShapeDtypeStruct((HALF, n * n), f32)...  9.06 us
    ppermute x3, starting transfers between devices, share_tables(): lax.ppermute(table, 'depth', [(i, i ^ k) for i in range(count)])  4.66 us
    ppermute x1, starting transfers between devices, share_tables(): lax.ppermute(table, 'depth', [(i, i ^ step) for i in range(count)])  2.59 us
    ppermute x2, starting transfers between devices, windows(): lax.ppermute(sent, axes, edge(1, other) + edge(-1, other))[None]  2.04 us
    unnamed x18, local copies, waits for them, and re-layouts  1.91 us
    ppermute x1, waiting for transfers between devices, share_tables(): lax.ppermute(table, 'depth', [(i, i ^ step) for i in range(count)])  1.23 us
    ppermute x3, waiting for transfers between devices, share_tables(): lax.ppermute(table, 'depth', [(i, i ^ k) for i in range(count)])  0.83 us
    pallas_call x1, Pallas kernels, per_device(): pl.pallas_call(turn, out_shape=[jax.ShapeDtypeStruct((12 * n, 4 * n), bf1...  0.67 us
  transfers between devices with their start and end apart: 7, of which 3 were waited for; matrix products, arithmetic and copies ran while one was open for 1% of the time, Pallas kernels for 3%

profile of v6, /device:TPU:0, one launch (start us, length us, event | category | flops | bytes accessed | tf_op | source)
XLA Modules:
  0.0 24.1 jit_solution(1154106680616985105)
XLA Ops:
  0.0 0.0 copy-start
  0.0 0.7 %copy-done.7 = s32[4,8]{1,0:T(4,128)S(1)} copy-done((s32[4,8]{1,0:T(4,128)S(1)}, s32[4,8]{1,0:T(4,128)}, u32[]{:S(2)}) %copy-start.7) | copy-done | bytes 152
  0.7 0.7 %copy-done.8 = f32[4,8]{1,0:T(4,128)S(1)} copy-done((f32[4,8]{1,0:T(4,128)S(1)}, f32[4,8]{1,0:T(4,128)}, u32[]{:S(2)}) %copy-start.8) | copy-done | bytes 152
  1.4 0.1 tile.10
  1.5 3.1 %collective-permute-start.1 = (f32[8,128]{1,0:T(8,128)S(1)}, f32[8,128]{1,0:T(8,128)S(1)}, u32[]{:S(2)}, u32[]{:S(2)}) collective-permute-start(f32[8,128]{1,0:T(8,128)S(1)} %broadcast_multiply_fusion), channel_id=1, source_target_pairs={{0,2},{1,3},{2,0},{3,1},{4,6},{5,7},{6,4},{7,5},{8,10},{9,11},{10,... | collective-permute-start | bytes 12296 | tf_op jit(solution)/shard_map/ppermute | solution.py:392
  4.7 1.4 %collective-permute-start.2 = (f32[8,128]{1,0:T(8,128)S(1)}, f32[8,128]{1,0:T(8,128)S(1)}, u32[]{:S(2)}, u32[]{:S(2)}) collective-permute-start(f32[8,128]{1,0:T(8,128)S(1)} %broadcast_multiply_fusion), channel_id=1, source_target_pairs={{0,3},{1,2},{2,1},{3,0},{4,7},{5,6},{6,5},{7,4},{8,11},{9,10},{10,... | collective-permute-start | bytes 12296 | tf_op jit(solution)/shard_map/ppermute | solution.py:392
  6.1 0.1 collective-permute-start
  6.2 0.1 constant_dynamic-slice_fusion
  6.3 0.1 reshape.38.own_ref
  6.5 0.0 copy-start.2
  6.5 0.0 copy-start.3
  6.5 0.5 %collective-permute-start.6 = (f32[4,2048]{1,0:T(4,128)S(1)}, f32[4,2048]{1,0:T(4,128)S(1)}, u32[]{:S(2)}, u32[]{:S(2)}) collective-permute-start(f32[4,2048]{1,0:T(4,128)S(1)} %slice_select_fusion.1), channel_id=1, source_target_pairs={{0,24},{1,25},{2,26},{3,27},{8,16},{9,17},{10,18},{11,19},{16,8},{... | collective-permute-start | bytes 98312 | tf_op jit(solution)/shard_map/ppermute | solution.py:427
  7.1 1.5 %collective-permute-start.5 = (f32[4,2048]{1,0:T(4,128)S(1)}, f32[4,2048]{1,0:T(4,128)S(1)}, u32[]{:S(2)}, u32[]{:S(2)}) collective-permute-start(f32[4,2048]{1,0:T(4,128)S(1)} %slice_select_fusion.1), channel_id=1, source_target_pairs={{0,8},{1,9},{2,10},{3,11},{8,0},{9,1},{10,2},{11,3},{16,24},{17,25... | collective-permute-start | bytes 98312 | tf_op jit(solution)/shard_map/ppermute | solution.py:427
  8.6 0.0 copy-start.1
  8.6 0.0 collective-permute-done.1
  8.6 0.2 collective-permute-start.4
  8.9 0.3 %collective-permute-done.2 = f32[8,128]{1,0:T(8,128)S(1)} collective-permute-done((f32[8,128]{1,0:T(8,128)S(1)}, f32[8,128]{1,0:T(8,128)S(1)}, u32[]{:S(2)}, u32[]{:S(2)}) %collective-permute-start.2) | collective-permute-done | bytes 4128 | tf_op jit(solution)/shard_map/ppermute | solution.py:392
  9.2 0.5 %collective-permute-done = f32[8,128]{1,0:T(8,128)S(1)} collective-permute-done((f32[8,128]{1,0:T(8,128)S(1)}, f32[8,128]{1,0:T(8,128)S(1)}, u32[]{:S(2)}, u32[]{:S(2)}) %collective-permute-start) | collective-permute-done | bytes 4128 | tf_op jit(solution)/shard_map/ppermute | solution.py:392
  9.7 2.6 %collective-permute-start.3 = (f32[8,128]{1,0:T(8,128)S(1)}, f32[8,128]{1,0:T(8,128)S(1)}, u32[]{:S(2)}, u32[]{:S(2)}) collective-permute-start(f32[8,128]{1,0:T(8,128)S(1)} %add_add_fusion), channel_id=1, source_target_pairs={{0,4},{1,5},{2,6},{3,7},{4,0},{5,1},{6,2},{7,3},{8,12},{9,13},{10,... | collective-permute-start | bytes 12296 | tf_op jit(solution)/shard_map/ppermute | solution.py:396
  12.3 0.0 copy-done.2
  12.3 0.0 copy-done.6
  12.3 0.7 %shard_map.92 = (bf16[768,256]{1,0:T(8,128)(2,1)S(1)}, bf16[64,144]{1,0:T(8,128)(2,1)S(1)}) custom-call(s32[1,3]{1,0:T(1,128)S(1)} %copy-done.6, f32[2,128,128]{2,1,0:T(8,128)S(1)} %copy-done.3, f32[2,2,128,128]{3,2,1,0:T(8,128)S(1)} %copy-done.2), custom_call_target="tpu_custom_call" | custom-call | tf_op jit(solution)/shard_map/pallas_call | solution.py:452
  13.0 1.2 %collective-permute-done.3 = f32[8,128]{1,0:T(8,128)S(1)} collective-permute-done((f32[8,128]{1,0:T(8,128)S(1)}, f32[8,128]{1,0:T(8,128)S(1)}, u32[]{:S(2)}, u32[]{:S(2)}) %collective-permute-start.3) | collective-permute-done | bytes 4128 | tf_op jit(solution)/shard_map/ppermute | solution.py:396
  14.2 0.0 collective-permute-done.6
  14.2 0.0 collective-permute-done.5
  14.2 0.0 collective-permute-done.4.other_ref
  14.2 0.0 copy-start.4
  14.2 0.0 copy-start.5
  14.2 0.3 %shard_map.91 = (f32[8,16384]{1,0:T(8,128)S(1)}, bf16[16,16384]{1,0:T(8,128)(2,1)S(1)}, bf16[16,16384]{1,0:T(8,128)(2,1)S(1)}) custom-call(f32[4,8192]{1,0:T(4,128)S(1)} %reshape.38.own_ref, f32[4,6144]{1,0:T(4,128)S(1)} %collective-permute-done.4.other_ref, f32[1,4,2048]{2,1,0:T(4,128)S(1)} %bitcast.6, f32[1,4,2048]{2,1,0:T(4,128)S(1)} %bitcast.5), custom_call_target="tpu_custom_call" | custom-call | tf_op jit(solution)/shard_map/pallas_call | solution.py:462
  14.5 0.4 %copy-done.4 = bf16[64,192]{1,0:T(8,128)(2,1)S(1)} copy-done((bf16[64,192]{1,0:T(8,128)(2,1)S(1)}, bf16[64,192]{1,0:T(8,128)(2,1)}, u32[]{:S(2)}) %copy-start.4) | copy-done | bytes 24600
  15.0 0.0 copy-done.5
  15.0 9.1 %shard_map.93 = f32[32,4096]{1,0:T(8,128)} custom-call(s32[1,3]{1,0:T(1,128)S(1)} %copy-done.6, f32[8,128]{1,0:T(8,128)S(1)} %add.39.tab_ref, f32[8,16384]{1,0:T(8,128)S(1)} %get-tuple-element.10.first_ref, bf16[16,16384]{1,0:T(8,128)(2,1)S(1)} %get-tuple-element.11.pack_in_ref, bf16[16,16384]{1,0:T(8,128)(2,1)S(1)} %get-tuple-element.12.high_in_ref, ...), custom_call_target="tpu_custom_call" | custom-call | tf_op jit(solution)/shard_map/pallas_call | solution.py:475
  (15 shorter events, 0.1 us)
Async XLA Ops:
  0.0 6.2 %copy-start = (f32[1,4,128,256]{3,2,1,0:T(8,128)S(1)}, f32[1,4,128,256]{3,2,1,0:T(8,128)}, u32[]{:S(2)}) copy-start(f32[1,4,128,256]{3,2,1,0:T(8,128)} %param.9) | copy-start | bytes 1572868
  0.0 0.7 %copy-start.7 = (s32[4,8]{1,0:T(4,128)S(1)}, s32[4,8]{1,0:T(4,128)}, u32[]{:S(2)}) copy-start(s32[4,8]{1,0:T(4,128)} %param.10) | copy-start | bytes 388
  0.7 0.7 %copy-start.8 = (f32[4,8]{1,0:T(4,128)S(1)}, f32[4,8]{1,0:T(4,128)}, u32[]{:S(2)}) copy-start(f32[4,8]{1,0:T(4,128)} %param.11) | copy-start | bytes 388
  1.5 7.1 %collective-permute-start.1 = (f32[8,128]{1,0:T(8,128)S(1)}, f32[8,128]{1,0:T(8,128)S(1)}, u32[]{:S(2)}, u32[]{:S(2)}) collective-permute-start(f32[8,128]{1,0:T(8,128)S(1)} %broadcast_multiply_fusion), channel_id=1, source_target_pairs={{0,2},{1,3},{2,0},{3,1},{4,6},{5,7},{6,4},{7,5},{8,10},{9,11},{10,... | collective-permute-start | bytes 12296 | tf_op jit(solution)/shard_map/ppermute | solution.py:392
  4.7 4.5 %collective-permute-start.2 = (f32[8,128]{1,0:T(8,128)S(1)}, f32[8,128]{1,0:T(8,128)S(1)}, u32[]{:S(2)}, u32[]{:S(2)}) collective-permute-start(f32[8,128]{1,0:T(8,128)S(1)} %broadcast_multiply_fusion), channel_id=1, source_target_pairs={{0,3},{1,2},{2,1},{3,0},{4,7},{5,6},{6,5},{7,4},{8,11},{9,10},{10,... | collective-permute-start | bytes 12296 | tf_op jit(solution)/shard_map/ppermute | solution.py:392
  6.1 3.6 %collective-permute-start = (f32[8,128]{1,0:T(8,128)S(1)}, f32[8,128]{1,0:T(8,128)S(1)}, u32[]{:S(2)}, u32[]{:S(2)}) collective-permute-start(f32[8,128]{1,0:T(8,128)S(1)} %broadcast_multiply_fusion), channel_id=1, source_target_pairs={{0,1},{1,0},{2,3},{3,2},{4,5},{5,4},{6,7},{7,6},{8,9},{9,8},{10,11... | collective-permute-start | bytes 12296 | tf_op jit(solution)/shard_map/ppermute | solution.py:392
  6.5 5.8 %copy-start.2 = (f32[2,2,128,128]{3,2,1,0:T(8,128)S(1)}, f32[2,2,128,128]{3,2,1,0:T(8,128)}, u32[]{:S(2)}) copy-start(f32[2,2,128,128]{3,2,1,0:T(8,128)} %constant.79.clone.z_inv_ref) | copy-start | bytes 786436
  6.5 5.8 %copy-start.3 = (f32[2,128,128]{2,1,0:T(8,128)S(1)}, f32[2,128,128]{2,1,0:T(8,128)}, u32[]{:S(2)}) copy-start(f32[2,128,128]{2,1,0:T(8,128)} %constant.78.clone.y_inv_ref) | copy-start | bytes 393220
  6.5 7.7 %collective-permute-start.6 = (f32[4,2048]{1,0:T(4,128)S(1)}, f32[4,2048]{1,0:T(4,128)S(1)}, u32[]{:S(2)}, u32[]{:S(2)}) collective-permute-start(f32[4,2048]{1,0:T(4,128)S(1)} %slice_select_fusion.1), channel_id=1, source_target_pairs={{0,24},{1,25},{2,26},{3,27},{8,16},{9,17},{10,18},{11,19},{16,8},{... | collective-permute-start | bytes 98312 | tf_op jit(solution)/shard_map/ppermute | solution.py:427
  7.1 7.1 %collective-permute-start.5 = (f32[4,2048]{1,0:T(4,128)S(1)}, f32[4,2048]{1,0:T(4,128)S(1)}, u32[]{:S(2)}, u32[]{:S(2)}) collective-permute-start(f32[4,2048]{1,0:T(4,128)S(1)} %slice_select_fusion.1), channel_id=1, source_target_pairs={{0,8},{1,9},{2,10},{3,11},{8,0},{9,1},{10,2},{11,3},{16,24},{17,25... | collective-permute-start | bytes 98312 | tf_op jit(solution)/shard_map/ppermute | solution.py:427
  8.6 3.7 %copy-start.6 = (s32[1,3]{1,0:T(1,128)S(1)}, s32[1,3]{1,0:T(1,128)}, u32[]{:S(2)}) copy-start(s32[1,3]{1,0:T(1,128)} %shift_any.1) | copy-start | bytes 40
  8.6 5.9 %copy-start.1 = (bf16[768,256]{1,0:T(8,128)(2,1)S(1)}, bf16[768,256]{1,0:T(8,128)(2,1)}, u32[]{:S(2)}) copy-start(bf16[768,256]{1,0:T(8,128)(2,1)} %constant.76.clone.y_fwd_ref) | copy-start | bytes 1179652
  8.6 5.6 %collective-permute-start.4 = (f32[4,6144]{1,0:T(4,128)S(1)}, f32[4,6144]{1,0:T(4,128)S(1)}, u32[]{:S(2)}, u32[]{:S(2)}) collective-permute-start(f32[4,6144]{1,0:T(4,128)S(1)} %slice_select_fusion), channel_id=1, source_target_pairs={{0,16},{16,0},{1,17},{17,1},{2,18},{18,2},{3,19},{19,3},{4,20},{20... | collective-permute-start | bytes 294920 | tf_op jit(solution)/shard_map/ppermute | solution.py:435
  9.7 4.5 %collective-permute-start.3 = (f32[8,128]{1,0:T(8,128)S(1)}, f32[8,128]{1,0:T(8,128)S(1)}, u32[]{:S(2)}, u32[]{:S(2)}) collective-permute-start(f32[8,128]{1,0:T(8,128)S(1)} %add_add_fusion), channel_id=1, source_target_pairs={{0,4},{1,5},{2,6},{3,7},{4,0},{5,1},{6,2},{7,3},{8,12},{9,13},{10,... | collective-permute-start | bytes 12296 | tf_op jit(solution)/shard_map/ppermute | solution.py:396
  14.2 0.8 %copy-start.4 = (bf16[64,192]{1,0:T(8,128)(2,1)S(1)}, bf16[64,192]{1,0:T(8,128)(2,1)}, u32[]{:S(2)}) copy-start(bf16[64,192]{1,0:T(8,128)(2,1)} %constant.77.clone.x_fwd_ref) | copy-start | bytes 73732
  14.2 0.8 %copy-start.5 = (bf16[64,192]{1,0:T(8,128)(2,1)S(1)}, bf16[64,192]{1,0:T(8,128)(2,1)}, u32[]{:S(2)}) copy-start(bf16[64,192]{1,0:T(8,128)(2,1)} %constant.75.clone.z_fwd_ref) | copy-start | bytes 73732

commit v7 on v6

--- a/solution.py
+++ b/solution.py
@@ -13,13 +13,13 @@
 BRICK = 64
 HALF = BRICK // 2
 ROWS = 40
-MARGIN = 32
+MARGIN = 26
 SHIFT_LOW = -8
 PAIRS = 9
 REACH = 18
 UNROLL = 2
 STEPS = 8
-PLANES = 18
+PLANES = 17
 GROUPS = 24
 GAP = 72
 spectral_floor = 0.01
@@ -168,7 +168,6 @@
     shift_copy = pltpu.make_async_copy(shift_any, shift_ref, shift_sem)
     shift_copy.start()
     line_ref[:, PLANES * GAP :, :] = jnp.zeros((2, (GROUPS - PLANES) * GAP, w), f32)
-    wave_ref[:, (PLANES - 1) * n :, :] = jnp.zeros((2, n, 2 * w), bf16)
 
     tab = tab_ref[...]
     rows = lax.broadcasted_iota(jnp.int32, (8, w), 0)
@@ -313,7 +312,17 @@
             wave_ref[0, pl.ds(pl.multiple_of(at * n, n), n), :] = high
             wave_ref[1, pl.ds(pl.multiple_of(at * n, n), n), :] = low
 
+    def wave_to_line(i, count=UNROLL):
+        rows = pl.ds(pl.multiple_of(i * (UNROLL * n), UNROLL * n), count * n)
+        high, low = wave_ref[0, rows, :], wave_ref[1, rows, :]
+        lines = dot(jnp.concatenate([high, low, high], axis=1), yi_ref[...])
+        for t in range(count):
+            to = pl.multiple_of((i * UNROLL + t) * GAP, 8)
+            line_ref[0, pl.ds(to, n), :] = lines[t * n : (t + 1) * n, :w]
+            line_ref[1, pl.ds(to, n), :] = lines[t * n : (t + 1) * n, w:]
+
     def spectra(i, _):
+        wave_to_line(i - 3)
         cross_to_wave(i - 2)
         spectrum_to_cross(False)
         columns_to_spectrum(i)
@@ -325,32 +334,24 @@
     columns_to_spectrum(0)
     spectrum_to_cross(True)
     columns_to_spectrum(1)
-    lax.fori_loop(2, STEPS, spectra, 0)
+    cross_to_wave(0)
+    spectrum_to_cross(False)
+    columns_to_spectrum(2)
+    lax.fori_loop(3, STEPS, spectra, 0)
+    wave_to_line(STEPS - 3)
     cross_to_wave(STEPS - 2)
     spectrum_to_cross(False)
     last_to_spectrum()
+    wave_to_line(STEPS - 2)
     cross_to_wave(STEPS - 1)
     spectrum_to_cross(False, 1)
+    wave_to_line(STEPS - 1)
     cross_to_wave(STEPS, 1)
-
-    done = PLANES
-    per = done // 2
-
-    def inverse_y(i, _):
-        at = pl.multiple_of(i * (per * n), per * n)
-        high, low = wave_ref[0, pl.ds(at, per * n), :], wave_ref[1, pl.ds(at, per * n), :]
-        lines = dot(jnp.concatenate([high, low, high], axis=1), yi_ref[...])
-        for t in range(per):
-            to = pl.multiple_of((i * per + t) * GAP, 8)
-            line_ref[0, pl.ds(to, n), :] = lines[t * n : (t + 1) * n, :w]
-            line_ref[1, pl.ds(to, n), :] = lines[t * n : (t + 1) * n, w:]
-        return 0
-
-    lax.fori_loop(0, 2, inverse_y, 0)
+    wave_to_line(STEPS, 1)
 
     lane = lax.broadcasted_iota(jnp.int32, (HALF, w), 1)
     x_per_step = 32
-    x_per_copy = 8
+    x_per_copy = 4
 
     def planes(i, _):
         for t in range(x_per_step):
@@ -380,13 +381,26 @@
         out_copy(i).wait()
 
 
+def table_kernel(offsets_ref, fractions_ref, out_ref):
+    slab = offsets_ref.shape[1]
+    width = out_ref.shape[1] // 2
+    both = jnp.concatenate([offsets_ref[...].astype(f32), fractions_ref[...]], axis=0)
+    wide = jnp.concatenate([both] * (2 * width // slab), axis=1)
+    lane = lax.broadcasted_iota(jnp.int32, wide.shape, 1)
+    out_ref[...] = jnp.where(lax.rem(lane, width) // slab == lax.axis_index("depth"), wide, 0.0)
+
+
 def share_tables(offsets, fractions):
-    both = jnp.concatenate([offsets.astype(f32), fractions], axis=0)
+    vmem = pl.BlockSpec(memory_space=pltpu.VMEM)
     count = lax.axis_size("depth")
-    slab = both.shape[1]
-    lane = jnp.arange(2 * count * slab, dtype=jnp.int32) % (count * slab)
-    mine = (lane // slab == lax.axis_index("depth")).astype(f32)
-    table = jnp.tile(both, (1, 2 * count)) * mine
+    cams, slab = offsets.shape
+    table = pl.pallas_call(
+        table_kernel,
+        out_shape=jax.ShapeDtypeStruct((2 * cams, 2 * count * slab), f32),
+        in_specs=[vmem] * 2,
+        out_specs=vmem,
+        compiler_params=pltpu.CompilerParams(vmem_limit_bytes=60 * 1024 * 1024),
+    )(offsets, fractions)
     total = table
     for k in (1, 2, 3):
         total = total + lax.ppermute(table, "depth", [(i, i ^ k) for i in range(count)])
@@ -490,7 +504,7 @@
             pltpu.VMEM((n, 224), bf16),
             pltpu.VMEM((8 * PAIRS, 3 * n), bf16),
             pltpu.VMEM((HALF, n * n), f32),
-            pltpu.SemaphoreType.DMA((4,)),
+            pltpu.SemaphoreType.DMA((8,)),
             pltpu.SMEM(shifts.shape, jnp.int32),
             pltpu.SemaphoreType.DMA(()),
             pltpu.SMEM((n,), jnp.int32),

time: 24.3 us -> 24.2 us (level)
  local copies, waits for them, and re-layouts: 2.28 us -> 0.8 us
  Pallas kernels: 10 us -> 11.2 us
  starting transfers between devices: 9.52 us -> 9.95 us
    pallas_call x0 -> x1, Pallas kernels: none -> 1.43 us  [share_tables(): pl.pallas_call(table_kernel, out_shape=jax.ShapeDtypeStruct((2 * cams, 2...]
    unnamed x18 -> x16, local copies, waits for them, and re-layouts: 1.91 us -> 0.53 us
    ppermute x1, starting transfers between devices: 0.23 us -> 0.66 us  [windows(): lax.ppermute(piece, 'exp', [(i, (i + 1) % exps) for i in range(exps)])]
where the time goes in v7:
time: 24.2 us; the launch traced here: 24 us
  Pallas kernels  11.2 us (46%)
  starting transfers between devices  9.95 us (41%)
  waiting for transfers between devices  1.84 us (8%)
  local copies, waits for them, and re-layouts  0.8 us (3%)
    pallas_call x1, Pallas kernels, per_device(): pl.pallas_call(kernel, out_shape=jax.ShapeDtypeStruct((HALF, n * n), f32)...  8.88 us
    ppermute x3, starting transfers between devices, share_tables(): lax.ppermute(table, 'depth', [(i, i ^ k) for i in range(count)])  4.57 us
    ppermute x1, starting transfers between devices, share_tables(): lax.ppermute(table, 'depth', [(i, i ^ step) for i in range(count)])  2.65 us
    ppermute x2, starting transfers between devices, windows(): lax.ppermute(sent, axes, edge(1, other) + edge(-1, other))[None]  2.06 us
    pallas_call x1, Pallas kernels, share_tables(): pl.pallas_call(table_kernel, out_shape=jax.ShapeDtypeStruct((2 * cams, 2...  1.43 us
    ppermute x1, waiting for transfers between devices, share_tables(): lax.ppermute(table, 'depth', [(i, i ^ step) for i in range(count)])  1.23 us
    pallas_call x1, Pallas kernels, per_device(): pl.pallas_call(turn, out_shape=[jax.ShapeDtypeStruct((12 * n, 4 * n), bf1...  0.67 us
    ppermute x1, starting transfers between devices, windows(): lax.ppermute(piece, 'exp', [(i, (i + 1) % exps) for i in range(exps)])  0.66 us
  transfers between devices with their start and end apart: 7, of which 3 were waited for; matrix products, arithmetic and copies ran while one was open for 1% of the time, Pallas kernels for 3%

profile of v7, /device:TPU:0, one launch (start us, length us, event | category | flops | bytes accessed | tf_op | source)
XLA Modules:
  0.0 24.0 jit_solution(9928446702017743913)
XLA Ops:
  0.0 0.0 copy-start
  0.0 1.4 %shard_map.91 = f32[8,128]{1,0:T(8,128)} custom-call(s32[4,8]{1,0:T(4,128)} %offsets_ref.1, f32[4,8]{1,0:T(4,128)} %fractions_ref.1), custom_call_target="tpu_custom_call" | custom-call | tf_op jit(solution)/shard_map/pallas_call | solution.py:397
  1.4 4.0 %collective-permute-start.2 = (f32[8,128]{1,0:T(8,128)}, f32[8,128]{1,0:T(8,128)S(1)}, u32[]{:S(2)}, u32[]{:S(2)}) collective-permute-start(f32[8,128]{1,0:T(8,128)} %shard_map.91), channel_id=1, source_target_pairs={{0,3},{1,2},{2,1},{3,0},{4,7},{5,6},{6,5},{7,4},{8,11},{9,10},{10,... | collective-permute-start | bytes 12296 | tf_op jit(solution)/shard_map/ppermute | solution.py:406
  5.4 0.4 %collective-permute-start.1 = (f32[8,128]{1,0:T(8,128)}, f32[8,128]{1,0:T(8,128)S(1)}, u32[]{:S(2)}, u32[]{:S(2)}) collective-permute-start(f32[8,128]{1,0:T(8,128)} %shard_map.91), channel_id=1, source_target_pairs={{0,2},{1,3},{2,0},{3,1},{4,6},{5,7},{6,4},{7,5},{8,10},{9,11},{10,... | collective-permute-start | bytes 12296 | tf_op jit(solution)/shard_map/ppermute | solution.py:406
  5.9 0.1 collective-permute-start
  6.0 0.0 copy-done
  6.0 0.1 constant_dynamic-slice_fusion
  6.2 0.1 reshape.8.own_ref
  6.3 0.0 copy-start.7
  6.3 0.0 copy-start.2
  6.3 0.0 copy-start.3
  6.3 0.5 %collective-permute-start.6 = (f32[4,1664]{1,0:T(4,128)S(1)}, f32[4,1664]{1,0:T(4,128)S(1)}, u32[]{:S(2)}, u32[]{:S(2)}) collective-permute-start(f32[4,1664]{1,0:T(4,128)S(1)} %slice_select_fusion.1), channel_id=1, source_target_pairs={{0,24},{1,25},{2,26},{3,27},{8,16},{9,17},{10,18},{11,19},{16,8},{... | collective-permute-start | bytes 79880 | tf_op jit(solution)/shard_map/ppermute | solution.py:441
  6.9 1.5 %collective-permute-start.5 = (f32[4,1664]{1,0:T(4,128)S(1)}, f32[4,1664]{1,0:T(4,128)S(1)}, u32[]{:S(2)}, u32[]{:S(2)}) collective-permute-start(f32[4,1664]{1,0:T(4,128)S(1)} %slice_select_fusion.1), channel_id=1, source_target_pairs={{0,8},{1,9},{2,10},{3,11},{8,0},{9,1},{10,2},{11,3},{16,24},{17,25... | collective-permute-start | bytes 79880 | tf_op jit(solution)/shard_map/ppermute | solution.py:441
  8.4 0.0 copy-start.1
  8.4 0.0 collective-permute-done.2
  8.5 0.7 %collective-permute-start.4 = (f32[4,6528]{1,0:T(4,128)S(1)}, f32[4,6528]{1,0:T(4,128)S(1)}, u32[]{:S(2)}, u32[]{:S(2)}) collective-permute-start(f32[4,6528]{1,0:T(4,128)S(1)} %slice_select_fusion), channel_id=1, source_target_pairs={{0,16},{16,0},{1,17},{17,1},{2,18},{18,2},{3,19},{19,3},{4,20},{20... | collective-permute-start | bytes 313352 | tf_op jit(solution)/shard_map/ppermute | solution.py:449
  9.1 0.1 collective-permute-done.1
  9.3 0.4 %collective-permute-done = f32[8,128]{1,0:T(8,128)S(1)} collective-permute-done((f32[8,128]{1,0:T(8,128)}, f32[8,128]{1,0:T(8,128)S(1)}, u32[]{:S(2)}, u32[]{:S(2)}) %collective-permute-start) | collective-permute-done | bytes 4128 | tf_op jit(solution)/shard_map/ppermute | solution.py:406
  9.7 0.0 copy-done.7
  9.7 2.6 %collective-permute-start.3 = (f32[8,128]{1,0:T(8,128)S(1)}, f32[8,128]{1,0:T(8,128)S(1)}, u32[]{:S(2)}, u32[]{:S(2)}) collective-permute-start(f32[8,128]{1,0:T(8,128)S(1)} %add_add_fusion), channel_id=1, source_target_pairs={{0,4},{1,5},{2,6},{3,7},{4,0},{5,1},{6,2},{7,3},{8,12},{9,13},{10,... | collective-permute-start | bytes 12296 | tf_op jit(solution)/shard_map/ppermute | solution.py:410
  12.4 0.0 copy-done.6
  12.4 0.7 %shard_map.93 = (bf16[768,256]{1,0:T(8,128)(2,1)S(1)}, bf16[64,144]{1,0:T(8,128)(2,1)S(1)}) custom-call(s32[1,3]{1,0:T(1,128)S(1)} %copy-done.6, f32[2,128,128]{2,1,0:T(8,128)S(1)} %copy-done.3, f32[2,2,128,128]{3,2,1,0:T(8,128)S(1)} %copy-done.2), custom_call_target="tpu_custom_call" | custom-call | tf_op jit(solution)/shard_map/pallas_call | solution.py:466
  13.1 1.2 %collective-permute-done.3 = f32[8,128]{1,0:T(8,128)S(1)} collective-permute-done((f32[8,128]{1,0:T(8,128)S(1)}, f32[8,128]{1,0:T(8,128)S(1)}, u32[]{:S(2)}, u32[]{:S(2)}) %collective-permute-start.3) | collective-permute-done | bytes 4128 | tf_op jit(solution)/shard_map/ppermute | solution.py:410
  14.3 0.0 collective-permute-done.6
  14.3 0.0 collective-permute-done.5
  14.3 0.0 collective-permute-done.4.other_ref
  14.3 0.0 copy-start.4
  14.3 0.0 copy-start.5
  14.3 0.3 %shard_map.92 = (f32[8,14848]{1,0:T(8,128)S(1)}, bf16[16,14848]{1,0:T(8,128)(2,1)S(1)}, bf16[16,14848]{1,0:T(8,128)(2,1)S(1)}) custom-call(f32[4,8192]{1,0:T(4,128)S(1)} %reshape.8.own_ref, f32[4,6528]{1,0:T(4,128)S(1)} %collective-permute-done.4.other_ref, f32[1,4,1664]{2,1,0:T(4,128)S(1)} %bitcast.6, f32[1,4,1664]{2,1,0:T(4,128)S(1)} %bitcast.5), custom_call_target="tpu_custom_call" | custom-call | tf_op jit(solution)/shard_map/pallas_call | solution.py:476
  14.6 0.5 %copy-done.4 = bf16[64,192]{1,0:T(8,128)(2,1)S(1)} copy-done((bf16[64,192]{1,0:T(8,128)(2,1)S(1)}, bf16[64,192]{1,0:T(8,128)(2,1)}, u32[]{:S(2)}) %copy-start.4) | copy-done | bytes 24600
  15.1 0.0 copy-done.5
  15.1 8.9 %shard_map.94 = f32[32,4096]{1,0:T(8,128)} custom-call(s32[1,3]{1,0:T(1,128)S(1)} %copy-done.6, f32[8,128]{1,0:T(8,128)S(1)} %add.23.tab_ref, f32[8,14848]{1,0:T(8,128)S(1)} %get-tuple-element.10.first_ref, bf16[16,14848]{1,0:T(8,128)(2,1)S(1)} %get-tuple-element.11.pack_in_ref, bf16[16,14848]{1,0:T(8,128)(2,1)S(1)} %get-tuple-element.12.high_in_ref, ...), custom_call_target="tpu_custom_call" | custom-call | tf_op jit(solution)/shard_map/pallas_call | solution.py:489
  (8 shorter events, 0.0 us)
Async XLA Ops:
  0.0 6.0 %copy-start = (f32[1,4,128,256]{3,2,1,0:T(8,128)S(1)}, f32[1,4,128,256]{3,2,1,0:T(8,128)}, u32[]{:S(2)}) copy-start(f32[1,4,128,256]{3,2,1,0:T(8,128)} %param.9) | copy-start | bytes 1572868
  1.4 7.0 %collective-permute-start.2 = (f32[8,128]{1,0:T(8,128)}, f32[8,128]{1,0:T(8,128)S(1)}, u32[]{:S(2)}, u32[]{:S(2)}) collective-permute-start(f32[8,128]{1,0:T(8,128)} %shard_map.91), channel_id=1, source_target_pairs={{0,3},{1,2},{2,1},{3,0},{4,7},{5,6},{6,5},{7,4},{8,11},{9,10},{10,... | collective-permute-start | bytes 12296 | tf_op jit(solution)/shard_map/ppermute | solution.py:406
  5.4 3.8 %collective-permute-start.1 = (f32[8,128]{1,0:T(8,128)}, f32[8,128]{1,0:T(8,128)S(1)}, u32[]{:S(2)}, u32[]{:S(2)}) collective-permute-start(f32[8,128]{1,0:T(8,128)} %shard_map.91), channel_id=1, source_target_pairs={{0,2},{1,3},{2,0},{3,1},{4,6},{5,7},{6,4},{7,5},{8,10},{9,11},{10,... | collective-permute-start | bytes 12296 | tf_op jit(solution)/shard_map/ppermute | solution.py:406
  5.9 3.8 %collective-permute-start = (f32[8,128]{1,0:T(8,128)}, f32[8,128]{1,0:T(8,128)S(1)}, u32[]{:S(2)}, u32[]{:S(2)}) collective-permute-start(f32[8,128]{1,0:T(8,128)} %shard_map.91), channel_id=1, source_target_pairs={{0,1},{1,0},{2,3},{3,2},{4,5},{5,4},{6,7},{7,6},{8,9},{9,8},{10,11... | collective-permute-start | bytes 12296 | tf_op jit(solution)/shard_map/ppermute | solution.py:406
  6.3 3.4 %copy-start.7 = (f32[8,128]{1,0:T(8,128)S(1)}, f32[8,128]{1,0:T(8,128)}, u32[]{:S(2)}) copy-start(f32[8,128]{1,0:T(8,128)} %shard_map.91) | copy-start | bytes 12292
  6.3 6.1 %copy-start.2 = (f32[2,2,128,128]{3,2,1,0:T(8,128)S(1)}, f32[2,2,128,128]{3,2,1,0:T(8,128)}, u32[]{:S(2)}) copy-start(f32[2,2,128,128]{3,2,1,0:T(8,128)} %constant.54.clone.z_inv_ref) | copy-start | bytes 786436
  6.3 6.0 %copy-start.3 = (f32[2,128,128]{2,1,0:T(8,128)S(1)}, f32[2,128,128]{2,1,0:T(8,128)}, u32[]{:S(2)}) copy-start(f32[2,128,128]{2,1,0:T(8,128)} %constant.53.clone.y_inv_ref) | copy-start | bytes 393220
  6.3 7.9 %collective-permute-start.6 = (f32[4,1664]{1,0:T(4,128)S(1)}, f32[4,1664]{1,0:T(4,128)S(1)}, u32[]{:S(2)}, u32[]{:S(2)}) collective-permute-start(f32[4,1664]{1,0:T(4,128)S(1)} %slice_select_fusion.1), channel_id=1, source_target_pairs={{0,24},{1,25},{2,26},{3,27},{8,16},{9,17},{10,18},{11,19},{16,8},{... | collective-permute-start | bytes 79880 | tf_op jit(solution)/shard_map/ppermute | solution.py:441
  6.9 7.4 %collective-permute-start.5 = (f32[4,1664]{1,0:T(4,128)S(1)}, f32[4,1664]{1,0:T(4,128)S(1)}, u32[]{:S(2)}, u32[]{:S(2)}) collective-permute-start(f32[4,1664]{1,0:T(4,128)S(1)} %slice_select_fusion.1), channel_id=1, source_target_pairs={{0,8},{1,9},{2,10},{3,11},{8,0},{9,1},{10,2},{11,3},{16,24},{17,25... | collective-permute-start | bytes 79880 | tf_op jit(solution)/shard_map/ppermute | solution.py:441
  8.4 4.0 %copy-start.6 = (s32[1,3]{1,0:T(1,128)S(1)}, s32[1,3]{1,0:T(1,128)}, u32[]{:S(2)}) copy-start(s32[1,3]{1,0:T(1,128)} %shift_any.1) | copy-start | bytes 40
  8.4 6.2 %copy-start.1 = (bf16[768,256]{1,0:T(8,128)(2,1)S(1)}, bf16[768,256]{1,0:T(8,128)(2,1)}, u32[]{:S(2)}) copy-start(bf16[768,256]{1,0:T(8,128)(2,1)} %constant.51.clone.y_fwd_ref) | copy-start | bytes 1179652
  8.5 5.8 %collective-permute-start.4 = (f32[4,6528]{1,0:T(4,128)S(1)}, f32[4,6528]{1,0:T(4,128)S(1)}, u32[]{:S(2)}, u32[]{:S(2)}) collective-permute-start(f32[4,6528]{1,0:T(4,128)S(1)} %slice_select_fusion), channel_id=1, source_target_pairs={{0,16},{16,0},{1,17},{17,1},{2,18},{18,2},{3,19},{19,3},{4,20},{20... | collective-permute-start | bytes 313352 | tf_op jit(solution)/shard_map/ppermute | solution.py:449
  9.7 4.6 %collective-permute-start.3 = (f32[8,128]{1,0:T(8,128)S(1)}, f32[8,128]{1,0:T(8,128)S(1)}, u32[]{:S(2)}, u32[]{:S(2)}) collective-permute-start(f32[8,128]{1,0:T(8,128)S(1)} %add_add_fusion), channel_id=1, source_target_pairs={{0,4},{1,5},{2,6},{3,7},{4,0},{5,1},{6,2},{7,3},{8,12},{9,13},{10,... | collective-permute-start | bytes 12296 | tf_op jit(solution)/shard_map/ppermute | solution.py:410
  14.3 0.8 %copy-start.4 = (bf16[64,192]{1,0:T(8,128)(2,1)S(1)}, bf16[64,192]{1,0:T(8,128)(2,1)}, u32[]{:S(2)}) copy-start(bf16[64,192]{1,0:T(8,128)(2,1)} %constant.52.clone.x_fwd_ref) | copy-start | bytes 73732
  14.3 0.8 %copy-start.5 = (bf16[64,192]{1,0:T(8,128)(2,1)S(1)}, bf16[64,192]{1,0:T(8,128)(2,1)}, u32[]{:S(2)}) copy-start(bf16[64,192]{1,0:T(8,128)(2,1)} %constant.50.clone.z_fwd_ref) | copy-start | bytes 73732
